TPU v7x, 256 devices: a whole 4x4x8 slice. The times are simulated.
256 devices in a mesh: row: 8 (over x, z_hi), col: 8 (over z_lo, core), depth: 4 (over y).
Axes of the slice: x: 4, y: 4, z: 8 (z_hi: 2, z_lo: 4; z = z_hi * 4 + z_lo), core: 2. Of those that a mesh axis runs over, the one named last changes fastest.
Arguments:
- tokens: bfloat16 [1024, 4096], P(('col', 'depth'), 'row'), may hold values from -72 to 72
- norm_gain: float32 [4096], P('row'), may hold values from 0.25 to 1.75
- w_gate: bfloat16 [4096, 14336], P('row', 'col'), may hold values from -0.09375 to 0.09375
- w_up: bfloat16 [4096, 14336], P('row', 'col'), may hold values from -0.09375 to 0.09375
- w_down: bfloat16 [14336, 4096], P('col', 'row'), may hold values from -0.046875 to 0.046875
- cotangent: bfloat16 [1024, 4096], P(('col', 'depth'), 'row'), may hold values from -1.5 to 1.5
Outputs:
- output: bfloat16 [1024, 4096], P(('col', 'depth'), 'row')
- grad_tokens: bfloat16 [1024, 4096], P(('col', 'depth'), 'row')
- grad_gain: float32 [4096], P('row')
- grad_gate: bfloat16 [4096, 14336], P('row', 'col')
- grad_up: bfloat16 [4096, 14336], P('row', 'col')
- grad_down: bfloat16 [14336, 4096], P('col', 'row')
All inputs are finite; a program needn't handle non-finite values.
Results may differ from a plain program's by a relative error of at most 0.023.
Values may be sent and summed in bfloat16 or wider, within the bound.
No kernel may reach another device: no remote copies, remote signals or barrier semaphores. Data moves between devices by JAX's collectives and lax.ppermute only.
A program may use at most 64 MiB of HBM per device.

v0:
```python
import jax
import jax.numpy as jnp
from jax import lax
from jax.sharding import PartitionSpec as P

D = 4096


EPS = 1e-05


def contract_rows(left, right):
    return lax.dot_general(
        left, right, (((0,), (0,)), ((), ())), preferred_element_type=jnp.float32
    )


def contract_cols(left, right):
    return lax.dot_general(
        left, right, (((1,), (1,)), ((), ())), preferred_element_type=jnp.float32
    )


def body(tokens, norm_gain, w_gate, w_up, w_down, cotangent):
    inputs = tokens.astype(jnp.float32)
    sumsq = lax.psum(jnp.sum(inputs * inputs, axis=1), "row")
    inv_rms = lax.rsqrt(sumsq / D + EPS)[:, None]
    normal_rows = inputs * inv_rms
    normed = (normal_rows * norm_gain[None, :]).astype(jnp.bfloat16)
    gathered = lax.all_gather(normed, "col", axis=0, tiled=True)
    piece = gathered
    gate = lax.psum_scatter(
        jnp.dot(piece, w_gate, preferred_element_type=jnp.float32).astype(jnp.bfloat16),
        "row",
        scatter_dimension=0,
        tiled=True,
    ).astype(jnp.float32)
    piece = gathered
    up = lax.psum_scatter(
        jnp.dot(piece, w_up, preferred_element_type=jnp.float32).astype(jnp.bfloat16),
        "row",
        scatter_dimension=0,
        tiled=True,
    ).astype(jnp.float32)
    sig = jax.nn.sigmoid(gate)
    act = gate * sig
    hidden = (act * up).astype(jnp.bfloat16)
    hidden_all = lax.all_gather(hidden, "row", axis=0, tiled=True)
    piece = hidden_all
    mixed = lax.psum_scatter(
        jnp.dot(piece, w_down, preferred_element_type=jnp.float32).astype(jnp.bfloat16),
        "col",
        scatter_dimension=0,
        tiled=True,
    ).astype(jnp.float32)
    output = (inputs + mixed).astype(jnp.bfloat16)
    cot_all = lax.all_gather(cotangent, "col", axis=0, tiled=True)
    piece = cot_all
    grad_hidden = lax.psum_scatter(
        contract_cols(piece, w_down).astype(jnp.bfloat16), "row", scatter_dimension=0, tiled=True
    ).astype(jnp.float32)
    down_grad = contract_rows(hidden_all, cot_all)
    down_sum = lax.psum(down_grad.astype(jnp.bfloat16), "depth")
    grad_up_h = (grad_hidden * act).astype(jnp.bfloat16)
    grad_gate_h = (grad_hidden * up * sig * (1.0 + gate * (1.0 - sig))).astype(jnp.bfloat16)
    gate_all, up_all = (
        lax.all_gather(grad_gate_h, "row", axis=0, tiled=True),
        lax.all_gather(grad_up_h, "row", axis=0, tiled=True),
    )
    gate_grad = contract_rows(gathered, gate_all)
    up_grad = contract_rows(gathered, up_all)
    grad_normed = lax.psum_scatter(
        (contract_cols(gate_all, w_gate) + contract_cols(up_all, w_up)).astype(jnp.bfloat16),
        "col",
        scatter_dimension=0,
        tiled=True,
    ).astype(jnp.float32)
    grad_scaled = grad_normed * norm_gain[None, :]
    proj = lax.psum(jnp.sum(grad_scaled * normal_rows, axis=1), "row")
    grad_tokens = (
        cotangent.astype(jnp.float32) + inv_rms * (grad_scaled - normal_rows * (proj / D)[:, None])
    ).astype(jnp.bfloat16)
    grad_gain = lax.psum(jnp.sum(grad_normed * normal_rows, axis=0), ("col", "depth"))
    gate_sum, up_sum = (
        lax.psum(gate_grad.astype(jnp.bfloat16), "depth").astype(jnp.float32),
        lax.psum(up_grad.astype(jnp.bfloat16), "depth").astype(jnp.float32),
    )
    return (
        output,
        grad_tokens,
        grad_gain,
        gate_sum.astype(jnp.bfloat16),
        up_sum.astype(jnp.bfloat16),
        down_sum,
    )


def solution(mesh):
    in_specs = (
        P(("col", "depth"), "row"),
        P("row"),
        P("row", "col"),
        P("row", "col"),
        P("col", "row"),
        P(("col", "depth"), "row"),
    )
    out_specs = (
        P(("col", "depth"), "row"),
        P(("col", "depth"), "row"),
        P("row"),
        P("row", "col"),
        P("row", "col"),
        P("col", "row"),
    )
    return jax.shard_map(body, mesh=mesh, in_specs=in_specs, out_specs=out_specs, check_vma=False)
```

profile of v0, /device:TPU:1, one launch (start us, length us, event | category | flops | bytes accessed | tf_op | source)
XLA Modules:
  0.0 635.6 jit_solution(9380735947653987925)
XLA Ops:
  7.2 0.0 copy-start
  7.2 0.0 reduce-scatter.12.cloned.1.call-start
  7.2 17.6 %all_gather.17 = bf16[256,512]{1,0:T(8,128)(2,1)S(1)} all-gather(bf16[32,512]{1,0:T(8,128)(2,1)} %param.11), channel_id=1, replica_groups=mesh['row'=8,'col'=8,'depth'=4] {'col'}, dimensions={0}, use_global_device_ids=true | all-gather | bytes 294912 | tf_op jit(solution)/shard_map/all_gather | solution.py:57
  24.8 0.0 copy-start.6
  24.8 0.0 copy-start.8
  24.8 3.1 convolution_convert_fusion.3
  27.9 0.0 reduce-scatter.12.cloned.1.call-update
  27.9 0.0 reduce-scatter.8.cloned.1.call-start
  28.0 0.0 copy-done.6
  28.0 0.1 fusion.21
  28.1 27.7 %psum.42 = f32[32]{0:T(128)S(1)} all-reduce(f32[32]{0:T(128)S(1)} %fusion.21), channel_id=1, replica_groups=mesh['row'=8,'col'=8,'depth'=4] {'row'}, use_global_device_ids=true, to_apply=%region_1.0 | all-reduce | flops 32 | bytes 256 | tf_op jit(solution)/shard_map/psum | solution.py:26
  55.9 0.0 copy-done.8
  55.9 0.1 fusion.18
  56.0 18.4 %all_gather.15 = bf16[256,512]{1,0:T(8,128)(2,1)S(1)} all-gather(bf16[32,512]{1,0:T(8,128)(2,1)S(1)} %fusion.18), channel_id=1, replica_groups=mesh['row'=8,'col'=8,'depth'=4] {'col'}, dimensions={0}, use_global_device_ids=true | all-gather | bytes 294912 | tf_op jit(solution)/shard_map/all_gather | solution.py:30
  74.4 3.1 convolution_convert_fusion.4
  77.5 0.0 reduce-scatter.8.cloned.1.call-update
  77.5 0.0 reduce-scatter.6.cloned.1.call-start
  77.5 0.0 copy-done
  77.5 1.6 convolution_convert_fusion.5
  79.1 0.0 reduce-scatter.6.cloned.1.call-update
  79.1 0.0 reduce-scatter.14.cloned.1.call-start
  79.2 35.7 %reduce-scatter.12.cloned.1.call-done = bf16[32,1792]{1,0:T(8,128)(2,1)} async-done(((bf16[256,1792]{1,0:T(8,128)(2,1)}), bf16[32,1792]{1,0:T(8,128)(2,1)}) %reduce-scatter.12.cloned.1.call-update) | async-done | bytes 114704 | tf_op jit(solution)/shard_map/reduce_scatter | solution.py:59
  114.9 87.8 %reduce-scatter.8.cloned.1.call-done = bf16[32,1792]{1,0:T(8,128)(2,1)} async-done(((bf16[256,1792]{1,0:T(8,128)(2,1)}), bf16[32,1792]{1,0:T(8,128)(2,1)}) %reduce-scatter.8.cloned.1.call-update) | async-done | bytes 114704 | tf_op jit(solution)/shard_map/reduce_scatter | solution.py:39
  202.7 87.7 %reduce-scatter.6.cloned.1.call-done = bf16[32,1792]{1,0:T(8,128)(2,1)} async-done(((bf16[256,1792]{1,0:T(8,128)(2,1)}), bf16[32,1792]{1,0:T(8,128)(2,1)}) %reduce-scatter.6.cloned.1.call-update) | async-done | bytes 114704 | tf_op jit(solution)/shard_map/reduce_scatter | solution.py:32
  290.4 1.1 fusion.5
  291.5 47.7 %all_gather.19 = bf16[256,1792]{1,0:T(8,128)(2,1)S(1)} all-gather(bf16[32,1792]{1,0:T(8,128)(2,1)S(1)} %get-tuple-element.11), channel_id=1, replica_groups=mesh['row'=8,'col'=8,'depth'=4] {'row'}, dimensions={0}, use_global_device_ids=true | all-gather | bytes 1032192 | tf_op jit(solution)/shard_map/all_gather | solution.py:68
  339.2 0.0 copy-start.1
  339.2 48.6 %all_gather.18 = bf16[256,1792]{1,0:T(8,128)(2,1)S(1)} all-gather(bf16[32,1792]{1,0:T(8,128)(2,1)S(1)} %get-tuple-element.12), channel_id=1, replica_groups=mesh['row'=8,'col'=8,'depth'=4] {'row'}, dimensions={0}, use_global_device_ids=true | all-gather | bytes 1032192 | tf_op jit(solution)/shard_map/all_gather | solution.py:67
  387.8 0.0 copy-start.2
  387.8 0.7 fusion.23
  388.5 0.0 copy-done.1
  388.5 0.8 copy-done.2
  389.3 1.4 fusion
  390.7 0.0 reduce-scatter.14.cloned.1.call-update
  390.7 0.0 reduce-scatter.10.cloned.1.call-start
  390.8 46.7 %all_gather.16 = bf16[256,1792]{1,0:T(8,128)(2,1)S(1)} all-gather(bf16[32,1792]{1,0:T(8,128)(2,1)S(1)} %get-tuple-element.13), channel_id=1, replica_groups=mesh['row'=8,'col'=8,'depth'=4] {'row'}, dimensions={0}, use_global_device_ids=true | all-gather | bytes 1032192 | tf_op jit(solution)/shard_map/all_gather | solution.py:48
  437.5 0.0 copy-start.3
  437.5 0.9 copy-done.3
  438.4 2.8 convolution_convert_fusion.6
  441.3 3.1 convolution_convert_fusion
  444.4 0.0 reduce-scatter.10.cloned.1.call-update
  444.4 0.0 all-reduce.3.cloned.1.call-start
  444.4 3.1 convolution_convert_fusion.1
  447.5 1.9 convolution_convert_fusion.2
  449.4 0.0 copy-start.7
  449.4 0.0 all-reduce.3.cloned.1.call-update
  449.5 0.0 reduce-scatter.14.cloned.1.call-done
  449.5 1.0 fusion.20
  450.4 20.6 %psum.43 = f32[32]{0:T(128)S(1)} all-reduce(f32[32]{0:T(128)S(1)} %get-tuple-element.7), channel_id=1, replica_groups=mesh['row'=8,'col'=8,'depth'=4] {'row'}, use_global_device_ids=true, to_apply=%region_8.0 | all-reduce | flops 32 | bytes 256 | tf_op jit(solution)/shard_map/psum | solution.py:79
  471.1 93.6 %psum.44 = f32[512]{0:T(512)} all-reduce(f32[512]{0:T(512)S(1)} %get-tuple-element.6), channel_id=1, replica_groups=mesh['row'=8,'col'=8,'depth'=4] {'col','depth'}, use_global_device_ids=true, to_apply=%region_10.0 | all-reduce | flops 512 | bytes 4096 | tf_op jit(solution)/shard_map/psum | solution.py:83
  564.7 0.0 reduce-scatter.10.cloned.1.call-done
  564.7 0.0 copy-done.7
  564.7 1.5 fusion.17
  566.2 56.2 %all-reduce.3.cloned.1.call-done = (bf16[512,1792]{1,0:T(8,128)(2,1)}, bf16[512,1792]{1,0:T(8,128)(2,1)}, bf16[1792,512]{1,0:T(8,128)(2,1)}) async-done(((bf16[512,1792]{1,0:T(8,128)(2,1)}, bf16[512,1792]{1,0:T(8,128)(2,1)}, bf16[1792,512]{1,0:T(8,128)(2,1)}), (bf16[512,1792]{1,0:T(8,128)(2,1)}, bf16[512,1792]{1,0:T(8,128)(2,1)}, bf16[1792,512]{1,0:T(8,128)(2,1)})) %all-reduce.3.cloned.1.call-update) | async-done | bytes 5505040 | tf_op jit(solution)/shard_map/psum | solution.py:85
  622.4 0.0 copy-start.5
  622.4 3.0 copy.15
  625.4 0.0 copy-done.5
  625.4 0.0 copy-start.4
  625.4 1.2 copy.16
  626.6 0.9 copy-done.4
  627.5 1.2 copy.17
  (2 shorter events, 0.0 us)
Async XLA Ops:
  7.2 70.4 %copy-start = (bf16[512,1792]{1,0:T(8,128)(2,1)S(1)}, bf16[512,1792]{1,0:T(8,128)(2,1)}, u32[]{:S(2)}) copy-start(bf16[512,1792]{1,0:T(8,128)(2,1)} %param.8) | copy-start | bytes 5505028
  7.2 107.7 %reduce-scatter.12.cloned.1.call-start = ((), (), s32[]{:S(2)}) async-start(), calls=%async_computation.8 | async-start | bytes 1032192 | tf_op jit(solution)/shard_map/reduce_scatter | solution.py:59
  24.8 3.2 copy-start.6
  24.8 31.1 %copy-start.8 = (f32[512]{0:T(512)S(1)}, f32[512]{0:T(512)}, u32[]{:S(2)}) copy-start(f32[512]{0:T(512)} %param.7) | copy-start | bytes 6148
  27.9 174.7 %reduce-scatter.8.cloned.1.call-start = ((), (), s32[]{:S(2)}) async-start(), calls=%async_computation.6 | async-start | bytes 1032192 | tf_op jit(solution)/shard_map/reduce_scatter | solution.py:39
  77.5 212.9 %reduce-scatter.6.cloned.1.call-start = ((), (), s32[]{:S(2)}) async-start(), calls=%async_computation.5 | async-start | bytes 1032192 | tf_op jit(solution)/shard_map/reduce_scatter | solution.py:32
  79.1 370.3 %reduce-scatter.14.cloned.1.call-start = ((), (), s32[]{:S(2)}) async-start(), calls=%async_computation.9 | async-start | bytes 294912 | tf_op jit(solution)/shard_map/reduce_scatter | solution.py:72
  339.2 49.3 %copy-start.1 = (bf16[256,1792]{1,0:T(8,128)(2,1)}, bf16[256,1792]{1,0:T(8,128)(2,1)S(1)}, u32[]{:S(2)}) copy-start(bf16[256,1792]{1,0:T(8,128)(2,1)S(1)} %all_gather.19) | copy-start | bytes 2752516
  387.8 1.5 copy-start.2
  390.7 173.9 %reduce-scatter.10.cloned.1.call-start = ((), (), s32[]{:S(2)}) async-start(), calls=%async_computation.7 | async-start | bytes 294912 | tf_op jit(solution)/shard_map/reduce_scatter | solution.py:50
  437.5 0.9 copy-start.3
  444.4 178.0 %all-reduce.3.cloned.1.call-start = ((), (), s32[]{:S(2)}) async-start(), calls=%async_computation.10 | async-start | bytes 11010048 | tf_op jit(solution)/shard_map/psum | solution.py:85
  449.4 115.2 %copy-start.7 = (bf16[32,512]{1,0:T(8,128)(2,1)S(1)}, bf16[32,512]{1,0:T(8,128)(2,1)}, u32[]{:S(2)}) copy-start(bf16[32,512]{1,0:T(8,128)(2,1)} %param.11) | copy-start | bytes 98308
  622.4 3.0 copy-start.5
  625.4 2.2 copy-start.4
Sparse Core Ops, SparseCore 0:
  28.1 86.7 reduce-scatter.11
  119.4 83.2 reduce-scatter.7
  207.2 83.1 reduce-scatter.5
  390.9 47.8 reduce-scatter.13
  444.5 53.3 reduce-scatter.9
  500.8 121.5 all-reduce.2
where the time goes:
time: 636 us
  blocking collectives  321 us (50%)
  waiting for transfers between devices  268 us (42%)
  matrix products  20.7 us (3%)
  between operations  14.2 us (2%)
  local copies, waits for them, and re-layouts  8.14 us (1%)
    psum x1, blocking collectives, body(): lax.psum(jnp.sum(grad_normed * normal_rows, axis=0), ('col', 'depth'))  93.6 us
    reduce_scatter x1, waiting for transfers between devices, body(): lax.psum_scatter(jnp.dot(piece, w_up, preferred_element_type=jnp.float32)...  87.8 us
    reduce_scatter x1, waiting for transfers between devices, body(): lax.psum_scatter(jnp.dot(piece, w_gate, preferred_element_type=jnp.float3...  87.7 us
    psum x1, waiting for transfers between devices, body(): lax.psum(gate_grad.astype(jnp.bfloat16), 'depth').astype(jnp.float32)  56.2 us
    all_gather x1, blocking collectives, body(): lax.all_gather(grad_gate_h, 'row', axis=0, tiled=True)  48.6 us
    all_gather x1, blocking collectives, body(): lax.all_gather(grad_up_h, 'row', axis=0, tiled=True)  47.7 us
    all_gather x1, blocking collectives, body(): hidden_all = lax.all_gather(hidden, 'row', axis=0, tiled=True)  46.7 us
    reduce_scatter x1, waiting for transfers between devices, body(): lax.psum_scatter(contract_cols(piece, w_down).astype(jnp.bfloat16), 'row'...  35.7 us
  transfers between devices with their start and end apart: 6, of which 4 were waited for; matrix products, arithmetic and copies ran while one was open for 3% of the time, Pallas kernels for 0%

commit v1 on v0

v1 whole, which is shorter than its diff:
```python
import jax
import jax.numpy as jnp
from jax import lax
from jax.experimental import pallas as pl
from jax.experimental.pallas import tpu as pltpu
from jax.sharding import PartitionSpec as P


D = 4096
EPS = 1e-05
FS = 448
CHUNKS = ((0, 224), (224, 224))


BF = jnp.bfloat16
F32 = jnp.float32


def perm_x(k):
    return [(r, ((r // 2 + k) % 4) * 2 + r % 2) for r in range(8)]


PERM_ZH = [(r, r ^ 1) for r in range(8)]


def perm_zl(k):
    return [(c, ((c // 2 + k) % 4) * 2 + c % 2) for c in range(8)]


PERM_CORE = [(c, c ^ 1) for c in range(8)]


def perm_y(k):
    return [(d, (d + k) % 4) for d in range(4)]


def send(v, axis, perm):
    return lax.ppermute(v, axis, perm)


def send_x(v, k):
    return send(v, "row", perm_x(k))


def send_zh(v):
    return send(v, "row", PERM_ZH)


def send_zl(v, k):
    return send(v, "col", perm_zl(k))


def send_core(v):
    return send(v, "col", PERM_CORE)


def send_y(v, k):
    return send(v, "depth", perm_y(k))


def nt(left, right):
    return lax.dot_general(left, right, (((1,), (1,)), ((), ())), preferred_element_type=F32)


def nn(left, right):
    return lax.dot_general(left, right, (((1,), (0,)), ((), ())), preferred_element_type=F32)


def tn(left, right):
    return lax.dot_general(left, right, (((0,), (0,)), ((), ())), preferred_element_type=F32)


VM = pl.BlockSpec(memory_space=pltpu.VMEM)
SM = pl.BlockSpec(memory_space=pltpu.SMEM)


def sds(shape, dtype):
    return jax.ShapeDtypeStruct(shape, dtype)


ANY = pl.BlockSpec(memory_space=pl.ANY)


def call(kernel, outs, scalars, *args, scratch=(), raw=0, hbm_in=(), hbm_out=(), limit=12):
    outs = [o if i in hbm_out else pltpu.VMEM(o.shape, o.dtype) for i, o in enumerate(outs)]
    run = pl.pallas_call(
        kernel,
        out_shape=outs,
        in_specs=[SM] * len(scalars) + [ANY] * raw + [VM] * (len(args) - raw),
        out_specs=[VM] * len(outs),
        scratch_shapes=list(scratch),
        compiler_params=pltpu.CompilerParams(vmem_limit_bytes=limit << 20),
    )
    placed = [
        a if i < raw or i in hbm_in else pltpu.with_memory_space_constraint(a, pltpu.VMEM)
        for i, a in enumerate(args)
    ]
    return run(*scalars, *placed)


def split(value):
    hi = value.astype(BF)
    return hi, (value - hi.astype(F32)).astype(BF)


def add_stat(message, size):
    return message[3 * size:3 * size + 8, :].astype(F32) + message[3 * size + 8:, :].astype(F32)


def pack_call(tokens, cotangent):
    def kernel(tok_ref, cot_ref, out_ref):
        out_ref[:, :512] = tok_ref[...]
        out_ref[:, 512:] = cot_ref[...]

    return call(kernel, [sds((32, 1024), BF)], (), tokens, cotangent, hbm_in=(0, 1))[0]


def prepare_call(depth_at, w_gate, w_up, w_down):
    def kernel(at_ref, gate_ref, up_ref, down_ref, *refs):
        outs, (cut_ref, turned_ref, sems) = refs[:-3], refs[-3:]
        at = at_ref[0]
        start = pl.multiple_of(((7 * at) // 2) * 128, 128)
        skip = pl.multiple_of((at % 2) * 64, 64)
        copies = [
            pltpu.make_async_copy(ref.at[:, pl.ds(start, 512)], cut_ref.at[i], sems.at[i])
            for i, ref in enumerate((gate_ref, up_ref))
        ]
        for i, (where, size) in enumerate(CHUNKS):
            rows = pl.ds(pl.multiple_of(at * FS + where, 16), size)
            copies.append(pltpu.make_async_copy(down_ref.at[rows, :], outs[2 * i + 1], sems.at[2 + i]))
        for copy in copies:
            copy.start()
        for which in (0, 1):
            copies[which].wait()
            turned_ref[which] = cut_ref[which].T
            for i, (where, size) in enumerate(CHUNKS):
                outs[2 * i][which * size:(which + 1) * size, :] = turned_ref[which, pl.ds(skip + where, size), :]
        for copy in copies[2:]:
            copy.wait()

    outs = []
    for _, size in CHUNKS:
        outs += [sds((2 * size, 512), BF), sds((size, 512), BF)]
    scratch = [pltpu.VMEM((2, 512, 512), BF), pltpu.VMEM((2, 512, 512), BF), pltpu.SemaphoreType.DMA((4,))]
    return call(kernel, outs, (depth_at,), w_gate, w_up, w_down, scratch=scratch, raw=3)


def block_rows(at_ref, k):
    return pl.ds(pl.multiple_of(((at_ref[0] + k + 4) % 4) * 256, 256), 256)


def block_part(rows, both_ref, gain_ref, wgu_ref, wd_ref, first):
    x = both_ref[rows, :512].astype(F32)
    parts = [nt(wgu_ref[...], (x * gain_ref[...]).astype(BF)), nt(wd_ref[...], both_ref[rows, 512:])]
    if first:
        hi, lo = split(x * x)
        ones = jnp.ones((8, 512), BF)
        parts.append(nt(ones, hi) + nt(ones, lo))
    return parts


def write_parts(ref, parts, size):
    ref[:2 * size, :] = parts[0].astype(BF)
    ref[2 * size:3 * size, :] = parts[1].astype(BF)
    if len(parts) > 2:
        hi, lo = split(parts[2])
        ref[3 * size:, :] = jnp.concatenate([hi, lo], axis=0)


def read_parts(ref, size, first):
    parts = [ref[:2 * size, :].astype(F32), ref[2 * size:3 * size, :].astype(F32)]
    if first:
        parts.append(add_stat(ref, size))
    return parts


def message_shape(size, first):
    return sds((3 * size + (16 if first else 0), 256), BF)


def partial_call(x_at, ks, both, gain, wgu, wd, size, first):
    def kernel(at_ref, both_ref, gain_ref, wgu_ref, wd_ref, *outs):
        for k, out_ref in zip(ks, outs):
            write_parts(out_ref, block_part(block_rows(at_ref, k), both_ref, gain_ref, wgu_ref, wd_ref, first), size)

    return call(kernel, [message_shape(size, first)] * len(ks), (x_at,), both, gain, wgu, wd, hbm_in=(1,))


def sum_call(x_at, both, gain, wgu, wd, received, size, first):
    def kernel(at_ref, both_ref, gain_ref, wgu_ref, wd_ref, a_ref, b_ref, c_ref, total_ref, out_ref):
        total = block_part(block_rows(at_ref, 0), both_ref, gain_ref, wgu_ref, wd_ref, first)
        for ref in (a_ref, b_ref, c_ref):
            total = [a + b for a, b in zip(total, read_parts(ref, size, first))]
        total_ref[:2 * size, :] = total[0]
        total_ref[2 * size:3 * size, :] = total[1]
        if first:
            total_ref[3 * size:, :] = total[2]
        write_parts(out_ref, total, size)

    outs = [sds((3 * size + (8 if first else 0), 256), F32), message_shape(size, first)]
    return call(kernel, outs, (x_at,), both, gain, wgu, wd, *received, hbm_in=(1,))


def middle_call(total, other, inv, size):
    first = inv is None

    def kernel(total_ref, other_ref, *refs):
        if first:
            out_ref, inv_ref = refs
            stat = total_ref[3 * size:, :] + add_stat(other_ref, size)
            inv_ref[...] = lax.rsqrt(stat / D + EPS)
        else:
            inv_ref, out_ref = refs
        scale = inv_ref[0:1, :]
        gate = (total_ref[:size, :] + other_ref[:size, :].astype(F32)) * scale
        up = (total_ref[size:2 * size, :] + other_ref[size:2 * size, :].astype(F32)) * scale
        grad = (total_ref[2 * size:3 * size, :] + other_ref[2 * size:3 * size, :].astype(F32)) * scale
        sig = jax.nn.sigmoid(gate)
        act = gate * sig
        out_ref[:size, :] = (act * up).astype(BF)
        out_ref[size:2 * size, :] = (grad * up * sig * (1.0 + gate * (1.0 - sig))).astype(BF)
        out_ref[2 * size:, :] = (grad * act).astype(BF)

    out = sds((3 * size, 256), BF)
    if first:
        return call(kernel, [out, sds((8, 256), F32)], (), total, other)
    return call(kernel, [out], (), total, other, inv)[0], inv


def weight_grad_call(x_at, pieces, both, gain, size):
    def kernel(at_ref, a_ref, b_ref, c_ref, d_ref, both_ref, gain_ref, out_ref):
        down = jnp.zeros((size, 512), F32)
        gate_up = jnp.zeros((2 * size, 512), F32)
        for k, ref in zip((0, 2, 1, -1), (a_ref, b_ref, c_ref, d_ref)):
            rows = block_rows(at_ref, -k)
            u = (both_ref[rows, :512].astype(F32) * gain_ref[...]).astype(BF)
            down = down + nn(ref[:size, :], both_ref[rows, 512:])
            gate_up = gate_up + nn(ref[size:, :], u)
        out_ref[:size, :] = down.astype(BF)
        out_ref[size:, :] = gate_up.astype(BF)

    return call(kernel, [sds((3 * size, 512), BF)], (x_at,), *pieces, both, gain, hbm_in=(5,))[0]


def write_gain(ref, rows, vector):
    hi, lo = split(vector)
    ref[rows:, :512] = jnp.concatenate([hi, hi], axis=0)
    ref[rows:, 512:] = jnp.concatenate([lo, lo], axis=0)


def read_gain(ref, rows):
    return ref[rows:rows + 8, :512].astype(F32) + ref[rows:rows + 8, 512:].astype(F32)


def back_call(x_at, pieces, wgu, wd, before, both, size, last):
    def kernel(at_ref, a_ref, b_ref, c_ref, d_ref, wgu_ref, wd_ref, both_ref, *refs):
        refs = list(refs)
        before_ref = refs.pop(0) if before is not None else None
        if last:
            own_ref, gain_ref, out_ref, acc_ref = refs
        else:
            acc_ref, = refs
        vector = jnp.zeros((1, 512), F32)
        for k, ref in zip((0, 2, 1, -1), (a_ref, b_ref, c_ref, d_ref)):
            rows = block_rows(at_ref, -k)
            mixed = tn(ref[:size, :], wd_ref[...])
            grad = tn(ref[size:, :], wgu_ref[...])
            if before is not None:
                mixed = mixed + before_ref[rows, :512]
                grad = grad + before_ref[rows, 512:]
            acc_ref[rows, :512] = mixed
            acc_ref[rows, 512:] = grad
            if last:
                vector = vector + jnp.sum(grad * both_ref[rows, :512].astype(F32), axis=0, keepdims=True)
        if last:
            own_ref[...] = acc_ref[:512, :]
            out_ref[:512, :] = acc_ref[512:, :].astype(BF)
            vector = jnp.broadcast_to(vector, (8, 512))
            gain_ref[...] = vector
            write_gain(out_ref, 512, vector)

    args = list(pieces) + [wgu, wd, both] + ([before] if before is not None else [])
    if last:
        outs = [sds((512, 1024), F32), sds((8, 512), F32), sds((528, 1024), BF)]
        return call(kernel, outs, (x_at,), *args, scratch=[pltpu.VMEM((1024, 1024), F32)])
    return call(kernel, [sds((1024, 1024), F32)], (x_at,), *args)[0]


def fold_call(own, vector, messages, strips):
    rows = own.shape[0]
    count = len(messages)
    keep = sum(size for _, size in strips[0])

    def kernel(own_ref, vector_ref, *refs):
        received = refs[:count]
        keep_ref, gain_ref = refs[count:count + 2]
        outs = refs[count + 2:]
        vec = vector_ref[...]
        for ref in received:
            vec = vec + read_gain(ref, rows)
        gain_ref[...] = vec
        for strip, out in zip(strips, (keep_ref,) + tuple(outs)):
            to = 0
            for at, size in strip:
                total = own_ref[at:at + size, :]
                for ref in received:
                    total = total + ref[at:at + size, :].astype(F32)
                out[to:to + size, :] = total.astype(out.dtype)
                to += size
        for ref in outs:
            write_gain(ref, keep, vec)

    outs = [sds((keep, 1024), F32), sds((8, 512), F32)] + [sds((keep + 16, 1024), BF)] * (len(strips) - 1)
    return call(kernel, outs, (), own, vector, *messages)


def final_call(own, vector, messages, tokens, gain):
    def kernel(own_ref, vector_ref, a_ref, b_ref, c_ref, tok_ref, gain_ref, out_ref, g_ref, vec_ref, stat_ref):
        total = own_ref[...]
        vec = vector_ref[...]
        for ref in (a_ref, b_ref, c_ref):
            total = total + ref[:32, :].astype(F32)
            vec = vec + read_gain(ref, 32)
        vec_ref[...] = vec[:1, :]
        x = tok_ref[...].astype(F32)
        out_ref[...] = (x + total[:, :512]).astype(BF)
        g = total[:, 512:] * gain_ref[...]
        g_ref[...] = g
        stat_ref[:, :128] = jnp.broadcast_to(jnp.sum(x * x, axis=1, keepdims=True), (32, 128))
        stat_ref[:, 128:] = jnp.broadcast_to(jnp.sum(g * x, axis=1, keepdims=True), (32, 128))

    outs = [sds((32, 512), BF), sds((32, 512), F32), sds((1, 512), F32), sds((32, 256), F32)]
    return call(kernel, outs, (), own, vector, *messages, tokens, gain, hbm_in=(5, 6), hbm_out=(0, 2))


def tail_call(stats, other, cotangent, tokens, g_own):
    def kernel(a_ref, b_ref, cot_ref, tok_ref, g_ref, out_ref):
        stat = a_ref[...] + b_ref[...]
        inv = lax.rsqrt(stat[:, :1] / D + EPS)
        proj = stat[:, 128:129]
        x = tok_ref[...].astype(F32)
        out_ref[...] = (cot_ref[...].astype(F32) + g_ref[...] - x * (inv * inv * (proj / D))).astype(BF)

    return call(kernel, [sds((32, 512), BF)], (), stats, other, cotangent, tokens, g_own, hbm_in=(2, 3), hbm_out=(0,))[0]


def add_call(parts):
    def kernel(a_ref, b_ref, c_ref, d_ref, out_ref):
        out_ref[...] = a_ref[...] + b_ref[...] + c_ref[...] + d_ref[...]

    return call(kernel, [sds(parts[0].shape, F32)], (), *parts)[0]


def assemble_call(depth_at, groups):
    count = len(groups)

    def kernel(at_ref, *refs):
        gate_ref, up_ref, down_ref, tgate_ref, tup_ref = refs[5 * count:]
        for i, (at, size, _) in enumerate(groups):
            own, prev, after, far_a, far_b = refs[5 * i:5 * i + 5]
            half = 3 * size // 2
            for k, ref in ((0, own), (3, prev), (1, after)):
                start = ((at_ref[0] + k) % 4) * FS + at
                rows = pl.ds(pl.multiple_of(start, 16), size)
                down_ref[rows, :] = ref[:size, :]
                tgate_ref[rows, :] = ref[size:2 * size, :]
                tup_ref[rows, :] = ref[2 * size:, :]
            start = ((at_ref[0] + 2) % 4) * FS + at
            rows = pl.ds(pl.multiple_of(start, 16), size)
            down_ref[rows, :] = far_a[:size, :]
            tgate_ref[pl.ds(pl.multiple_of(start, 16), half - size), :] = far_a[size:, :]
            tgate_ref[pl.ds(pl.multiple_of(start + half - size, 16), 2 * size - half), :] = far_b[:2 * size - half, :]
            tup_ref[rows, :] = far_b[2 * size - half:, :]

        def turn(i, carry):
            cut = pl.ds(pl.multiple_of(i * 128, 128), 128)
            gate_ref[:, cut] = tgate_ref[cut, :].T
            up_ref[:, cut] = tup_ref[cut, :].T
            return carry

        lax.fori_loop(0, 14, turn, 0)

    args = [a for g in groups for a in g[2]]
    outs = [sds((512, 4 * FS), BF), sds((512, 4 * FS), BF), sds((4 * FS, 512), BF)]
    scratch = [pltpu.VMEM((4 * FS, 512), BF), pltpu.VMEM((4 * FS, 512), BF)]
    return call(kernel, outs, (depth_at,), *args, scratch=scratch, hbm_out=(0, 1, 2), limit=24)


def step(tokens, norm_gain, w_gate, w_up, w_down, cotangent):
    x_at = jnp.reshape(lax.axis_index("row") // 2, (1,)).astype(jnp.int32)
    depth_at = jnp.reshape(lax.axis_index("depth"), (1,)).astype(jnp.int32)
    gain = norm_gain[None, :]
    count = len(CHUNKS)

    both = pack_call(tokens, cotangent)
    near = [send_zl(both, k) for k in (1, 2, 3)]
    weights = prepare_call(depth_at, w_gate, w_up, w_down)
    both = jnp.concatenate([both] + near, axis=0)
    both = jnp.concatenate([both] + [send_y(both, k) for k in (1, -1, 2)], axis=0)
    both = jnp.concatenate([both, send_core(both)], axis=0)
    chunks = [(at, size, weights[2 * i], weights[2 * i + 1]) for i, (at, size) in enumerate(CHUNKS)]

    received = []
    for n, (at, size, wgu, wd) in enumerate(chunks):
        groups = [(2,), (1,), (-1,)] if n == 0 else [(2, 1, -1)]
        arrived = []
        for ks in groups:
            parts = partial_call(x_at, ks, both, gain, wgu, wd, size, n == 0)
            arrived += [send_x(part, k) for k, part in zip(ks, parts)]
        received.append(arrived)
    halves = []
    for n, (at, size, wgu, wd) in enumerate(chunks):
        total, message = sum_call(x_at, both, gain, wgu, wd, received[n], size, n == 0)
        halves.append((total, send_zh(message)))
    inv = None
    pieces = []
    for n, (at, size, wgu, wd) in enumerate(chunks):
        mine, inv = middle_call(*halves[n], inv, size)
        pieces.append([mine] + [send_x(mine, k) for k in (2, 1, -1)])

    def weight_grad(n):
        at, size, _, _ = chunks[n]
        grad = weight_grad_call(x_at, pieces[n], both, gain, size)
        return at, size, grad, send_y(grad, 1), send_y(grad, -1)

    def relay(at, size, grad, prev, after):
        half = 3 * size // 2
        return at, size, [grad, prev, after, send_y(prev[:half], 1), send_y(after[half:], -1)]

    def back(n, before):
        _, size, wgu, wd = chunks[n]
        return back_call(x_at, pieces[n], wgu, wd, before, both, size, n == count - 1)

    grads = []
    before = None
    for n in range(count - 1):
        grads.append(weight_grad(n))
        before = back(n, before)
    own, vector, message = back(count - 1, before)
    message = send_core(message)
    groups = [relay(*g) for g in grads]
    last = weight_grad(count - 1)
    strips = [[(128 * a + 32 * j, 32) for a in range(4)] for j in range(4)]
    own, vector, *messages = fold_call(own, vector, [message], strips)
    messages = [send_zl(m, -k) for k, m in zip((1, 2, 3), messages)]
    own, vector, *messages = fold_call(own, vector, messages, [[(32 * j, 32)] for j in range(4)])
    messages = [send_y(m, k) for k, m in zip((-1, 1, 2), messages)]
    groups.append(relay(*last))
    output, g_own, vector, stats = final_call(own, vector, messages, tokens, gain)
    stats = add_call([stats] + [send_x(stats, k) for k in (1, -1, 2)])
    grad_tokens = tail_call(stats, send_zh(stats), cotangent, tokens, g_own)
    out_gate, out_up, out_down = assemble_call(depth_at, groups)
    return output, grad_tokens, vector[0], out_gate, out_up, out_down


def solution(mesh):
    in_specs = (
        P(("col", "depth"), "row"),
        P("row"),
        P("row", "col"),
        P("row", "col"),
        P("col", "row"),
        P(("col", "depth"), "row"),
    )
    out_specs = (
        P(("col", "depth"), "row"),
        P(("col", "depth"), "row"),
        P("row"),
        P("row", "col"),
        P("row", "col"),
        P("col", "row"),
    )
    function = jax.shard_map(step, mesh=mesh, in_specs=in_specs, out_specs=out_specs, check_vma=False)
    shapes = [((1024, D), BF), ((D,), F32), ((D, 32 * FS), BF), ((D, 32 * FS), BF), ((32 * FS, D), BF), ((1024, D), BF)]
    jax.eval_shape(function, *[sds(*shape) for shape in shapes])
    return function
```

time: 636 us -> 214 us (0.34)
  the two profiles are of different devices: /device:TPU:1 before, /device:TPU:6 now
where the time goes in v1:
time: 214 us
  waiting for transfers between devices  131 us (61%)
  starting transfers between devices  54.3 us (25%)
  Pallas kernels  15.3 us (7%)
  local copies, waits for them, and re-layouts  11.6 us (5%)
    ppermute x40, waiting for transfers between devices, send(): return lax.ppermute(v, axis, perm)  131 us
    ppermute x40, starting transfers between devices, send(): return lax.ppermute(v, axis, perm)  54.3 us
    pallas_call x20, Pallas kernels, call(): return run(*scalars, *placed)  15.3 us
    unnamed x22, local copies, waits for them, and re-layouts  10.7 us
  transfers between devices with their start and end apart: 40, of which 26 were waited for; matrix products, arithmetic and copies ran while one was open for 2% of the time, Pallas kernels for 5%

profile of v1, /device:TPU:6, one launch (start us, length us, event | category | flops | bytes accessed | tf_op | source)
XLA Modules:
  0.0 213.6 jit_solution(17004479512769453612)
XLA Ops:
  1.4 0.8 copy-done.6
  2.2 1.9 collective-permute-start
  4.1 3.3 %collective-permute-start.1 = (bf16[32,1024]{1,0:T(8,128)(2,1)S(1)}, bf16[32,1024]{1,0:T(8,128)(2,1)S(1)}, u32[]{:S(2)}, u32[]{:S(2)}) collective-permute-start(bf16[32,1024]{1,0:T(8,128)(2,1)S(1)} %shard_map.109), channel_id=1, source_target_pairs={{0,16},{4,20},{8,24},{12,28},{16,0},{20,4},{24,8},{28,12},{1,17},{... | collective-permute-start | bytes 196616 | tf_op jit(solution)/shard_map/ppermute | solution.py:38
  7.3 1.0 collective-permute-start.2
  9.6 2.3 %collective-permute-done.1 = bf16[32,1024]{1,0:T(8,128)(2,1)S(1)} collective-permute-done((bf16[32,1024]{1,0:T(8,128)(2,1)S(1)}, bf16[32,1024]{1,0:T(8,128)(2,1)S(1)}, u32[]{:S(2)}, u32[]{:S(2)}) %collective-permute-start.1) | collective-permute-done | bytes 65568 | tf_op jit(solution)/shard_map/ppermute | solution.py:38
  12.2 1.7 collective-permute-start.3
  13.9 1.7 collective-permute-start.4
  15.5 2.0 collective-permute-start.5
  19.4 2.1 %collective-permute-done.3 = bf16[128,1024]{1,0:T(8,128)(2,1)S(1)} collective-permute-done((bf16[128,1024]{1,0:T(8,128)(2,1)S(1)}, bf16[128,1024]{1,0:T(8,128)(2,1)S(1)}, u32[]{:S(2)}, u32[]{:S(2)}) %collective-permute-start.3) | collective-permute-done | bytes 262176 | tf_op jit(solution)/shard_map/ppermute | solution.py:38
  21.6 0.8 constant_dynamic-update-slice_fusion.2
  22.3 3.9 %collective-permute-done.4 = bf16[128,1024]{1,0:T(8,128)(2,1)S(1)} collective-permute-done((bf16[128,1024]{1,0:T(8,128)(2,1)S(1)}, bf16[128,1024]{1,0:T(8,128)(2,1)S(1)}, u32[]{:S(2)}, u32[]{:S(2)}) %collective-permute-start.4) | collective-permute-done | bytes 262176 | tf_op jit(solution)/shard_map/ppermute | solution.py:38
  26.2 0.8 constant_dynamic-update-slice_fusion.1
  27.0 1.0 collective-permute-done.5
  28.0 0.8 constant_dynamic-update-slice_fusion
  28.8 1.5 copy-done
  30.3 1.5 copy-done.1
  31.8 1.5 copy-done.2
  33.3 1.2 shard_map.110
  36.6 1.5 collective-permute-start.11
  38.1 2.1 collective-permute-start.12
  40.2 9.2 %collective-permute-done.11.a_ref = bf16[688,256]{1,0:T(8,128)(2,1)S(1)} collective-permute-done((bf16[688,256]{1,0:T(8,128)(2,1)S(1)}, bf16[688,256]{1,0:T(8,128)(2,1)S(1)}, u32[]{:S(2)}, u32[]{:S(2)}) %collective-permute-start.11) | collective-permute-done | bytes 352288 | tf_op jit(solution)/shard_map/ppermute | solution.py:38
  49.4 4.9 %collective-permute-done.12.b_ref = bf16[688,256]{1,0:T(8,128)(2,1)S(1)} collective-permute-done((bf16[688,256]{1,0:T(8,128)(2,1)S(1)}, bf16[688,256]{1,0:T(8,128)(2,1)S(1)}, u32[]{:S(2)}, u32[]{:S(2)}) %collective-permute-start.12) | collective-permute-done | bytes 352288 | tf_op jit(solution)/shard_map/ppermute | solution.py:38
  54.3 2.2 %collective-permute-done.13.c_ref = bf16[688,256]{1,0:T(8,128)(2,1)S(1)} collective-permute-done((bf16[688,256]{1,0:T(8,128)(2,1)S(1)}, bf16[688,256]{1,0:T(8,128)(2,1)S(1)}, u32[]{:S(2)}, u32[]{:S(2)}) %collective-permute-start.13) | collective-permute-done | bytes 352288 | tf_op jit(solution)/shard_map/ppermute | solution.py:38
  57.0 5.9 %collective-permute-start.14 = (bf16[688,256]{1,0:T(8,128)(2,1)S(1)}, bf16[688,256]{1,0:T(8,128)(2,1)S(1)}, u32[]{:S(2)}, u32[]{:S(2)}) collective-permute-start(bf16[688,256]{1,0:T(8,128)(2,1)S(1)} %get-tuple-element.49), channel_id=1, source_target_pairs={{0,32},{32,0},{64,96},{96,64},{128,160},{160,128},{192,224},{224,1... | collective-permute-start | bytes 1056776 | tf_op jit(solution)/shard_map/ppermute | solution.py:38
  62.9 0.8 shard_map.111
  63.8 1.6 collective-permute-start.7
  65.3 1.2 collective-permute-start.8
  66.5 0.9 collective-permute-start.9
  67.3 9.0 %collective-permute-done.7.a_ref = bf16[672,256]{1,0:T(8,128)(2,1)S(1)} collective-permute-done((bf16[672,256]{1,0:T(8,128)(2,1)S(1)}, bf16[672,256]{1,0:T(8,128)(2,1)S(1)}, u32[]{:S(2)}, u32[]{:S(2)}) %collective-permute-start.7) | collective-permute-done | bytes 344096 | tf_op jit(solution)/shard_map/ppermute | solution.py:38
  76.3 4.0 %collective-permute-done.8.b_ref = bf16[672,256]{1,0:T(8,128)(2,1)S(1)} collective-permute-done((bf16[672,256]{1,0:T(8,128)(2,1)S(1)}, bf16[672,256]{1,0:T(8,128)(2,1)S(1)}, u32[]{:S(2)}, u32[]{:S(2)}) %collective-permute-start.8) | collective-permute-done | bytes 344096 | tf_op jit(solution)/shard_map/ppermute | solution.py:38
  80.3 2.1 %collective-permute-done.9.c_ref = bf16[672,256]{1,0:T(8,128)(2,1)S(1)} collective-permute-done((bf16[672,256]{1,0:T(8,128)(2,1)S(1)}, bf16[672,256]{1,0:T(8,128)(2,1)S(1)}, u32[]{:S(2)}, u32[]{:S(2)}) %collective-permute-start.9) | collective-permute-done | bytes 344096 | tf_op jit(solution)/shard_map/ppermute | solution.py:38
  83.6 1.5 collective-permute-start.18
  85.1 1.2 collective-permute-start.19
  86.3 0.8 collective-permute-start.20
  87.1 15.7 %collective-permute-done.10.other_ref = bf16[672,256]{1,0:T(8,128)(2,1)S(1)} collective-permute-done((bf16[672,256]{1,0:T(8,128)(2,1)S(1)}, bf16[672,256]{1,0:T(8,128)(2,1)S(1)}, u32[]{:S(2)}, u32[]{:S(2)}) %collective-permute-start.10) | collective-permute-done | bytes 344096 | tf_op jit(solution)/shard_map/ppermute | solution.py:38
  103.0 1.5 collective-permute-start.15
  104.5 0.8 collective-permute-start.16
  105.4 1.2 collective-permute-start.17
  106.6 1.0 shard_map.119.refs_0_
  107.6 5.9 %collective-permute-done.15.b_ref = bf16[672,256]{1,0:T(8,128)(2,1)S(1)} collective-permute-done((bf16[672,256]{1,0:T(8,128)(2,1)S(1)}, bf16[672,256]{1,0:T(8,128)(2,1)S(1)}, u32[]{:S(2)}, u32[]{:S(2)}) %collective-permute-start.15) | collective-permute-done | bytes 344096 | tf_op jit(solution)/shard_map/ppermute | solution.py:38
  113.5 1.5 collective-permute-done.16.c_ref
  114.9 2.1 collective-permute-done.17.d_ref
  117.0 1.3 shard_map.120
  118.4 2.7 %collective-permute-done.21.refs_0_ = bf16[528,1024]{1,0:T(8,128)(2,1)S(1)} collective-permute-done((bf16[528,1024]{1,0:T(8,128)(2,1)S(1)}, bf16[528,1024]{1,0:T(8,128)(2,1)S(1)}, u32[]{:S(2)}, u32[]{:S(2)}) %collective-permute-start.21) | collective-permute-done | bytes 1081376 | tf_op jit(solution)/shard_map/ppermute | solution.py:38
  121.4 1.7 collective-permute-start.22
  123.1 0.9 shard_map.126.refs_0_
  124.0 1.2 collective-permute-start.32
  125.2 2.1 collective-permute-start.33
  127.3 0.9 shard_map.127.refs_5_
  128.5 3.2 %collective-permute-start.37 = (bf16[672,512]{1,0:T(8,128)(2,1)S(1)}, bf16[672,512]{1,0:T(8,128)(2,1)S(1)}, u32[]{:S(2)}, u32[]{:S(2)}) collective-permute-start(bf16[672,512]{1,0:T(8,128)(2,1)S(1)} %shard_map.127.refs_5_), channel_id=1, source_target_pairs={{0,3},{1,0},{2,1},{3,2},{4,7},{5,4},{6,5},{7,6},{8,11},{9,8},{10,9... | collective-permute-start | bytes 2064392 | tf_op jit(solution)/shard_map/ppermute | solution.py:38
  131.8 4.9 %collective-permute-done.22.refs_0_ = bf16[144,1024]{1,0:T(8,128)(2,1)S(1)} collective-permute-done((bf16[144,1024]{1,0:T(8,128)(2,1)S(1)}, bf16[144,1024]{1,0:T(8,128)(2,1)S(1)}, u32[]{:S(2)}, u32[]{:S(2)}) %collective-permute-start.22) | collective-permute-done | bytes 294944 | tf_op jit(solution)/shard_map/ppermute | solution.py:38
  136.6 2.8 %collective-permute-start.23 = (bf16[144,1024]{1,0:T(8,128)(2,1)S(1)}, bf16[144,1024]{1,0:T(8,128)(2,1)S(1)}, u32[]{:S(2)}, u32[]{:S(2)}) collective-permute-start(bf16[144,1024]{1,0:T(8,128)(2,1)S(1)} %get-tuple-element.58), channel_id=1, source_target_pairs={{0,16},{4,20},{8,24},{12,28},{16,0},{20,4},{24,8},{28,12},{1,17},{... | collective-permute-start | bytes 884744 | tf_op jit(solution)/shard_map/ppermute | solution.py:38
  139.4 12.9 %collective-permute-done.23.refs_1_ = bf16[144,1024]{1,0:T(8,128)(2,1)S(1)} collective-permute-done((bf16[144,1024]{1,0:T(8,128)(2,1)S(1)}, bf16[144,1024]{1,0:T(8,128)(2,1)S(1)}, u32[]{:S(2)}, u32[]{:S(2)}) %collective-permute-start.23) | collective-permute-done | bytes 294944 | tf_op jit(solution)/shard_map/ppermute | solution.py:38
  152.3 9.8 %collective-permute-done.24.refs_2_ = bf16[144,1024]{1,0:T(8,128)(2,1)S(1)} collective-permute-done((bf16[144,1024]{1,0:T(8,128)(2,1)S(1)}, bf16[144,1024]{1,0:T(8,128)(2,1)S(1)}, u32[]{:S(2)}, u32[]{:S(2)}) %collective-permute-start.24) | collective-permute-done | bytes 294944 | tf_op jit(solution)/shard_map/ppermute | solution.py:38
  162.3 2.7 %collective-permute-start.25 = (bf16[48,1024]{1,0:T(8,128)(2,1)S(1)}, bf16[48,1024]{1,0:T(8,128)(2,1)S(1)}, u32[]{:S(2)}, u32[]{:S(2)}) collective-permute-start(bf16[48,1024]{1,0:T(8,128)(2,1)S(1)} %get-tuple-element.62), channel_id=1, source_target_pairs={{0,3},{1,0},{2,1},{3,2},{4,7},{5,4},{6,5},{7,6},{8,11},{9,8},{10,9... | collective-permute-start | bytes 294920 | tf_op jit(solution)/shard_map/ppermute | solution.py:38
  165.2 3.3 %collective-permute-start.35 = (bf16[336,512]{1,0:T(8,128)(2,1)S(1)}, bf16[336,512]{1,0:T(8,128)(2,1)S(1)}, u32[]{:S(2)}, u32[]{:S(2)}) collective-permute-start(bf16[336,512]{1,0:T(8,128)(2,1)S(1)} %slice.17), channel_id=1, source_target_pairs={{0,3},{1,0},{2,1},{3,2},{4,7},{5,4},{6,5},{7,6},{8,11},{9,8},{10,9... | collective-permute-start | bytes 1032200 | tf_op jit(solution)/shard_map/ppermute | solution.py:38
  168.6 3.3 %collective-permute-start.39 = (bf16[336,512]{1,0:T(8,128)(2,1)S(1)}, bf16[336,512]{1,0:T(8,128)(2,1)S(1)}, u32[]{:S(2)}, u32[]{:S(2)}) collective-permute-start(bf16[336,512]{1,0:T(8,128)(2,1)S(1)} %slice.19), channel_id=1, source_target_pairs={{0,3},{1,0},{2,1},{3,2},{4,7},{5,4},{6,5},{7,6},{8,11},{9,8},{10,9... | collective-permute-start | bytes 1032200 | tf_op jit(solution)/shard_map/ppermute | solution.py:38
  171.9 11.8 %collective-permute-done.26.b_ref = bf16[48,1024]{1,0:T(8,128)(2,1)S(1)} collective-permute-done((bf16[48,1024]{1,0:T(8,128)(2,1)S(1)}, bf16[48,1024]{1,0:T(8,128)(2,1)S(1)}, u32[]{:S(2)}, u32[]{:S(2)}) %collective-permute-start.26) | collective-permute-done | bytes 98336 | tf_op jit(solution)/shard_map/ppermute | solution.py:38
  183.8 6.1 %collective-permute-done.27.c_ref = bf16[48,1024]{1,0:T(8,128)(2,1)S(1)} collective-permute-done((bf16[48,1024]{1,0:T(8,128)(2,1)S(1)}, bf16[48,1024]{1,0:T(8,128)(2,1)S(1)}, u32[]{:S(2)}, u32[]{:S(2)}) %collective-permute-start.27) | collective-permute-done | bytes 98336 | tf_op jit(solution)/shard_map/ppermute | solution.py:38
  191.2 3.3 %collective-permute-done.28.b_ref = f32[32,256]{1,0:T(8,128)S(1)} collective-permute-done((f32[32,256]{1,0:T(8,128)S(1)}, f32[32,256]{1,0:T(8,128)S(1)}, u32[]{:S(2)}, u32[]{:S(2)}) %collective-permute-start.28) | collective-permute-done | bytes 32800 | tf_op jit(solution)/shard_map/ppermute | solution.py:38
  194.5 5.1 %collective-permute-done.29.c_ref = f32[32,256]{1,0:T(8,128)S(1)} collective-permute-done((f32[32,256]{1,0:T(8,128)S(1)}, f32[32,256]{1,0:T(8,128)S(1)}, u32[]{:S(2)}, u32[]{:S(2)}) %collective-permute-start.29) | collective-permute-done | bytes 32800 | tf_op jit(solution)/shard_map/ppermute | solution.py:38
  199.8 5.2 %collective-permute-done.30.d_ref = f32[32,256]{1,0:T(8,128)S(1)} collective-permute-done((f32[32,256]{1,0:T(8,128)S(1)}, f32[32,256]{1,0:T(8,128)S(1)}, u32[]{:S(2)}, u32[]{:S(2)}) %collective-permute-start.30) | collective-permute-done | bytes 32800 | tf_op jit(solution)/shard_map/ppermute | solution.py:38
  205.6 4.5 %shard_map.128 = (bf16[512,1792]{1,0:T(8,128)(2,1)}, bf16[512,1792]{1,0:T(8,128)(2,1)}, bf16[1792,512]{1,0:T(8,128)(2,1)}) custom-call(s32[1]{0:T(128)} %bitcast.2.at_ref, bf16[672,512]{1,0:T(8,128)(2,1)S(1)} %shard_map.126.refs_0_, bf16[672,512]{1,0:T(8,128)(2,1)S(1)} %collective-permute-done.32.refs_1_, ...), custom_call_target="tpu_custom_call" | custom-call | tf_op jit(solution)/shard_map/pallas_call | solution.py:98
  210.1 2.9 %collective-permute-done.31.b_ref = f32[32,256]{1,0:T(8,128)S(1)} collective-permute-done((f32[32,256]{1,0:T(8,128)S(1)}, f32[32,256]{1,0:T(8,128)S(1)}, u32[]{:S(2)}, u32[]{:S(2)}) %collective-permute-start.31) | collective-permute-done | bytes 32800 | tf_op jit(solution)/shard_map/ppermute | solution.py:38
  (65 shorter events, 12.1 us)
Async XLA Ops:
  0.6 0.8 copy-start.3
  1.4 0.8 copy-start.6
  2.2 7.4 %collective-permute-start = (bf16[32,1024]{1,0:T(8,128)(2,1)S(1)}, bf16[32,1024]{1,0:T(8,128)(2,1)S(1)}, u32[]{:S(2)}, u32[]{:S(2)}) collective-permute-start(bf16[32,1024]{1,0:T(8,128)(2,1)S(1)} %shard_map.109), channel_id=1, source_target_pairs={{0,8},{4,12},{8,16},{12,20},{16,24},{20,28},{24,0},{28,4},{1,9},{5... | collective-permute-start | bytes 196616 | tf_op jit(solution)/shard_map/ppermute | solution.py:38
  4.1 7.8 %collective-permute-start.1 = (bf16[32,1024]{1,0:T(8,128)(2,1)S(1)}, bf16[32,1024]{1,0:T(8,128)(2,1)S(1)}, u32[]{:S(2)}, u32[]{:S(2)}) collective-permute-start(bf16[32,1024]{1,0:T(8,128)(2,1)S(1)} %shard_map.109), channel_id=1, source_target_pairs={{0,16},{4,20},{8,24},{12,28},{16,0},{20,4},{24,8},{28,12},{1,17},{... | collective-permute-start | bytes 196616 | tf_op jit(solution)/shard_map/ppermute | solution.py:38
  7.3 4.8 %collective-permute-start.2 = (bf16[32,1024]{1,0:T(8,128)(2,1)S(1)}, bf16[32,1024]{1,0:T(8,128)(2,1)S(1)}, u32[]{:S(2)}, u32[]{:S(2)}) collective-permute-start(bf16[32,1024]{1,0:T(8,128)(2,1)S(1)} %shard_map.109), channel_id=1, source_target_pairs={{0,24},{4,28},{8,0},{12,4},{16,8},{20,12},{24,16},{28,20},{1,25},{... | collective-permute-start | bytes 196616 | tf_op jit(solution)/shard_map/ppermute | solution.py:38
  12.2 9.4 %collective-permute-start.3 = (bf16[128,1024]{1,0:T(8,128)(2,1)S(1)}, bf16[128,1024]{1,0:T(8,128)(2,1)S(1)}, u32[]{:S(2)}, u32[]{:S(2)}) collective-permute-start(bf16[128,1024]{1,0:T(8,128)(2,1)S(1)} %pad_maximum_fusion), channel_id=1, source_target_pairs={{0,1},{1,2},{2,3},{3,0},{4,5},{5,6},{6,7},{7,4},{8,9},{9,10},{10,1... | collective-permute-start | bytes 786440 | tf_op jit(solution)/shard_map/ppermute | solution.py:38
  13.9 12.4 %collective-permute-start.4 = (bf16[128,1024]{1,0:T(8,128)(2,1)S(1)}, bf16[128,1024]{1,0:T(8,128)(2,1)S(1)}, u32[]{:S(2)}, u32[]{:S(2)}) collective-permute-start(bf16[128,1024]{1,0:T(8,128)(2,1)S(1)} %pad_maximum_fusion), channel_id=1, source_target_pairs={{0,3},{1,0},{2,1},{3,2},{4,7},{5,4},{6,5},{7,6},{8,11},{9,8},{10,9... | collective-permute-start | bytes 786440 | tf_op jit(solution)/shard_map/ppermute | solution.py:38
  15.5 12.5 %collective-permute-start.5 = (bf16[128,1024]{1,0:T(8,128)(2,1)S(1)}, bf16[128,1024]{1,0:T(8,128)(2,1)S(1)}, u32[]{:S(2)}, u32[]{:S(2)}) collective-permute-start(bf16[128,1024]{1,0:T(8,128)(2,1)S(1)} %pad_maximum_fusion), channel_id=1, source_target_pairs={{0,2},{1,3},{2,0},{3,1},{4,6},{5,7},{6,4},{7,5},{8,10},{9,11},{10,... | collective-permute-start | bytes 786440 | tf_op jit(solution)/shard_map/ppermute | solution.py:38
  28.8 5.7 %collective-permute-start.6 = (bf16[512,1024]{1,0:T(8,128)(2,1)}, bf16[512,1024]{1,0:T(8,128)(2,1)S(1)}, u32[]{:S(2)}, u32[]{:S(2)}) collective-permute-start(bf16[512,1024]{1,0:T(8,128)(2,1)} %get-tuple-element.72), channel_id=1, source_target_pairs={{0,4},{4,0},{8,12},{12,8},{16,20},{20,16},{24,28},{28,24},{1,5},{5... | collective-permute-start | bytes 3145736 | tf_op jit(solution)/shard_map/ppermute | solution.py:38
  28.8 1.5 copy-start
  30.3 1.5 copy-start.1
  31.8 1.5 copy-start.2
  34.5 0.7 copy-start.5
  36.6 12.7 %collective-permute-start.11 = (bf16[688,256]{1,0:T(8,128)(2,1)S(1)}, bf16[688,256]{1,0:T(8,128)(2,1)S(1)}, u32[]{:S(2)}, u32[]{:S(2)}) collective-permute-start(bf16[688,256]{1,0:T(8,128)(2,1)S(1)} %shard_map.113), channel_id=1, source_target_pairs={{0,128},{32,160},{64,192},{96,224},{128,0},{160,32},{192,64},{224,... | collective-permute-start | bytes 1056776 | tf_op jit(solution)/shard_map/ppermute | solution.py:38
  38.1 16.1 %collective-permute-start.12 = (bf16[688,256]{1,0:T(8,128)(2,1)S(1)}, bf16[688,256]{1,0:T(8,128)(2,1)S(1)}, u32[]{:S(2)}, u32[]{:S(2)}) collective-permute-start(bf16[688,256]{1,0:T(8,128)(2,1)S(1)} %shard_map.114), channel_id=1, source_target_pairs={{0,64},{32,96},{64,128},{96,160},{128,192},{160,224},{192,0},{224,... | collective-permute-start | bytes 1056776 | tf_op jit(solution)/shard_map/ppermute | solution.py:38
  40.2 16.2 %collective-permute-start.13 = (bf16[688,256]{1,0:T(8,128)(2,1)S(1)}, bf16[688,256]{1,0:T(8,128)(2,1)S(1)}, u32[]{:S(2)}, u32[]{:S(2)}) collective-permute-start(bf16[688,256]{1,0:T(8,128)(2,1)S(1)} %shard_map.115), channel_id=1, source_target_pairs={{0,192},{32,224},{64,0},{96,32},{128,64},{160,96},{192,128},{224,1... | collective-permute-start | bytes 1056776 | tf_op jit(solution)/shard_map/ppermute | solution.py:38
  57.0 26.3 %collective-permute-start.14 = (bf16[688,256]{1,0:T(8,128)(2,1)S(1)}, bf16[688,256]{1,0:T(8,128)(2,1)S(1)}, u32[]{:S(2)}, u32[]{:S(2)}) collective-permute-start(bf16[688,256]{1,0:T(8,128)(2,1)S(1)} %get-tuple-element.49), channel_id=1, source_target_pairs={{0,32},{32,0},{64,96},{96,64},{128,160},{160,128},{192,224},{224,1... | collective-permute-start | bytes 1056776 | tf_op jit(solution)/shard_map/ppermute | solution.py:38
  63.8 12.6 %collective-permute-start.7 = (bf16[672,256]{1,0:T(8,128)(2,1)S(1)}, bf16[672,256]{1,0:T(8,128)(2,1)S(1)}, u32[]{:S(2)}, u32[]{:S(2)}) collective-permute-start(bf16[672,256]{1,0:T(8,128)(2,1)S(1)} %get-tuple-element.41), channel_id=1, source_target_pairs={{0,128},{32,160},{64,192},{96,224},{128,0},{160,32},{192,64},{224,... | collective-permute-start | bytes 1032200 | tf_op jit(solution)/shard_map/ppermute | solution.py:38
  65.3 15.0 %collective-permute-start.8 = (bf16[672,256]{1,0:T(8,128)(2,1)S(1)}, bf16[672,256]{1,0:T(8,128)(2,1)S(1)}, u32[]{:S(2)}, u32[]{:S(2)}) collective-permute-start(bf16[672,256]{1,0:T(8,128)(2,1)S(1)} %get-tuple-element.42), channel_id=1, source_target_pairs={{0,64},{32,96},{64,128},{96,160},{128,192},{160,224},{192,0},{224,... | collective-permute-start | bytes 1032200 | tf_op jit(solution)/shard_map/ppermute | solution.py:38
  66.5 15.9 %collective-permute-start.9 = (bf16[672,256]{1,0:T(8,128)(2,1)S(1)}, bf16[672,256]{1,0:T(8,128)(2,1)S(1)}, u32[]{:S(2)}, u32[]{:S(2)}) collective-permute-start(bf16[672,256]{1,0:T(8,128)(2,1)S(1)} %get-tuple-element.43), channel_id=1, source_target_pairs={{0,192},{32,224},{64,0},{96,32},{128,64},{160,96},{192,128},{224,1... | collective-permute-start | bytes 1032200 | tf_op jit(solution)/shard_map/ppermute | solution.py:38
  82.9 19.9 %collective-permute-start.10 = (bf16[672,256]{1,0:T(8,128)(2,1)S(1)}, bf16[672,256]{1,0:T(8,128)(2,1)S(1)}, u32[]{:S(2)}, u32[]{:S(2)}) collective-permute-start(bf16[672,256]{1,0:T(8,128)(2,1)S(1)} %get-tuple-element.45), channel_id=1, source_target_pairs={{0,32},{32,0},{64,96},{96,64},{128,160},{160,128},{192,224},{224,1... | collective-permute-start | bytes 1032200 | tf_op jit(solution)/shard_map/ppermute | solution.py:38
  83.6 21.8 %collective-permute-start.18 = (bf16[672,256]{1,0:T(8,128)(2,1)S(1)}, bf16[672,256]{1,0:T(8,128)(2,1)S(1)}, u32[]{:S(2)}, u32[]{:S(2)}) collective-permute-start(bf16[672,256]{1,0:T(8,128)(2,1)S(1)} %get-tuple-element.51.a_ref), channel_id=1, source_target_pairs={{0,128},{32,160},{64,192},{96,224},{128,0},{160,32},{192,64},{224,... | collective-permute-start | bytes 1032200 | tf_op jit(solution)/shard_map/ppermute | solution.py:38
  85.1 21.5 %collective-permute-start.19 = (bf16[672,256]{1,0:T(8,128)(2,1)S(1)}, bf16[672,256]{1,0:T(8,128)(2,1)S(1)}, u32[]{:S(2)}, u32[]{:S(2)}) collective-permute-start(bf16[672,256]{1,0:T(8,128)(2,1)S(1)} %get-tuple-element.51.a_ref), channel_id=1, source_target_pairs={{0,64},{32,96},{64,128},{96,160},{128,192},{160,224},{192,0},{224,... | collective-permute-start | bytes 1032200 | tf_op jit(solution)/shard_map/ppermute | solution.py:38
  86.3 20.3 %collective-permute-start.20 = (bf16[672,256]{1,0:T(8,128)(2,1)S(1)}, bf16[672,256]{1,0:T(8,128)(2,1)S(1)}, u32[]{:S(2)}, u32[]{:S(2)}) collective-permute-start(bf16[672,256]{1,0:T(8,128)(2,1)S(1)} %get-tuple-element.51.a_ref), channel_id=1, source_target_pairs={{0,192},{32,224},{64,0},{96,32},{128,64},{160,96},{192,128},{224,1... | collective-permute-start | bytes 1032200 | tf_op jit(solution)/shard_map/ppermute | solution.py:38
  103.0 10.4 %collective-permute-start.15 = (bf16[672,256]{1,0:T(8,128)(2,1)S(1)}, bf16[672,256]{1,0:T(8,128)(2,1)S(1)}, u32[]{:S(2)}, u32[]{:S(2)}) collective-permute-start(bf16[672,256]{1,0:T(8,128)(2,1)S(1)} %shard_map.118.a_ref), channel_id=1, source_target_pairs={{0,128},{32,160},{64,192},{96,224},{128,0},{160,32},{192,64},{224,... | collective-permute-start | bytes 1032200 | tf_op jit(solution)/shard_map/ppermute | solution.py:38
  104.5 10.4 %collective-permute-start.16 = (bf16[672,256]{1,0:T(8,128)(2,1)S(1)}, bf16[672,256]{1,0:T(8,128)(2,1)S(1)}, u32[]{:S(2)}, u32[]{:S(2)}) collective-permute-start(bf16[672,256]{1,0:T(8,128)(2,1)S(1)} %shard_map.118.a_ref), channel_id=1, source_target_pairs={{0,64},{32,96},{64,128},{96,160},{128,192},{160,224},{192,0},{224,... | collective-permute-start | bytes 1032200 | tf_op jit(solution)/shard_map/ppermute | solution.py:38
  105.4 11.6 %collective-permute-start.17 = (bf16[672,256]{1,0:T(8,128)(2,1)S(1)}, bf16[672,256]{1,0:T(8,128)(2,1)S(1)}, u32[]{:S(2)}, u32[]{:S(2)}) collective-permute-start(bf16[672,256]{1,0:T(8,128)(2,1)S(1)} %shard_map.118.a_ref), channel_id=1, source_target_pairs={{0,192},{32,224},{64,0},{96,32},{128,64},{160,96},{192,128},{224,1... | collective-permute-start | bytes 1032200 | tf_op jit(solution)/shard_map/ppermute | solution.py:38
  118.3 2.8 %collective-permute-start.21 = (bf16[528,1024]{1,0:T(8,128)(2,1)S(1)}, bf16[528,1024]{1,0:T(8,128)(2,1)S(1)}, u32[]{:S(2)}, u32[]{:S(2)}) collective-permute-start(bf16[528,1024]{1,0:T(8,128)(2,1)S(1)} %get-tuple-element.54), channel_id=1, source_target_pairs={{0,4},{4,0},{8,12},{12,8},{16,20},{20,16},{24,28},{28,24},{1,5},{5... | collective-permute-start | bytes 3244040 | tf_op jit(solution)/shard_map/ppermute | solution.py:38
  121.4 15.2 %collective-permute-start.22 = (bf16[144,1024]{1,0:T(8,128)(2,1)S(1)}, bf16[144,1024]{1,0:T(8,128)(2,1)S(1)}, u32[]{:S(2)}, u32[]{:S(2)}) collective-permute-start(bf16[144,1024]{1,0:T(8,128)(2,1)S(1)} %get-tuple-element.57), channel_id=1, source_target_pairs={{0,24},{4,28},{8,0},{12,4},{16,8},{20,12},{24,16},{28,20},{1,25},{... | collective-permute-start | bytes 884744 | tf_op jit(solution)/shard_map/ppermute | solution.py:38
  124.0 41.0 %collective-permute-start.32 = (bf16[672,512]{1,0:T(8,128)(2,1)S(1)}, bf16[672,512]{1,0:T(8,128)(2,1)S(1)}, u32[]{:S(2)}, u32[]{:S(2)}) collective-permute-start(bf16[672,512]{1,0:T(8,128)(2,1)S(1)} %shard_map.126.refs_0_), channel_id=1, source_target_pairs={{0,1},{1,2},{2,3},{3,0},{4,5},{5,6},{6,7},{7,4},{8,9},{9,10},{10,1... | collective-permute-start | bytes 2064392 | tf_op jit(solution)/shard_map/ppermute | solution.py:38
  125.2 39.9 %collective-permute-start.33 = (bf16[672,512]{1,0:T(8,128)(2,1)S(1)}, bf16[672,512]{1,0:T(8,128)(2,1)S(1)}, u32[]{:S(2)}, u32[]{:S(2)}) collective-permute-start(bf16[672,512]{1,0:T(8,128)(2,1)S(1)} %shard_map.126.refs_0_), channel_id=1, source_target_pairs={{0,3},{1,0},{2,1},{3,2},{4,7},{5,4},{6,5},{7,6},{8,11},{9,8},{10,9... | collective-permute-start | bytes 2064392 | tf_op jit(solution)/shard_map/ppermute | solution.py:38
  128.2 40.2 %collective-permute-start.36 = (bf16[672,512]{1,0:T(8,128)(2,1)S(1)}, bf16[672,512]{1,0:T(8,128)(2,1)S(1)}, u32[]{:S(2)}, u32[]{:S(2)}) collective-permute-start(bf16[672,512]{1,0:T(8,128)(2,1)S(1)} %shard_map.127.refs_5_), channel_id=1, source_target_pairs={{0,1},{1,2},{2,3},{3,0},{4,5},{5,6},{6,7},{7,4},{8,9},{9,10},{10,1... | collective-permute-start | bytes 2064392 | tf_op jit(solution)/shard_map/ppermute | solution.py:38
  128.5 40.0 %collective-permute-start.37 = (bf16[672,512]{1,0:T(8,128)(2,1)S(1)}, bf16[672,512]{1,0:T(8,128)(2,1)S(1)}, u32[]{:S(2)}, u32[]{:S(2)}) collective-permute-start(bf16[672,512]{1,0:T(8,128)(2,1)S(1)} %shard_map.127.refs_5_), channel_id=1, source_target_pairs={{0,3},{1,0},{2,1},{3,2},{4,7},{5,4},{6,5},{7,6},{8,11},{9,8},{10,9... | collective-permute-start | bytes 2064392 | tf_op jit(solution)/shard_map/ppermute | solution.py:38
  136.6 53.2 %copy-start.4 = (bf16[32,512]{1,0:T(8,128)(2,1)S(1)}, bf16[32,512]{1,0:T(8,128)(2,1)}, u32[]{:S(2)}) copy-start(bf16[32,512]{1,0:T(8,128)(2,1)} %tok_ref.5) | copy-start | bytes 98308
  136.6 15.7 %collective-permute-start.23 = (bf16[144,1024]{1,0:T(8,128)(2,1)S(1)}, bf16[144,1024]{1,0:T(8,128)(2,1)S(1)}, u32[]{:S(2)}, u32[]{:S(2)}) collective-permute-start(bf16[144,1024]{1,0:T(8,128)(2,1)S(1)} %get-tuple-element.58), channel_id=1, source_target_pairs={{0,16},{4,20},{8,24},{12,28},{16,0},{20,4},{24,8},{28,12},{1,17},{... | collective-permute-start | bytes 884744 | tf_op jit(solution)/shard_map/ppermute | solution.py:38
  152.3 9.8 %collective-permute-start.24 = (bf16[144,1024]{1,0:T(8,128)(2,1)S(1)}, bf16[144,1024]{1,0:T(8,128)(2,1)S(1)}, u32[]{:S(2)}, u32[]{:S(2)}) collective-permute-start(bf16[144,1024]{1,0:T(8,128)(2,1)S(1)} %get-tuple-element.59), channel_id=1, source_target_pairs={{0,8},{4,12},{8,16},{12,20},{16,24},{20,28},{24,0},{28,4},{1,9},{5... | collective-permute-start | bytes 884744 | tf_op jit(solution)/shard_map/ppermute | solution.py:38
  162.3 9.6 %collective-permute-start.25 = (bf16[48,1024]{1,0:T(8,128)(2,1)S(1)}, bf16[48,1024]{1,0:T(8,128)(2,1)S(1)}, u32[]{:S(2)}, u32[]{:S(2)}) collective-permute-start(bf16[48,1024]{1,0:T(8,128)(2,1)S(1)} %get-tuple-element.62), channel_id=1, source_target_pairs={{0,3},{1,0},{2,1},{3,2},{4,7},{5,4},{6,5},{7,6},{8,11},{9,8},{10,9... | collective-permute-start | bytes 294920 | tf_op jit(solution)/shard_map/ppermute | solution.py:38
  165.0 40.5 %collective-permute-start.34 = (bf16[336,512]{1,0:T(8,128)(2,1)S(1)}, bf16[336,512]{1,0:T(8,128)(2,1)S(1)}, u32[]{:S(2)}, u32[]{:S(2)}) collective-permute-start(bf16[336,512]{1,0:T(8,128)(2,1)S(1)} %slice.16), channel_id=1, source_target_pairs={{0,1},{1,2},{2,3},{3,0},{4,5},{5,6},{6,7},{7,4},{8,9},{9,10},{10,1... | collective-permute-start | bytes 1032200 | tf_op jit(solution)/shard_map/ppermute | solution.py:38
  165.2 40.4 %collective-permute-start.35 = (bf16[336,512]{1,0:T(8,128)(2,1)S(1)}, bf16[336,512]{1,0:T(8,128)(2,1)S(1)}, u32[]{:S(2)}, u32[]{:S(2)}) collective-permute-start(bf16[336,512]{1,0:T(8,128)(2,1)S(1)} %slice.17), channel_id=1, source_target_pairs={{0,3},{1,0},{2,1},{3,2},{4,7},{5,4},{6,5},{7,6},{8,11},{9,8},{10,9... | collective-permute-start | bytes 1032200 | tf_op jit(solution)/shard_map/ppermute | solution.py:38
  168.5 37.1 %collective-permute-start.38 = (bf16[336,512]{1,0:T(8,128)(2,1)S(1)}, bf16[336,512]{1,0:T(8,128)(2,1)S(1)}, u32[]{:S(2)}, u32[]{:S(2)}) collective-permute-start(bf16[336,512]{1,0:T(8,128)(2,1)S(1)} %slice.18), channel_id=1, source_target_pairs={{0,1},{1,2},{2,3},{3,0},{4,5},{5,6},{6,7},{7,4},{8,9},{9,10},{10,1... | collective-permute-start | bytes 1032200 | tf_op jit(solution)/shard_map/ppermute | solution.py:38
  168.6 36.9 %collective-permute-start.39 = (bf16[336,512]{1,0:T(8,128)(2,1)S(1)}, bf16[336,512]{1,0:T(8,128)(2,1)S(1)}, u32[]{:S(2)}, u32[]{:S(2)}) collective-permute-start(bf16[336,512]{1,0:T(8,128)(2,1)S(1)} %slice.19), channel_id=1, source_target_pairs={{0,3},{1,0},{2,1},{3,2},{4,7},{5,4},{6,5},{7,6},{8,11},{9,8},{10,9... | collective-permute-start | bytes 1032200 | tf_op jit(solution)/shard_map/ppermute | solution.py:38
  171.9 11.8 %collective-permute-start.26 = (bf16[48,1024]{1,0:T(8,128)(2,1)S(1)}, bf16[48,1024]{1,0:T(8,128)(2,1)S(1)}, u32[]{:S(2)}, u32[]{:S(2)}) collective-permute-start(bf16[48,1024]{1,0:T(8,128)(2,1)S(1)} %get-tuple-element.63), channel_id=1, source_target_pairs={{0,1},{1,2},{2,3},{3,0},{4,5},{5,6},{6,7},{7,4},{8,9},{9,10},{10,1... | collective-permute-start | bytes 294920 | tf_op jit(solution)/shard_map/ppermute | solution.py:38
  183.8 6.1 %collective-permute-start.27 = (bf16[48,1024]{1,0:T(8,128)(2,1)S(1)}, bf16[48,1024]{1,0:T(8,128)(2,1)S(1)}, u32[]{:S(2)}, u32[]{:S(2)}) collective-permute-start(bf16[48,1024]{1,0:T(8,128)(2,1)S(1)} %get-tuple-element.64), channel_id=1, source_target_pairs={{0,2},{1,3},{2,0},{3,1},{4,6},{5,7},{6,4},{7,5},{8,10},{9,11},{10,... | collective-permute-start | bytes 294920 | tf_op jit(solution)/shard_map/ppermute | solution.py:38
  190.5 3.9 %collective-permute-start.28 = (f32[32,256]{1,0:T(8,128)S(1)}, f32[32,256]{1,0:T(8,128)S(1)}, u32[]{:S(2)}, u32[]{:S(2)}) collective-permute-start(f32[32,256]{1,0:T(8,128)S(1)} %get-tuple-element.66.a_ref), channel_id=1, source_target_pairs={{0,64},{32,96},{64,128},{96,160},{128,192},{160,224},{192,0},{224,... | collective-permute-start | bytes 98312 | tf_op jit(solution)/shard_map/ppermute | solution.py:38
  194.5 5.1 %collective-permute-start.29 = (f32[32,256]{1,0:T(8,128)S(1)}, f32[32,256]{1,0:T(8,128)S(1)}, u32[]{:S(2)}, u32[]{:S(2)}) collective-permute-start(f32[32,256]{1,0:T(8,128)S(1)} %get-tuple-element.66.a_ref), channel_id=1, source_target_pairs={{0,192},{32,224},{64,0},{96,32},{128,64},{160,96},{192,128},{224,1... | collective-permute-start | bytes 98312 | tf_op jit(solution)/shard_map/ppermute | solution.py:38
  199.6 5.4 %collective-permute-start.30 = (f32[32,256]{1,0:T(8,128)S(1)}, f32[32,256]{1,0:T(8,128)S(1)}, u32[]{:S(2)}, u32[]{:S(2)}) collective-permute-start(f32[32,256]{1,0:T(8,128)S(1)} %get-tuple-element.66.a_ref), channel_id=1, source_target_pairs={{0,128},{32,160},{64,192},{96,224},{128,0},{160,32},{192,64},{224,... | collective-permute-start | bytes 98312 | tf_op jit(solution)/shard_map/ppermute | solution.py:38
  205.0 7.9 %copy-start.7 = (bf16[32,512]{1,0:T(8,128)(2,1)S(1)}, bf16[32,512]{1,0:T(8,128)(2,1)}, u32[]{:S(2)}) copy-start(bf16[32,512]{1,0:T(8,128)(2,1)} %cot_ref.3) | copy-start | bytes 98308
  205.0 7.9 %collective-permute-start.31 = (f32[32,256]{1,0:T(8,128)S(1)}, f32[32,256]{1,0:T(8,128)S(1)}, u32[]{:S(2)}, u32[]{:S(2)}) collective-permute-start(f32[32,256]{1,0:T(8,128)S(1)} %shard_map.124.a_ref), channel_id=1, source_target_pairs={{0,32},{32,0},{64,96},{96,64},{128,160},{160,128},{192,224},{224,1... | collective-permute-start | bytes 98312 | tf_op jit(solution)/shard_map/ppermute | solution.py:38

commit v2 on v1

--- a/solution.py
+++ b/solution.py
@@ -92,7 +92,7 @@
         compiler_params=pltpu.CompilerParams(vmem_limit_bytes=limit << 20),
     )
     placed = [
-        a if i < raw or i in hbm_in else pltpu.with_memory_space_constraint(a, pltpu.VMEM)
+        pltpu.with_memory_space_constraint(a, pltpu.HBM if i < raw or i in hbm_in else pltpu.VMEM)
         for i, a in enumerate(args)
     ]
     return run(*scalars, *placed)
@@ -113,6 +113,16 @@
         out_ref[:, 512:] = cot_ref[...]
 
     return call(kernel, [sds((32, 1024), BF)], (), tokens, cotangent, hbm_in=(0, 1))[0]
+
+
+def join_call(parts):
+    rows = parts[0].shape[0]
+
+    def kernel(*refs):
+        for i, ref in enumerate(refs[:-1]):
+            refs[-1][rows * i:rows * (i + 1), :] = ref[...]
+
+    return call(kernel, [sds((rows * len(parts), 1024), BF)], (), *parts)[0]
 
 
 def prepare_call(depth_at, w_gate, w_up, w_down):
@@ -183,7 +193,7 @@
         for k, out_ref in zip(ks, outs):
             write_parts(out_ref, block_part(block_rows(at_ref, k), both_ref, gain_ref, wgu_ref, wd_ref, first), size)
 
-    return call(kernel, [message_shape(size, first)] * len(ks), (x_at,), both, gain, wgu, wd, hbm_in=(1,))
+    return call(kernel, [message_shape(size, first)] * len(ks), (x_at,), both, gain, wgu, wd)
 
 
 def sum_call(x_at, both, gain, wgu, wd, received, size, first):
@@ -198,7 +208,7 @@
         write_parts(out_ref, total, size)
 
     outs = [sds((3 * size + (8 if first else 0), 256), F32), message_shape(size, first)]
-    return call(kernel, outs, (x_at,), both, gain, wgu, wd, *received, hbm_in=(1,))
+    return call(kernel, outs, (x_at,), both, gain, wgu, wd, *received)
 
 
 def middle_call(total, other, inv, size):
@@ -218,10 +228,18 @@
         sig = jax.nn.sigmoid(gate)
         act = gate * sig
         out_ref[:size, :] = (act * up).astype(BF)
-        out_ref[size:2 * size, :] = (grad * up * sig * (1.0 + gate * (1.0 - sig))).astype(BF)
-        out_ref[2 * size:, :] = (grad * act).astype(BF)
-
-    out = sds((3 * size, 256), BF)
+        grad_gate = grad * up * sig * (1.0 + gate * (1.0 - sig))
+        grad_up = grad * act
+        out_ref[size:2 * size, :] = grad_gate.astype(BF)
+        out_ref[2 * size:3 * size, :] = grad_up.astype(BF)
+        inner = jnp.sum(grad_gate * gate + grad_up * up, axis=0, keepdims=True)
+        hi, lo = split(jnp.broadcast_to(inner, (8, 256)))
+        out_ref[3 * size:3 * size + 16, :] = jnp.concatenate([hi, lo], axis=0)
+        if first:
+            hi, lo = split(inv_ref[...])
+            out_ref[3 * size + 16:, :] = jnp.concatenate([hi, lo], axis=0)
+
+    out = sds((3 * size + (32 if first else 16), 256), BF)
     if first:
         return call(kernel, [out, sds((8, 256), F32)], (), total, other)
     return call(kernel, [out], (), total, other, inv)[0], inv
@@ -235,70 +253,100 @@
             rows = block_rows(at_ref, -k)
             u = (both_ref[rows, :512].astype(F32) * gain_ref[...]).astype(BF)
             down = down + nn(ref[:size, :], both_ref[rows, 512:])
-            gate_up = gate_up + nn(ref[size:, :], u)
+            gate_up = gate_up + nn(ref[size:3 * size, :], u)
         out_ref[:size, :] = down.astype(BF)
         out_ref[size:, :] = gate_up.astype(BF)
 
-    return call(kernel, [sds((3 * size, 512), BF)], (x_at,), *pieces, both, gain, hbm_in=(5,))[0]
-
-
-def write_gain(ref, rows, vector):
-    hi, lo = split(vector)
-    ref[rows:, :512] = jnp.concatenate([hi, hi], axis=0)
-    ref[rows:, 512:] = jnp.concatenate([lo, lo], axis=0)
-
-
-def read_gain(ref, rows):
-    return ref[rows:rows + 8, :512].astype(F32) + ref[rows:rows + 8, 512:].astype(F32)
+    return call(kernel, [sds((3 * size, 512), BF)], (x_at,), *pieces, both, gain)[0]
+
+
+def write_extra(ref, rows, gain_part, inner):
+    gain_hi, gain_lo = split(gain_part)
+    inner_hi, inner_lo = split(inner)
+    ref[rows:, :512] = jnp.concatenate([gain_hi, inner_hi], axis=0)
+    ref[rows:, 512:] = jnp.concatenate([gain_lo, inner_lo], axis=0)
+
+
+def read_extra(ref, rows):
+    extra = ref[rows:, :].astype(F32)
+    extra = extra[:, :512] + extra[:, 512:]
+    return extra[:8, :], extra[8:, :]
+
+
+def read_pair(ref, at):
+    return ref[at:at + 8, :].astype(F32) + ref[at + 8:at + 16, :].astype(F32)
 
 
 def back_call(x_at, pieces, wgu, wd, before, both, size, last):
+    first = before is None
+
     def kernel(at_ref, a_ref, b_ref, c_ref, d_ref, wgu_ref, wd_ref, both_ref, *refs):
         refs = list(refs)
-        before_ref = refs.pop(0) if before is not None else None
+        if not first:
+            before_ref, before_inner_ref = refs.pop(0), refs.pop(0)
         if last:
-            own_ref, gain_ref, out_ref, acc_ref = refs
+            own_ref, gain_ref, own_inner_ref, out_ref, acc_ref, inner_ref = refs
         else:
-            acc_ref, = refs
-        vector = jnp.zeros((1, 512), F32)
+            acc_ref, inner_ref, inv_ref, all_inv_ref = refs
+        gain_part = jnp.zeros((1, 512), F32)
         for k, ref in zip((0, 2, 1, -1), (a_ref, b_ref, c_ref, d_ref)):
             rows = block_rows(at_ref, -k)
             mixed = tn(ref[:size, :], wd_ref[...])
-            grad = tn(ref[size:, :], wgu_ref[...])
-            if before is not None:
+            grad = tn(ref[size:3 * size, :], wgu_ref[...])
+            inner = read_pair(ref, 3 * size)
+            if not first:
                 mixed = mixed + before_ref[rows, :512]
                 grad = grad + before_ref[rows, 512:]
+                inner = inner + before_inner_ref[:, rows]
             acc_ref[rows, :512] = mixed
             acc_ref[rows, 512:] = grad
+            inner_ref[:, rows] = inner
+            if first:
+                all_inv_ref[:, rows] = read_pair(ref, 3 * size + 16)
             if last:
-                vector = vector + jnp.sum(grad * both_ref[rows, :512].astype(F32), axis=0, keepdims=True)
+                gain_part = gain_part + jnp.sum(grad * both_ref[rows, :512].astype(F32), axis=0, keepdims=True)
+        if first:
+            inv_ref[...] = all_inv_ref[:, :128]
         if last:
             own_ref[...] = acc_ref[:512, :]
+            own_inner_ref[...] = inner_ref[:, :512]
             out_ref[:512, :] = acc_ref[512:, :].astype(BF)
-            vector = jnp.broadcast_to(vector, (8, 512))
-            gain_ref[...] = vector
-            write_gain(out_ref, 512, vector)
-
-    args = list(pieces) + [wgu, wd, both] + ([before] if before is not None else [])
+            gain_part = jnp.broadcast_to(gain_part, (8, 512))
+            gain_ref[...] = gain_part
+            write_extra(out_ref, 512, gain_part, inner_ref[:, 512:])
+
+    args = list(pieces) + [wgu, wd, both] + ([] if first else list(before))
+    acc, inner = sds((1024, 1024), F32), sds((8, 1024), F32)
     if last:
-        outs = [sds((512, 1024), F32), sds((8, 512), F32), sds((528, 1024), BF)]
-        return call(kernel, outs, (x_at,), *args, scratch=[pltpu.VMEM((1024, 1024), F32)])
-    return call(kernel, [sds((1024, 1024), F32)], (x_at,), *args)[0]
-
-
-def fold_call(own, vector, messages, strips):
+        outs = [sds((512, 1024), F32), sds((8, 512), F32), sds((8, 512), F32), sds((528, 1024), BF)]
+        scratch = [pltpu.VMEM(acc.shape, F32), pltpu.VMEM(inner.shape, F32)]
+        return call(kernel, outs, (x_at,), *args, scratch=scratch)
+    return call(kernel, [acc, inner, sds((8, 128), F32)], (x_at,), *args, scratch=[pltpu.VMEM((8, 1024), F32)])
+
+
+def turn_left(inner, lanes):
+    if not lanes:
+        return inner
+    return jnp.concatenate(
+        [pltpu.roll(inner[:, 128 * i:128 * (i + 1)], 128 - lanes, 1) for i in range(4)], axis=1)
+
+
+def fold_call(own, gain_part, inner, messages, turns, strips):
     rows = own.shape[0]
     count = len(messages)
     keep = sum(size for _, size in strips[0])
 
-    def kernel(own_ref, vector_ref, *refs):
+    def kernel(own_ref, gain_ref, inner_ref, *refs):
         received = refs[:count]
-        keep_ref, gain_ref = refs[count:count + 2]
-        outs = refs[count + 2:]
-        vec = vector_ref[...]
-        for ref in received:
-            vec = vec + read_gain(ref, rows)
-        gain_ref[...] = vec
+        keep_ref, gain_out_ref, inner_out_ref = refs[count:count + 3]
+        outs = refs[count + 3:]
+        gain_sum, inner_sum = gain_ref[...], inner_ref[...]
+        for ref, lanes in zip(received, turns):
+            gain_more, inner_more = read_extra(ref, rows)
+            gain_sum = gain_sum + gain_more
+            inner_sum = inner_sum + turn_left(inner_more, lanes)
+        gain_out_ref[...] = gain_sum
+        inner_out_ref[...] = inner_sum
         for strip, out in zip(strips, (keep_ref,) + tuple(outs)):
             to = 0
             for at, size in strip:
@@ -308,47 +356,36 @@
                 out[to:to + size, :] = total.astype(out.dtype)
                 to += size
         for ref in outs:
-            write_gain(ref, keep, vec)
-
-    outs = [sds((keep, 1024), F32), sds((8, 512), F32)] + [sds((keep + 16, 1024), BF)] * (len(strips) - 1)
-    return call(kernel, outs, (), own, vector, *messages)
-
-
-def final_call(own, vector, messages, tokens, gain):
-    def kernel(own_ref, vector_ref, a_ref, b_ref, c_ref, tok_ref, gain_ref, out_ref, g_ref, vec_ref, stat_ref):
+            write_extra(ref, keep, gain_sum, inner_sum)
+
+    outs = [sds((keep, 1024), F32), sds((8, 512), F32), sds((8, 512), F32)]
+    outs += [sds((keep + 16, 1024), BF)] * (len(strips) - 1)
+    return call(kernel, outs, (), own, gain_part, inner, *messages)
+
+
+def as_column(rows):
+    hi, lo = split(rows)
+    eighth = jnp.full((16, 128), 0.125, BF)
+    return tn(jnp.concatenate([hi, lo], axis=0), eighth)[:32, :1]
+
+
+def final_call(own, gain_part, inner, inv, messages, tokens, cotangent, gain):
+    def kernel(own_ref, part_ref, inner_ref, inv_ref, a_ref, b_ref, c_ref, tok_ref, cot_ref, gain_ref, out_ref, grad_ref, vec_ref):
         total = own_ref[...]
-        vec = vector_ref[...]
-        for ref in (a_ref, b_ref, c_ref):
+        gain_sum, inner_sum = part_ref[...], inner_ref[:, :128]
+        for i, ref in enumerate((a_ref, b_ref, c_ref)):
             total = total + ref[:32, :].astype(F32)
-            vec = vec + read_gain(ref, 32)
-        vec_ref[...] = vec[:1, :]
+            gain_more, inner_more = read_extra(ref, 32)
+            gain_sum = gain_sum + gain_more
+            inner_sum = inner_sum + inner_more[:, 128 * (i + 1):128 * (i + 2)]
+        vec_ref[...] = gain_sum[:1, :]
         x = tok_ref[...].astype(F32)
         out_ref[...] = (x + total[:, :512]).astype(BF)
-        g = total[:, 512:] * gain_ref[...]
-        g_ref[...] = g
-        stat_ref[:, :128] = jnp.broadcast_to(jnp.sum(x * x, axis=1, keepdims=True), (32, 128))
-        stat_ref[:, 128:] = jnp.broadcast_to(jnp.sum(g * x, axis=1, keepdims=True), (32, 128))
-
-    outs = [sds((32, 512), BF), sds((32, 512), F32), sds((1, 512), F32), sds((32, 256), F32)]
-    return call(kernel, outs, (), own, vector, *messages, tokens, gain, hbm_in=(5, 6), hbm_out=(0, 2))
-
-
-def tail_call(stats, other, cotangent, tokens, g_own):
-    def kernel(a_ref, b_ref, cot_ref, tok_ref, g_ref, out_ref):
-        stat = a_ref[...] + b_ref[...]
-        inv = lax.rsqrt(stat[:, :1] / D + EPS)
-        proj = stat[:, 128:129]
-        x = tok_ref[...].astype(F32)
-        out_ref[...] = (cot_ref[...].astype(F32) + g_ref[...] - x * (inv * inv * (proj / D))).astype(BF)
-
-    return call(kernel, [sds((32, 512), BF)], (), stats, other, cotangent, tokens, g_own, hbm_in=(2, 3), hbm_out=(0,))[0]
-
-
-def add_call(parts):
-    def kernel(a_ref, b_ref, c_ref, d_ref, out_ref):
-        out_ref[...] = a_ref[...] + b_ref[...] + c_ref[...] + d_ref[...]
-
-    return call(kernel, [sds(parts[0].shape, F32)], (), *parts)[0]
+        scale = as_column(inv_ref[...]) * (as_column(inner_sum) / D)
+        grad_ref[...] = (cot_ref[...].astype(F32) + total[:, 512:] * gain_ref[...] - x * scale).astype(BF)
+
+    outs = [sds((32, 512), BF), sds((32, 512), BF), sds((1, 512), F32)]
+    return call(kernel, outs, (), own, gain_part, inner, inv, *messages, tokens, cotangent, gain, hbm_out=(0, 1, 2))
 
 
 def assemble_call(depth_at, groups):
@@ -393,11 +430,11 @@
     count = len(CHUNKS)
 
     both = pack_call(tokens, cotangent)
-    near = [send_zl(both, k) for k in (1, 2, 3)]
+    both = join_call([both] + [send_zl(both, k) for k in (1, 2, 3)])
+    near = [send_y(both, k) for k in (1, -1, 2)]
     weights = prepare_call(depth_at, w_gate, w_up, w_down)
-    both = jnp.concatenate([both] + near, axis=0)
-    both = jnp.concatenate([both] + [send_y(both, k) for k in (1, -1, 2)], axis=0)
-    both = jnp.concatenate([both, send_core(both)], axis=0)
+    both = join_call([both] + near)
+    both = join_call([both, send_core(both)])
     chunks = [(at, size, weights[2 * i], weights[2 * i + 1]) for i, (at, size) in enumerate(CHUNKS)]
 
     received = []
@@ -412,18 +449,22 @@
     for n, (at, size, wgu, wd) in enumerate(chunks):
         total, message = sum_call(x_at, both, gain, wgu, wd, received[n], size, n == 0)
         halves.append((total, send_zh(message)))
-    inv = None
     pieces = []
-    for n, (at, size, wgu, wd) in enumerate(chunks):
+    grads = []
+
+    def middle(n, inv):
+        _, size, _, _ = chunks[n]
         mine, inv = middle_call(*halves[n], inv, size)
         pieces.append([mine] + [send_x(mine, k) for k in (2, 1, -1)])
+        return inv
 
     def weight_grad(n):
         at, size, _, _ = chunks[n]
         grad = weight_grad_call(x_at, pieces[n], both, gain, size)
-        return at, size, grad, send_y(grad, 1), send_y(grad, -1)
-
-    def relay(at, size, grad, prev, after):
+        grads.append((at, size, grad, send_y(grad, 1), send_y(grad, -1)))
+
+    def relay(n):
+        at, size, grad, prev, after = grads[n]
         half = 3 * size // 2
         return at, size, [grad, prev, after, send_y(prev[:half], 1), send_y(after[half:], -1)]
 
@@ -431,26 +472,24 @@
         _, size, wgu, wd = chunks[n]
         return back_call(x_at, pieces[n], wgu, wd, before, both, size, n == count - 1)
 
-    grads = []
-    before = None
-    for n in range(count - 1):
-        grads.append(weight_grad(n))
-        before = back(n, before)
-    own, vector, message = back(count - 1, before)
+    inv = middle(0, None)
+    weight_grad(0)
+    middle(1, inv)
+    *before, inv = back(0, None)
+    groups = [relay(0)]
+    own, gain_part, inner, message = back(1, before)
     message = send_core(message)
-    groups = [relay(*g) for g in grads]
-    last = weight_grad(count - 1)
+    weight_grad(1)
     strips = [[(128 * a + 32 * j, 32) for a in range(4)] for j in range(4)]
-    own, vector, *messages = fold_call(own, vector, [message], strips)
+    own, gain_part, inner, *messages = fold_call(own, gain_part, inner, [message], [0], strips)
     messages = [send_zl(m, -k) for k, m in zip((1, 2, 3), messages)]
-    own, vector, *messages = fold_call(own, vector, messages, [[(32 * j, 32)] for j in range(4)])
+    groups.append(relay(1))
+    strips = [[(32 * j, 32)] for j in range(4)]
+    own, gain_part, inner, *messages = fold_call(own, gain_part, inner, messages, [32, 64, 96], strips)
     messages = [send_y(m, k) for k, m in zip((-1, 1, 2), messages)]
-    groups.append(relay(*last))
-    output, g_own, vector, stats = final_call(own, vector, messages, tokens, gain)
-    stats = add_call([stats] + [send_x(stats, k) for k in (1, -1, 2)])
-    grad_tokens = tail_call(stats, send_zh(stats), cotangent, tokens, g_own)
+    output, grad_tokens, gain_grad = final_call(own, gain_part, inner, inv, messages, tokens, cotangent, gain)
     out_gate, out_up, out_down = assemble_call(depth_at, groups)
-    return output, grad_tokens, vector[0], out_gate, out_up, out_down
+    return output, grad_tokens, gain_grad[0], out_gate, out_up, out_down
 
 
 def solution(mesh):

time: 214 us -> 178 us (0.83)
  the two profiles are of different devices: /device:TPU:6 before, /device:TPU:1 now
where the time goes in v2:
time: 178 us; the launch traced here: 175 us
  waiting for transfers between devices  106 us (60%)
  starting transfers between devices  51.3 us (29%)
  Pallas kernels  16.4 us (9%)
    ppermute x36, waiting for transfers between devices, send(): return lax.ppermute(v, axis, perm)  106 us
    ppermute x36, starting transfers between devices, send(): return lax.ppermute(v, axis, perm)  51.3 us
    pallas_call x21, Pallas kernels, call(): return run(*scalars, *placed)  16.4 us
  transfers between devices with their start and end apart: 36, of which 19 were waited for; matrix products, arithmetic and copies ran while one was open for 0% of the time, Pallas kernels for 6%

profile of v2, /device:TPU:1, one launch (start us, length us, event | category | flops | bytes accessed | tf_op | source)
XLA Modules:
  0.0 175.0 jit_solution(12518289628360201558)
XLA Ops:
  0.6 0.8 shard_map.109.refs_0_
  1.4 2.5 %collective-permute-start = (bf16[32,1024]{1,0:T(8,128)(2,1)S(1)}, bf16[32,1024]{1,0:T(8,128)(2,1)S(1)}, u32[]{:S(2)}, u32[]{:S(2)}) collective-permute-start(bf16[32,1024]{1,0:T(8,128)(2,1)S(1)} %shard_map.109.refs_0_), channel_id=1, source_target_pairs={{0,8},{4,12},{8,16},{12,20},{16,24},{20,28},{24,0},{28,4},{1,9},{5... | collective-permute-start | bytes 196616 | tf_op jit(solution)/shard_map/ppermute | solution.py:38
  3.9 3.0 %collective-permute-start.1 = (bf16[32,1024]{1,0:T(8,128)(2,1)S(1)}, bf16[32,1024]{1,0:T(8,128)(2,1)S(1)}, u32[]{:S(2)}, u32[]{:S(2)}) collective-permute-start(bf16[32,1024]{1,0:T(8,128)(2,1)S(1)} %shard_map.109.refs_0_), channel_id=1, source_target_pairs={{0,16},{4,20},{8,24},{12,28},{16,0},{20,4},{24,8},{28,12},{1,17},{... | collective-permute-start | bytes 196616 | tf_op jit(solution)/shard_map/ppermute | solution.py:38
  6.9 0.7 collective-permute-start.2
  7.6 0.7 collective-permute-done.refs_1_
  8.3 3.5 %collective-permute-done.1.refs_2_ = bf16[32,1024]{1,0:T(8,128)(2,1)S(1)} collective-permute-done((bf16[32,1024]{1,0:T(8,128)(2,1)S(1)}, bf16[32,1024]{1,0:T(8,128)(2,1)S(1)}, u32[]{:S(2)}, u32[]{:S(2)}) %collective-permute-start.1) | collective-permute-done | bytes 65568 | tf_op jit(solution)/shard_map/ppermute | solution.py:38
  11.7 0.7 collective-permute-done.2.refs_3_
  12.4 0.9 collective-permute-start.3
  13.3 1.9 %collective-permute-start.4 = (bf16[128,1024]{1,0:T(8,128)(2,1)S(1)}, bf16[128,1024]{1,0:T(8,128)(2,1)S(1)}, u32[]{:S(2)}, u32[]{:S(2)}) collective-permute-start(bf16[128,1024]{1,0:T(8,128)(2,1)S(1)} %shard_map.110.refs_0_), channel_id=1, source_target_pairs={{0,3},{1,0},{2,1},{3,2},{4,7},{5,4},{6,5},{7,6},{8,11},{9,8},{10,9... | collective-permute-start | bytes 786440 | tf_op jit(solution)/shard_map/ppermute | solution.py:38
  15.2 1.2 collective-permute-start.5
  16.4 4.5 %collective-permute-done.3.refs_1_ = bf16[128,1024]{1,0:T(8,128)(2,1)S(1)} collective-permute-done((bf16[128,1024]{1,0:T(8,128)(2,1)S(1)}, bf16[128,1024]{1,0:T(8,128)(2,1)S(1)}, u32[]{:S(2)}, u32[]{:S(2)}) %collective-permute-start.3) | collective-permute-done | bytes 262176 | tf_op jit(solution)/shard_map/ppermute | solution.py:38
  20.9 6.0 %collective-permute-done.5.refs_3_ = bf16[128,1024]{1,0:T(8,128)(2,1)S(1)} collective-permute-done((bf16[128,1024]{1,0:T(8,128)(2,1)S(1)}, bf16[128,1024]{1,0:T(8,128)(2,1)S(1)}, u32[]{:S(2)}, u32[]{:S(2)}) %collective-permute-start.5) | collective-permute-done | bytes 262176 | tf_op jit(solution)/shard_map/ppermute | solution.py:38
  26.9 2.0 %collective-permute-start.6 = (bf16[512,1024]{1,0:T(8,128)(2,1)S(1)}, bf16[512,1024]{1,0:T(8,128)(2,1)S(1)}, u32[]{:S(2)}, u32[]{:S(2)}) collective-permute-start(bf16[512,1024]{1,0:T(8,128)(2,1)S(1)} %shard_map.111.refs_0_), channel_id=1, source_target_pairs={{0,4},{4,0},{8,12},{12,8},{16,20},{20,16},{24,28},{28,24},{1,5},{5... | collective-permute-start | bytes 3145736 | tf_op jit(solution)/shard_map/ppermute | solution.py:38
  28.9 1.5 shard_map.113
  30.5 0.7 collective-permute-done.6.refs_1_
  31.4 0.5 shard_map.116
  31.9 0.5 shard_map.117
  32.4 0.5 shard_map.118
  32.9 2.8 %collective-permute-start.11 = (bf16[688,256]{1,0:T(8,128)(2,1)S(1)}, bf16[688,256]{1,0:T(8,128)(2,1)S(1)}, u32[]{:S(2)}, u32[]{:S(2)}) collective-permute-start(bf16[688,256]{1,0:T(8,128)(2,1)S(1)} %shard_map.116), channel_id=1, source_target_pairs={{0,128},{32,160},{64,192},{96,224},{128,0},{160,32},{192,64},{224,... | collective-permute-start | bytes 1056776 | tf_op jit(solution)/shard_map/ppermute | solution.py:38
  35.7 0.3 collective-permute-start.12
  36.0 2.4 %collective-permute-start.13 = (bf16[688,256]{1,0:T(8,128)(2,1)S(1)}, bf16[688,256]{1,0:T(8,128)(2,1)S(1)}, u32[]{:S(2)}, u32[]{:S(2)}) collective-permute-start(bf16[688,256]{1,0:T(8,128)(2,1)S(1)} %shard_map.118), channel_id=1, source_target_pairs={{0,192},{32,224},{64,0},{96,32},{128,64},{160,96},{192,128},{224,1... | collective-permute-start | bytes 1056776 | tf_op jit(solution)/shard_map/ppermute | solution.py:38
  38.4 5.5 %collective-permute-done.11.a_ref = bf16[688,256]{1,0:T(8,128)(2,1)S(1)} collective-permute-done((bf16[688,256]{1,0:T(8,128)(2,1)S(1)}, bf16[688,256]{1,0:T(8,128)(2,1)S(1)}, u32[]{:S(2)}, u32[]{:S(2)}) %collective-permute-start.11) | collective-permute-done | bytes 352288 | tf_op jit(solution)/shard_map/ppermute | solution.py:38
  43.9 8.2 %collective-permute-done.12.b_ref = bf16[688,256]{1,0:T(8,128)(2,1)S(1)} collective-permute-done((bf16[688,256]{1,0:T(8,128)(2,1)S(1)}, bf16[688,256]{1,0:T(8,128)(2,1)S(1)}, u32[]{:S(2)}, u32[]{:S(2)}) %collective-permute-start.12) | collective-permute-done | bytes 352288 | tf_op jit(solution)/shard_map/ppermute | solution.py:38
  52.1 0.6 shard_map.119
  52.7 5.6 %collective-permute-start.14 = (bf16[688,256]{1,0:T(8,128)(2,1)S(1)}, bf16[688,256]{1,0:T(8,128)(2,1)S(1)}, u32[]{:S(2)}, u32[]{:S(2)}) collective-permute-start(bf16[688,256]{1,0:T(8,128)(2,1)S(1)} %get-tuple-element.54), channel_id=1, source_target_pairs={{0,32},{32,0},{64,96},{96,64},{128,160},{160,128},{192,224},{224,1... | collective-permute-start | bytes 1056776 | tf_op jit(solution)/shard_map/ppermute | solution.py:38
  58.4 0.8 shard_map.114
  59.2 1.2 collective-permute-start.7
  60.4 1.9 %collective-permute-start.8 = (bf16[672,256]{1,0:T(8,128)(2,1)S(1)}, bf16[672,256]{1,0:T(8,128)(2,1)S(1)}, u32[]{:S(2)}, u32[]{:S(2)}) collective-permute-start(bf16[672,256]{1,0:T(8,128)(2,1)S(1)} %get-tuple-element.47), channel_id=1, source_target_pairs={{0,64},{32,96},{64,128},{96,160},{128,192},{160,224},{192,0},{224,... | collective-permute-start | bytes 1032200 | tf_op jit(solution)/shard_map/ppermute | solution.py:38
  62.3 0.8 collective-permute-start.9
  63.1 4.7 %collective-permute-done.14.other_ref = bf16[688,256]{1,0:T(8,128)(2,1)S(1)} collective-permute-done((bf16[688,256]{1,0:T(8,128)(2,1)S(1)}, bf16[688,256]{1,0:T(8,128)(2,1)S(1)}, u32[]{:S(2)}, u32[]{:S(2)}) %collective-permute-start.14) | collective-permute-done | bytes 352288 | tf_op jit(solution)/shard_map/ppermute | solution.py:38
  67.8 0.3 shard_map.120
  68.2 0.6 collective-permute-start.18
  68.7 0.8 collective-permute-done.7.a_ref
  69.5 9.8 %collective-permute-done.8.b_ref = bf16[672,256]{1,0:T(8,128)(2,1)S(1)} collective-permute-done((bf16[672,256]{1,0:T(8,128)(2,1)S(1)}, bf16[672,256]{1,0:T(8,128)(2,1)S(1)}, u32[]{:S(2)}, u32[]{:S(2)}) %collective-permute-start.8) | collective-permute-done | bytes 344096 | tf_op jit(solution)/shard_map/ppermute | solution.py:38
  79.3 0.5 shard_map.115
  79.9 1.2 collective-permute-start.19
  81.1 1.5 collective-permute-start.20
  82.7 15.8 %collective-permute-done.10.other_ref = bf16[672,256]{1,0:T(8,128)(2,1)S(1)} collective-permute-done((bf16[672,256]{1,0:T(8,128)(2,1)S(1)}, bf16[672,256]{1,0:T(8,128)(2,1)S(1)}, u32[]{:S(2)}, u32[]{:S(2)}) %collective-permute-start.10) | collective-permute-done | bytes 344096 | tf_op jit(solution)/shard_map/ppermute | solution.py:38
  98.7 2.5 %collective-permute-start.15 = (bf16[688,256]{1,0:T(8,128)(2,1)S(1)}, bf16[688,256]{1,0:T(8,128)(2,1)S(1)}, u32[]{:S(2)}, u32[]{:S(2)}) collective-permute-start(bf16[688,256]{1,0:T(8,128)(2,1)S(1)} %shard_map.121.a_ref), channel_id=1, source_target_pairs={{0,128},{32,160},{64,192},{96,224},{128,0},{160,32},{192,64},{224,... | collective-permute-start | bytes 1056776 | tf_op jit(solution)/shard_map/ppermute | solution.py:38
  101.2 0.3 collective-permute-start.16
  101.5 2.4 %collective-permute-start.17 = (bf16[688,256]{1,0:T(8,128)(2,1)S(1)}, bf16[688,256]{1,0:T(8,128)(2,1)S(1)}, u32[]{:S(2)}, u32[]{:S(2)}) collective-permute-start(bf16[688,256]{1,0:T(8,128)(2,1)S(1)} %shard_map.121.a_ref), channel_id=1, source_target_pairs={{0,192},{32,224},{64,0},{96,32},{128,64},{160,96},{192,128},{224,1... | collective-permute-start | bytes 1056776 | tf_op jit(solution)/shard_map/ppermute | solution.py:38
  103.9 1.0 shard_map.122
  104.9 2.9 %collective-permute-done.15.b_ref = bf16[688,256]{1,0:T(8,128)(2,1)S(1)} collective-permute-done((bf16[688,256]{1,0:T(8,128)(2,1)S(1)}, bf16[688,256]{1,0:T(8,128)(2,1)S(1)}, u32[]{:S(2)}, u32[]{:S(2)}) %collective-permute-start.15) | collective-permute-done | bytes 352288 | tf_op jit(solution)/shard_map/ppermute | solution.py:38
  107.8 10.1 %collective-permute-done.16.c_ref = bf16[688,256]{1,0:T(8,128)(2,1)S(1)} collective-permute-done((bf16[688,256]{1,0:T(8,128)(2,1)S(1)}, bf16[688,256]{1,0:T(8,128)(2,1)S(1)}, u32[]{:S(2)}, u32[]{:S(2)}) %collective-permute-start.16) | collective-permute-done | bytes 352288 | tf_op jit(solution)/shard_map/ppermute | solution.py:38
  118.0 1.4 shard_map.123
  119.4 0.7 collective-permute-start.21
  120.0 0.9 shard_map.128.refs_5_
  120.9 0.9 collective-permute-start.32
  121.8 1.8 %collective-permute-start.33 = (bf16[672,512]{1,0:T(8,128)(2,1)S(1)}, bf16[672,512]{1,0:T(8,128)(2,1)S(1)}, u32[]{:S(2)}, u32[]{:S(2)}) collective-permute-start(bf16[672,512]{1,0:T(8,128)(2,1)S(1)} %shard_map.128.refs_5_), channel_id=1, source_target_pairs={{0,3},{1,0},{2,1},{3,2},{4,7},{5,4},{6,5},{7,6},{8,11},{9,8},{10,9... | collective-permute-start | bytes 2064392 | tf_op jit(solution)/shard_map/ppermute | solution.py:38
  123.7 0.9 shard_map.127.refs_0_
  124.7 2.7 %collective-permute-start.29 = (bf16[672,512]{1,0:T(8,128)(2,1)S(1)}, bf16[672,512]{1,0:T(8,128)(2,1)S(1)}, u32[]{:S(2)}, u32[]{:S(2)}) collective-permute-start(bf16[672,512]{1,0:T(8,128)(2,1)S(1)} %shard_map.127.refs_0_), channel_id=1, source_target_pairs={{0,3},{1,0},{2,1},{3,2},{4,7},{5,4},{6,5},{7,6},{8,11},{9,8},{10,9... | collective-permute-start | bytes 2064392 | tf_op jit(solution)/shard_map/ppermute | solution.py:38
  127.7 11.5 %collective-permute-done.32.refs_6_ = bf16[672,512]{1,0:T(8,128)(2,1)S(1)} collective-permute-done((bf16[672,512]{1,0:T(8,128)(2,1)S(1)}, bf16[672,512]{1,0:T(8,128)(2,1)S(1)}, u32[]{:S(2)}, u32[]{:S(2)}) %collective-permute-start.32) | collective-permute-done | bytes 688160 | tf_op jit(solution)/shard_map/ppermute | solution.py:38
  139.3 14.6 %collective-permute-done.28.refs_1_ = bf16[672,512]{1,0:T(8,128)(2,1)S(1)} collective-permute-done((bf16[672,512]{1,0:T(8,128)(2,1)S(1)}, bf16[672,512]{1,0:T(8,128)(2,1)S(1)}, u32[]{:S(2)}, u32[]{:S(2)}) %collective-permute-start.28) | collective-permute-done | bytes 688160 | tf_op jit(solution)/shard_map/ppermute | solution.py:38
  153.9 0.4 collective-permute-start.35
  154.3 2.3 %collective-permute-start.24 = (bf16[144,1024]{1,0:T(8,128)(2,1)S(1)}, bf16[144,1024]{1,0:T(8,128)(2,1)S(1)}, u32[]{:S(2)}, u32[]{:S(2)}) collective-permute-start(bf16[144,1024]{1,0:T(8,128)(2,1)S(1)} %get-tuple-element.68), channel_id=1, source_target_pairs={{0,8},{4,12},{8,16},{12,20},{16,24},{20,28},{24,0},{28,4},{1,9},{5... | collective-permute-start | bytes 884744 | tf_op jit(solution)/shard_map/ppermute | solution.py:38
  156.6 1.2 collective-permute-start.30
  157.8 1.6 collective-permute-start.31
  159.4 3.6 %collective-permute-done.24.refs_2_ = bf16[144,1024]{1,0:T(8,128)(2,1)S(1)} collective-permute-done((bf16[144,1024]{1,0:T(8,128)(2,1)S(1)}, bf16[144,1024]{1,0:T(8,128)(2,1)S(1)}, u32[]{:S(2)}, u32[]{:S(2)}) %collective-permute-start.24) | collective-permute-done | bytes 294944 | tf_op jit(solution)/shard_map/ppermute | solution.py:38
  163.2 2.6 %collective-permute-start.25 = (bf16[48,1024]{1,0:T(8,128)(2,1)S(1)}, bf16[48,1024]{1,0:T(8,128)(2,1)S(1)}, u32[]{:S(2)}, u32[]{:S(2)}) collective-permute-start(bf16[48,1024]{1,0:T(8,128)(2,1)S(1)} %get-tuple-element.73), channel_id=1, source_target_pairs={{0,3},{1,0},{2,1},{3,2},{4,7},{5,4},{6,5},{7,6},{8,11},{9,8},{10,9... | collective-permute-start | bytes 294920 | tf_op jit(solution)/shard_map/ppermute | solution.py:38
  165.8 1.3 collective-permute-start.27
  167.1 0.8 collective-permute-done.30.refs_3_
  167.9 1.6 collective-permute-done.31.refs_4_
  169.5 4.5 %shard_map.129 = (bf16[512,1792]{1,0:T(8,128)(2,1)}, bf16[512,1792]{1,0:T(8,128)(2,1)}, bf16[1792,512]{1,0:T(8,128)(2,1)}) custom-call(s32[1]{0:T(128)} %bitcast.2.at_ref, bf16[672,512]{1,0:T(8,128)(2,1)S(1)} %shard_map.127.refs_0_, bf16[672,512]{1,0:T(8,128)(2,1)S(1)} %collective-permute-done.28.refs_1_, ...), custom_call_target="tpu_custom_call" | custom-call | tf_op jit(solution)/shard_map/pallas_call | solution.py:98
  174.1 0.9 shard_map.126
  (39 shorter events, 1.4 us)
Async XLA Ops:
  1.4 6.9 %collective-permute-start = (bf16[32,1024]{1,0:T(8,128)(2,1)S(1)}, bf16[32,1024]{1,0:T(8,128)(2,1)S(1)}, u32[]{:S(2)}, u32[]{:S(2)}) collective-permute-start(bf16[32,1024]{1,0:T(8,128)(2,1)S(1)} %shard_map.109.refs_0_), channel_id=1, source_target_pairs={{0,8},{4,12},{8,16},{12,20},{16,24},{20,28},{24,0},{28,4},{1,9},{5... | collective-permute-start | bytes 196616 | tf_op jit(solution)/shard_map/ppermute | solution.py:38
  3.9 7.9 %collective-permute-start.1 = (bf16[32,1024]{1,0:T(8,128)(2,1)S(1)}, bf16[32,1024]{1,0:T(8,128)(2,1)S(1)}, u32[]{:S(2)}, u32[]{:S(2)}) collective-permute-start(bf16[32,1024]{1,0:T(8,128)(2,1)S(1)} %shard_map.109.refs_0_), channel_id=1, source_target_pairs={{0,16},{4,20},{8,24},{12,28},{16,0},{20,4},{24,8},{28,12},{1,17},{... | collective-permute-start | bytes 196616 | tf_op jit(solution)/shard_map/ppermute | solution.py:38
  6.9 5.5 %collective-permute-start.2 = (bf16[32,1024]{1,0:T(8,128)(2,1)S(1)}, bf16[32,1024]{1,0:T(8,128)(2,1)S(1)}, u32[]{:S(2)}, u32[]{:S(2)}) collective-permute-start(bf16[32,1024]{1,0:T(8,128)(2,1)S(1)} %shard_map.109.refs_0_), channel_id=1, source_target_pairs={{0,24},{4,28},{8,0},{12,4},{16,8},{20,12},{24,16},{28,20},{1,25},{... | collective-permute-start | bytes 196616 | tf_op jit(solution)/shard_map/ppermute | solution.py:38
  12.4 8.4 %collective-permute-start.3 = (bf16[128,1024]{1,0:T(8,128)(2,1)S(1)}, bf16[128,1024]{1,0:T(8,128)(2,1)S(1)}, u32[]{:S(2)}, u32[]{:S(2)}) collective-permute-start(bf16[128,1024]{1,0:T(8,128)(2,1)S(1)} %shard_map.110.refs_0_), channel_id=1, source_target_pairs={{0,1},{1,2},{2,3},{3,0},{4,5},{5,6},{6,7},{7,4},{8,9},{9,10},{10,1... | collective-permute-start | bytes 786440 | tf_op jit(solution)/shard_map/ppermute | solution.py:38
  13.3 7.6 %collective-permute-start.4 = (bf16[128,1024]{1,0:T(8,128)(2,1)S(1)}, bf16[128,1024]{1,0:T(8,128)(2,1)S(1)}, u32[]{:S(2)}, u32[]{:S(2)}) collective-permute-start(bf16[128,1024]{1,0:T(8,128)(2,1)S(1)} %shard_map.110.refs_0_), channel_id=1, source_target_pairs={{0,3},{1,0},{2,1},{3,2},{4,7},{5,4},{6,5},{7,6},{8,11},{9,8},{10,9... | collective-permute-start | bytes 786440 | tf_op jit(solution)/shard_map/ppermute | solution.py:38
  15.2 11.7 %collective-permute-start.5 = (bf16[128,1024]{1,0:T(8,128)(2,1)S(1)}, bf16[128,1024]{1,0:T(8,128)(2,1)S(1)}, u32[]{:S(2)}, u32[]{:S(2)}) collective-permute-start(bf16[128,1024]{1,0:T(8,128)(2,1)S(1)} %shard_map.110.refs_0_), channel_id=1, source_target_pairs={{0,2},{1,3},{2,0},{3,1},{4,6},{5,7},{6,4},{7,5},{8,10},{9,11},{10,... | collective-permute-start | bytes 786440 | tf_op jit(solution)/shard_map/ppermute | solution.py:38
  26.9 4.3 %collective-permute-start.6 = (bf16[512,1024]{1,0:T(8,128)(2,1)S(1)}, bf16[512,1024]{1,0:T(8,128)(2,1)S(1)}, u32[]{:S(2)}, u32[]{:S(2)}) collective-permute-start(bf16[512,1024]{1,0:T(8,128)(2,1)S(1)} %shard_map.111.refs_0_), channel_id=1, source_target_pairs={{0,4},{4,0},{8,12},{12,8},{16,20},{20,16},{24,28},{28,24},{1,5},{5... | collective-permute-start | bytes 3145736 | tf_op jit(solution)/shard_map/ppermute | solution.py:38
  30.5 0.9 copy-start
  32.9 11.0 %collective-permute-start.11 = (bf16[688,256]{1,0:T(8,128)(2,1)S(1)}, bf16[688,256]{1,0:T(8,128)(2,1)S(1)}, u32[]{:S(2)}, u32[]{:S(2)}) collective-permute-start(bf16[688,256]{1,0:T(8,128)(2,1)S(1)} %shard_map.116), channel_id=1, source_target_pairs={{0,128},{32,160},{64,192},{96,224},{128,0},{160,32},{192,64},{224,... | collective-permute-start | bytes 1056776 | tf_op jit(solution)/shard_map/ppermute | solution.py:38
  35.7 16.5 %collective-permute-start.12 = (bf16[688,256]{1,0:T(8,128)(2,1)S(1)}, bf16[688,256]{1,0:T(8,128)(2,1)S(1)}, u32[]{:S(2)}, u32[]{:S(2)}) collective-permute-start(bf16[688,256]{1,0:T(8,128)(2,1)S(1)} %shard_map.117), channel_id=1, source_target_pairs={{0,64},{32,96},{64,128},{96,160},{128,192},{160,224},{192,0},{224,... | collective-permute-start | bytes 1056776 | tf_op jit(solution)/shard_map/ppermute | solution.py:38
  36.0 16.2 %collective-permute-start.13 = (bf16[688,256]{1,0:T(8,128)(2,1)S(1)}, bf16[688,256]{1,0:T(8,128)(2,1)S(1)}, u32[]{:S(2)}, u32[]{:S(2)}) collective-permute-start(bf16[688,256]{1,0:T(8,128)(2,1)S(1)} %shard_map.118), channel_id=1, source_target_pairs={{0,192},{32,224},{64,0},{96,32},{128,64},{160,96},{192,128},{224,1... | collective-permute-start | bytes 1056776 | tf_op jit(solution)/shard_map/ppermute | solution.py:38
  52.7 15.1 %collective-permute-start.14 = (bf16[688,256]{1,0:T(8,128)(2,1)S(1)}, bf16[688,256]{1,0:T(8,128)(2,1)S(1)}, u32[]{:S(2)}, u32[]{:S(2)}) collective-permute-start(bf16[688,256]{1,0:T(8,128)(2,1)S(1)} %get-tuple-element.54), channel_id=1, source_target_pairs={{0,32},{32,0},{64,96},{96,64},{128,160},{160,128},{192,224},{224,1... | collective-permute-start | bytes 1056776 | tf_op jit(solution)/shard_map/ppermute | solution.py:38
  59.2 10.4 %collective-permute-start.7 = (bf16[672,256]{1,0:T(8,128)(2,1)S(1)}, bf16[672,256]{1,0:T(8,128)(2,1)S(1)}, u32[]{:S(2)}, u32[]{:S(2)}) collective-permute-start(bf16[672,256]{1,0:T(8,128)(2,1)S(1)} %get-tuple-element.46), channel_id=1, source_target_pairs={{0,128},{32,160},{64,192},{96,224},{128,0},{160,32},{192,64},{224,... | collective-permute-start | bytes 1032200 | tf_op jit(solution)/shard_map/ppermute | solution.py:38
  60.4 18.9 %collective-permute-start.8 = (bf16[672,256]{1,0:T(8,128)(2,1)S(1)}, bf16[672,256]{1,0:T(8,128)(2,1)S(1)}, u32[]{:S(2)}, u32[]{:S(2)}) collective-permute-start(bf16[672,256]{1,0:T(8,128)(2,1)S(1)} %get-tuple-element.47), channel_id=1, source_target_pairs={{0,64},{32,96},{64,128},{96,160},{128,192},{160,224},{192,0},{224,... | collective-permute-start | bytes 1032200 | tf_op jit(solution)/shard_map/ppermute | solution.py:38
  62.3 17.0 %collective-permute-start.9 = (bf16[672,256]{1,0:T(8,128)(2,1)S(1)}, bf16[672,256]{1,0:T(8,128)(2,1)S(1)}, u32[]{:S(2)}, u32[]{:S(2)}) collective-permute-start(bf16[672,256]{1,0:T(8,128)(2,1)S(1)} %get-tuple-element.48), channel_id=1, source_target_pairs={{0,192},{32,224},{64,0},{96,32},{128,64},{160,96},{192,128},{224,1... | collective-permute-start | bytes 1032200 | tf_op jit(solution)/shard_map/ppermute | solution.py:38
  68.2 33.4 %collective-permute-start.18 = (bf16[704,256]{1,0:T(8,128)(2,1)S(1)}, bf16[704,256]{1,0:T(8,128)(2,1)S(1)}, u32[]{:S(2)}, u32[]{:S(2)}) collective-permute-start(bf16[704,256]{1,0:T(8,128)(2,1)S(1)} %get-tuple-element.56.a_ref), channel_id=1, source_target_pairs={{0,128},{32,160},{64,192},{96,224},{128,0},{160,32},{192,64},{224,... | collective-permute-start | bytes 1081352 | tf_op jit(solution)/shard_map/ppermute | solution.py:38
  79.8 18.7 %collective-permute-start.10 = (bf16[672,256]{1,0:T(8,128)(2,1)S(1)}, bf16[672,256]{1,0:T(8,128)(2,1)S(1)}, u32[]{:S(2)}, u32[]{:S(2)}) collective-permute-start(bf16[672,256]{1,0:T(8,128)(2,1)S(1)} %get-tuple-element.50), channel_id=1, source_target_pairs={{0,32},{32,0},{64,96},{96,64},{128,160},{160,128},{192,224},{224,1... | collective-permute-start | bytes 1032200 | tf_op jit(solution)/shard_map/ppermute | solution.py:38
  79.9 24.0 %collective-permute-start.19 = (bf16[704,256]{1,0:T(8,128)(2,1)S(1)}, bf16[704,256]{1,0:T(8,128)(2,1)S(1)}, u32[]{:S(2)}, u32[]{:S(2)}) collective-permute-start(bf16[704,256]{1,0:T(8,128)(2,1)S(1)} %get-tuple-element.56.a_ref), channel_id=1, source_target_pairs={{0,64},{32,96},{64,128},{96,160},{128,192},{160,224},{192,0},{224,... | collective-permute-start | bytes 1081352 | tf_op jit(solution)/shard_map/ppermute | solution.py:38
  81.1 22.7 %collective-permute-start.20 = (bf16[704,256]{1,0:T(8,128)(2,1)S(1)}, bf16[704,256]{1,0:T(8,128)(2,1)S(1)}, u32[]{:S(2)}, u32[]{:S(2)}) collective-permute-start(bf16[704,256]{1,0:T(8,128)(2,1)S(1)} %get-tuple-element.56.a_ref), channel_id=1, source_target_pairs={{0,192},{32,224},{64,0},{96,32},{128,64},{160,96},{192,128},{224,1... | collective-permute-start | bytes 1081352 | tf_op jit(solution)/shard_map/ppermute | solution.py:38
  98.7 9.1 %collective-permute-start.15 = (bf16[688,256]{1,0:T(8,128)(2,1)S(1)}, bf16[688,256]{1,0:T(8,128)(2,1)S(1)}, u32[]{:S(2)}, u32[]{:S(2)}) collective-permute-start(bf16[688,256]{1,0:T(8,128)(2,1)S(1)} %shard_map.121.a_ref), channel_id=1, source_target_pairs={{0,128},{32,160},{64,192},{96,224},{128,0},{160,32},{192,64},{224,... | collective-permute-start | bytes 1056776 | tf_op jit(solution)/shard_map/ppermute | solution.py:38
  101.2 16.8 %collective-permute-start.16 = (bf16[688,256]{1,0:T(8,128)(2,1)S(1)}, bf16[688,256]{1,0:T(8,128)(2,1)S(1)}, u32[]{:S(2)}, u32[]{:S(2)}) collective-permute-start(bf16[688,256]{1,0:T(8,128)(2,1)S(1)} %shard_map.121.a_ref), channel_id=1, source_target_pairs={{0,64},{32,96},{64,128},{96,160},{128,192},{160,224},{192,0},{224,... | collective-permute-start | bytes 1056776 | tf_op jit(solution)/shard_map/ppermute | solution.py:38
  101.5 16.4 %collective-permute-start.17 = (bf16[688,256]{1,0:T(8,128)(2,1)S(1)}, bf16[688,256]{1,0:T(8,128)(2,1)S(1)}, u32[]{:S(2)}, u32[]{:S(2)}) collective-permute-start(bf16[688,256]{1,0:T(8,128)(2,1)S(1)} %shard_map.121.a_ref), channel_id=1, source_target_pairs={{0,192},{32,224},{64,0},{96,32},{128,64},{160,96},{192,128},{224,1... | collective-permute-start | bytes 1056776 | tf_op jit(solution)/shard_map/ppermute | solution.py:38
  119.4 8.0 %collective-permute-start.21 = (bf16[528,1024]{1,0:T(8,128)(2,1)S(1)}, bf16[528,1024]{1,0:T(8,128)(2,1)S(1)}, u32[]{:S(2)}, u32[]{:S(2)}) collective-permute-start(bf16[528,1024]{1,0:T(8,128)(2,1)S(1)} %get-tuple-element.62), channel_id=1, source_target_pairs={{0,4},{4,0},{8,12},{12,8},{16,20},{20,16},{24,28},{28,24},{1,5},{5... | collective-permute-start | bytes 3244040 | tf_op jit(solution)/shard_map/ppermute | solution.py:38
  120.9 18.3 %collective-permute-start.32 = (bf16[672,512]{1,0:T(8,128)(2,1)S(1)}, bf16[672,512]{1,0:T(8,128)(2,1)S(1)}, u32[]{:S(2)}, u32[]{:S(2)}) collective-permute-start(bf16[672,512]{1,0:T(8,128)(2,1)S(1)} %shard_map.128.refs_5_), channel_id=1, source_target_pairs={{0,1},{1,2},{2,3},{3,0},{4,5},{5,6},{6,7},{7,4},{8,9},{9,10},{10,1... | collective-permute-start | bytes 2064392 | tf_op jit(solution)/shard_map/ppermute | solution.py:38
  121.8 17.4 %collective-permute-start.33 = (bf16[672,512]{1,0:T(8,128)(2,1)S(1)}, bf16[672,512]{1,0:T(8,128)(2,1)S(1)}, u32[]{:S(2)}, u32[]{:S(2)}) collective-permute-start(bf16[672,512]{1,0:T(8,128)(2,1)S(1)} %shard_map.128.refs_5_), channel_id=1, source_target_pairs={{0,3},{1,0},{2,1},{3,2},{4,7},{5,4},{6,5},{7,6},{8,11},{9,8},{10,9... | collective-permute-start | bytes 2064392 | tf_op jit(solution)/shard_map/ppermute | solution.py:38
  124.6 29.3 %collective-permute-start.28 = (bf16[672,512]{1,0:T(8,128)(2,1)S(1)}, bf16[672,512]{1,0:T(8,128)(2,1)S(1)}, u32[]{:S(2)}, u32[]{:S(2)}) collective-permute-start(bf16[672,512]{1,0:T(8,128)(2,1)S(1)} %shard_map.127.refs_0_), channel_id=1, source_target_pairs={{0,1},{1,2},{2,3},{3,0},{4,5},{5,6},{6,7},{7,4},{8,9},{9,10},{10,1... | collective-permute-start | bytes 2064392 | tf_op jit(solution)/shard_map/ppermute | solution.py:38
  124.7 29.6 %collective-permute-start.29 = (bf16[672,512]{1,0:T(8,128)(2,1)S(1)}, bf16[672,512]{1,0:T(8,128)(2,1)S(1)}, u32[]{:S(2)}, u32[]{:S(2)}) collective-permute-start(bf16[672,512]{1,0:T(8,128)(2,1)S(1)} %shard_map.127.refs_0_), channel_id=1, source_target_pairs={{0,3},{1,0},{2,1},{3,2},{4,7},{5,4},{6,5},{7,6},{8,11},{9,8},{10,9... | collective-permute-start | bytes 2064392 | tf_op jit(solution)/shard_map/ppermute | solution.py:38
  127.6 29.0 %collective-permute-start.22 = (bf16[144,1024]{1,0:T(8,128)(2,1)S(1)}, bf16[144,1024]{1,0:T(8,128)(2,1)S(1)}, u32[]{:S(2)}, u32[]{:S(2)}) collective-permute-start(bf16[144,1024]{1,0:T(8,128)(2,1)S(1)} %get-tuple-element.66), channel_id=1, source_target_pairs={{0,24},{4,28},{8,0},{12,4},{16,8},{20,12},{24,16},{28,20},{1,25},{... | collective-permute-start | bytes 884744 | tf_op jit(solution)/shard_map/ppermute | solution.py:38
  139.2 18.6 %collective-permute-start.23 = (bf16[144,1024]{1,0:T(8,128)(2,1)S(1)}, bf16[144,1024]{1,0:T(8,128)(2,1)S(1)}, u32[]{:S(2)}, u32[]{:S(2)}) collective-permute-start(bf16[144,1024]{1,0:T(8,128)(2,1)S(1)} %get-tuple-element.67), channel_id=1, source_target_pairs={{0,16},{4,20},{8,24},{12,28},{16,0},{20,4},{24,8},{28,12},{1,17},{... | collective-permute-start | bytes 884744 | tf_op jit(solution)/shard_map/ppermute | solution.py:38
  139.2 26.6 %collective-permute-start.34 = (bf16[336,512]{1,0:T(8,128)(2,1)S(1)}, bf16[336,512]{1,0:T(8,128)(2,1)S(1)}, u32[]{:S(2)}, u32[]{:S(2)}) collective-permute-start(bf16[336,512]{1,0:T(8,128)(2,1)S(1)} %slice.18), channel_id=1, source_target_pairs={{0,1},{1,2},{2,3},{3,0},{4,5},{5,6},{6,7},{7,4},{8,9},{9,10},{10,1... | collective-permute-start | bytes 1032200 | tf_op jit(solution)/shard_map/ppermute | solution.py:38
  153.9 11.9 %collective-permute-start.35 = (bf16[336,512]{1,0:T(8,128)(2,1)S(1)}, bf16[336,512]{1,0:T(8,128)(2,1)S(1)}, u32[]{:S(2)}, u32[]{:S(2)}) collective-permute-start(bf16[336,512]{1,0:T(8,128)(2,1)S(1)} %slice.19), channel_id=1, source_target_pairs={{0,3},{1,0},{2,1},{3,2},{4,7},{5,4},{6,5},{7,6},{8,11},{9,8},{10,9... | collective-permute-start | bytes 1032200 | tf_op jit(solution)/shard_map/ppermute | solution.py:38
  154.3 8.7 %collective-permute-start.24 = (bf16[144,1024]{1,0:T(8,128)(2,1)S(1)}, bf16[144,1024]{1,0:T(8,128)(2,1)S(1)}, u32[]{:S(2)}, u32[]{:S(2)}) collective-permute-start(bf16[144,1024]{1,0:T(8,128)(2,1)S(1)} %get-tuple-element.68), channel_id=1, source_target_pairs={{0,8},{4,12},{8,16},{12,20},{16,24},{20,28},{24,0},{28,4},{1,9},{5... | collective-permute-start | bytes 884744 | tf_op jit(solution)/shard_map/ppermute | solution.py:38
  156.6 11.2 %collective-permute-start.30 = (bf16[336,512]{1,0:T(8,128)(2,1)S(1)}, bf16[336,512]{1,0:T(8,128)(2,1)S(1)}, u32[]{:S(2)}, u32[]{:S(2)}) collective-permute-start(bf16[336,512]{1,0:T(8,128)(2,1)S(1)} %slice.16), channel_id=1, source_target_pairs={{0,1},{1,2},{2,3},{3,0},{4,5},{5,6},{6,7},{7,4},{8,9},{9,10},{10,1... | collective-permute-start | bytes 1032200 | tf_op jit(solution)/shard_map/ppermute | solution.py:38
  157.8 11.7 %collective-permute-start.31 = (bf16[336,512]{1,0:T(8,128)(2,1)S(1)}, bf16[336,512]{1,0:T(8,128)(2,1)S(1)}, u32[]{:S(2)}, u32[]{:S(2)}) collective-permute-start(bf16[336,512]{1,0:T(8,128)(2,1)S(1)} %slice.17), channel_id=1, source_target_pairs={{0,3},{1,0},{2,1},{3,2},{4,7},{5,4},{6,5},{7,6},{8,11},{9,8},{10,9... | collective-permute-start | bytes 1032200 | tf_op jit(solution)/shard_map/ppermute | solution.py:38
  163.2 10.8 %collective-permute-start.25 = (bf16[48,1024]{1,0:T(8,128)(2,1)S(1)}, bf16[48,1024]{1,0:T(8,128)(2,1)S(1)}, u32[]{:S(2)}, u32[]{:S(2)}) collective-permute-start(bf16[48,1024]{1,0:T(8,128)(2,1)S(1)} %get-tuple-element.73), channel_id=1, source_target_pairs={{0,3},{1,0},{2,1},{3,2},{4,7},{5,4},{6,5},{7,6},{8,11},{9,8},{10,9... | collective-permute-start | bytes 294920 | tf_op jit(solution)/shard_map/ppermute | solution.py:38
  165.8 8.2 %collective-permute-start.26 = (bf16[48,1024]{1,0:T(8,128)(2,1)S(1)}, bf16[48,1024]{1,0:T(8,128)(2,1)S(1)}, u32[]{:S(2)}, u32[]{:S(2)}) collective-permute-start(bf16[48,1024]{1,0:T(8,128)(2,1)S(1)} %get-tuple-element.74), channel_id=1, source_target_pairs={{0,1},{1,2},{2,3},{3,0},{4,5},{5,6},{6,7},{7,4},{8,9},{9,10},{10,1... | collective-permute-start | bytes 294920 | tf_op jit(solution)/shard_map/ppermute | solution.py:38
  165.8 8.2 %copy-start.1 = (bf16[32,512]{1,0:T(8,128)(2,1)S(1)}, bf16[32,512]{1,0:T(8,128)(2,1)}, u32[]{:S(2)}) copy-start(bf16[32,512]{1,0:T(8,128)(2,1)} %tok_ref.3) | copy-start | bytes 98308
  165.8 8.2 %copy-start.2 = (bf16[32,512]{1,0:T(8,128)(2,1)S(1)}, bf16[32,512]{1,0:T(8,128)(2,1)}, u32[]{:S(2)}) copy-start(bf16[32,512]{1,0:T(8,128)(2,1)} %cot_ref.3) | copy-start | bytes 98308
  165.8 8.2 %collective-permute-start.27 = (bf16[48,1024]{1,0:T(8,128)(2,1)S(1)}, bf16[48,1024]{1,0:T(8,128)(2,1)S(1)}, u32[]{:S(2)}, u32[]{:S(2)}) collective-permute-start(bf16[48,1024]{1,0:T(8,128)(2,1)S(1)} %get-tuple-element.75), channel_id=1, source_target_pairs={{0,2},{1,3},{2,0},{3,1},{4,6},{5,7},{6,4},{7,5},{8,10},{9,11},{10,... | collective-permute-start | bytes 294920 | tf_op jit(solution)/shard_map/ppermute | solution.py:38

commit v3 on v2

--- a/solution.py
+++ b/solution.py
@@ -9,7 +9,7 @@
 D = 4096
 EPS = 1e-05
 FS = 448
-CHUNKS = ((0, 224), (224, 224))
+CHUNKS = ((0, 128), (128, 160), (288, 160))
 
 
 BF = jnp.bfloat16
@@ -24,14 +24,14 @@
 
 
 def perm_zl(k):
-    return [(c, ((c // 2 + k) % 4) * 2 + c % 2) for c in range(8)]
+    return [(c, c ^ (2 * k)) for c in range(8)]
 
 
 PERM_CORE = [(c, c ^ 1) for c in range(8)]
 
 
 def perm_y(k):
-    return [(d, (d + k) % 4) for d in range(4)]
+    return [(d, d ^ k) for d in range(4)]
 
 
 def send(v, axis, perm):
@@ -151,7 +151,7 @@
     outs = []
     for _, size in CHUNKS:
         outs += [sds((2 * size, 512), BF), sds((size, 512), BF)]
-    scratch = [pltpu.VMEM((2, 512, 512), BF), pltpu.VMEM((2, 512, 512), BF), pltpu.SemaphoreType.DMA((4,))]
+    scratch = [pltpu.VMEM((2, 512, 512), BF), pltpu.VMEM((2, 512, 512), BF), pltpu.SemaphoreType.DMA((2 + len(CHUNKS),))]
     return call(kernel, outs, (depth_at,), w_gate, w_up, w_down, scratch=scratch, raw=3)
 
 
@@ -245,19 +245,24 @@
     return call(kernel, [out], (), total, other, inv)[0], inv
 
 
-def weight_grad_call(x_at, pieces, both, gain, size):
-    def kernel(at_ref, a_ref, b_ref, c_ref, d_ref, both_ref, gain_ref, out_ref):
-        down = jnp.zeros((size, 512), F32)
-        gate_up = jnp.zeros((2 * size, 512), F32)
-        for k, ref in zip((0, 2, 1, -1), (a_ref, b_ref, c_ref, d_ref)):
-            rows = block_rows(at_ref, -k)
-            u = (both_ref[rows, :512].astype(F32) * gain_ref[...]).astype(BF)
-            down = down + nn(ref[:size, :], both_ref[rows, 512:])
-            gate_up = gate_up + nn(ref[size:3 * size, :], u)
-        out_ref[:size, :] = down.astype(BF)
-        out_ref[size:, :] = gate_up.astype(BF)
-
-    return call(kernel, [sds((3 * size, 512), BF)], (x_at,), *pieces, both, gain)[0]
+def weight_grad_call(x_at, groups, sizes, both, gain):
+    def kernel(at_ref, *refs):
+        both_ref, gain_ref, out_ref = refs[-3:]
+        to = 0
+        for i, size in enumerate(sizes):
+            down = jnp.zeros((size, 512), F32)
+            gate_up = jnp.zeros((2 * size, 512), F32)
+            for k, ref in zip((0, 2, 1, -1), refs[4 * i:4 * i + 4]):
+                rows = block_rows(at_ref, -k)
+                u = (both_ref[rows, :512].astype(F32) * gain_ref[...]).astype(BF)
+                down = down + nn(ref[:size, :], both_ref[rows, 512:])
+                gate_up = gate_up + nn(ref[size:3 * size, :], u)
+            out_ref[to:to + size, :] = down.astype(BF)
+            out_ref[to + size:to + 3 * size, :] = gate_up.astype(BF)
+            to += 3 * size
+
+    pieces = [piece for group in groups for piece in group]
+    return call(kernel, [sds((3 * sum(sizes), 512), BF)], (x_at,), *pieces, both, gain)[0]
 
 
 def write_extra(ref, rows, gain_part, inner):
@@ -286,8 +291,10 @@
             before_ref, before_inner_ref = refs.pop(0), refs.pop(0)
         if last:
             own_ref, gain_ref, own_inner_ref, out_ref, acc_ref, inner_ref = refs
+        elif first:
+            acc_ref, inner_ref, inv_ref, all_inv_ref = refs
         else:
-            acc_ref, inner_ref, inv_ref, all_inv_ref = refs
+            acc_ref, inner_ref = refs
         gain_part = jnp.zeros((1, 512), F32)
         for k, ref in zip((0, 2, 1, -1), (a_ref, b_ref, c_ref, d_ref)):
             rows = block_rows(at_ref, -k)
@@ -321,14 +328,18 @@
         outs = [sds((512, 1024), F32), sds((8, 512), F32), sds((8, 512), F32), sds((528, 1024), BF)]
         scratch = [pltpu.VMEM(acc.shape, F32), pltpu.VMEM(inner.shape, F32)]
         return call(kernel, outs, (x_at,), *args, scratch=scratch)
-    return call(kernel, [acc, inner, sds((8, 128), F32)], (x_at,), *args, scratch=[pltpu.VMEM((8, 1024), F32)])
+    if first:
+        return call(kernel, [acc, inner, sds((8, 128), F32)], (x_at,), *args, scratch=[pltpu.VMEM((8, 1024), F32)])
+    return call(kernel, [acc, inner], (x_at,), *args)
 
 
 def turn_left(inner, lanes):
-    if not lanes:
-        return inner
     return jnp.concatenate(
         [pltpu.roll(inner[:, 128 * i:128 * (i + 1)], 128 - lanes, 1) for i in range(4)], axis=1)
+
+
+def upper_half(inner):
+    return jnp.concatenate([inner[:, 256:], inner[:, 256:]], axis=1)
 
 
 def fold_call(own, gain_part, inner, messages, turns, strips):
@@ -341,10 +352,10 @@
         keep_ref, gain_out_ref, inner_out_ref = refs[count:count + 3]
         outs = refs[count + 3:]
         gain_sum, inner_sum = gain_ref[...], inner_ref[...]
-        for ref, lanes in zip(received, turns):
+        for ref, turn in zip(received, turns):
             gain_more, inner_more = read_extra(ref, rows)
             gain_sum = gain_sum + gain_more
-            inner_sum = inner_sum + turn_left(inner_more, lanes)
+            inner_sum = inner_sum + (turn(inner_more) if turn else inner_more)
         gain_out_ref[...] = gain_sum
         inner_out_ref[...] = inner_sum
         for strip, out in zip(strips, (keep_ref,) + tuple(outs)):
@@ -369,15 +380,12 @@
     return tn(jnp.concatenate([hi, lo], axis=0), eighth)[:32, :1]
 
 
-def final_call(own, gain_part, inner, inv, messages, tokens, cotangent, gain):
-    def kernel(own_ref, part_ref, inner_ref, inv_ref, a_ref, b_ref, c_ref, tok_ref, cot_ref, gain_ref, out_ref, grad_ref, vec_ref):
-        total = own_ref[...]
-        gain_sum, inner_sum = part_ref[...], inner_ref[:, :128]
-        for i, ref in enumerate((a_ref, b_ref, c_ref)):
-            total = total + ref[:32, :].astype(F32)
-            gain_more, inner_more = read_extra(ref, 32)
-            gain_sum = gain_sum + gain_more
-            inner_sum = inner_sum + inner_more[:, 128 * (i + 1):128 * (i + 2)]
+def final_call(own, gain_part, inner, inv, message, tokens, cotangent, gain):
+    def kernel(own_ref, part_ref, inner_ref, inv_ref, a_ref, tok_ref, cot_ref, gain_ref, out_ref, grad_ref, vec_ref):
+        total = own_ref[...] + a_ref[:32, :].astype(F32)
+        gain_more, inner_more = read_extra(a_ref, 32)
+        gain_sum = part_ref[...] + gain_more
+        inner_sum = inner_ref[:, :128] + inner_more[:, 128:256]
         vec_ref[...] = gain_sum[:1, :]
         x = tok_ref[...].astype(F32)
         out_ref[...] = (x + total[:, :512]).astype(BF)
@@ -385,29 +393,31 @@
         grad_ref[...] = (cot_ref[...].astype(F32) + total[:, 512:] * gain_ref[...] - x * scale).astype(BF)
 
     outs = [sds((32, 512), BF), sds((32, 512), BF), sds((1, 512), F32)]
-    return call(kernel, outs, (), own, gain_part, inner, inv, *messages, tokens, cotangent, gain, hbm_out=(0, 1, 2))
+    return call(kernel, outs, (), own, gain_part, inner, inv, message, tokens, cotangent, gain, hbm_out=(0, 1, 2))
 
 
 def assemble_call(depth_at, groups):
-    count = len(groups)
+    counts = [sum(len(pieces) for _, pieces in arrived) for _, arrived in groups]
 
     def kernel(at_ref, *refs):
-        gate_ref, up_ref, down_ref, tgate_ref, tup_ref = refs[5 * count:]
-        for i, (at, size, _) in enumerate(groups):
-            own, prev, after, far_a, far_b = refs[5 * i:5 * i + 5]
-            half = 3 * size // 2
-            for k, ref in ((0, own), (3, prev), (1, after)):
-                start = ((at_ref[0] + k) % 4) * FS + at
-                rows = pl.ds(pl.multiple_of(start, 16), size)
-                down_ref[rows, :] = ref[:size, :]
-                tgate_ref[rows, :] = ref[size:2 * size, :]
-                tup_ref[rows, :] = ref[2 * size:, :]
-            start = ((at_ref[0] + 2) % 4) * FS + at
-            rows = pl.ds(pl.multiple_of(start, 16), size)
-            down_ref[rows, :] = far_a[:size, :]
-            tgate_ref[pl.ds(pl.multiple_of(start, 16), half - size), :] = far_a[size:, :]
-            tgate_ref[pl.ds(pl.multiple_of(start + half - size, 16), 2 * size - half), :] = far_b[:2 * size - half, :]
-            tup_ref[rows, :] = far_b[2 * size - half:, :]
+        gate_ref, up_ref, down_ref, tgate_ref, tup_ref = refs[sum(counts):]
+        refs = list(refs[:sum(counts)])
+        for chunks, arrived in groups:
+            segments = []
+            for at, size in chunks:
+                segments += [(ref, at, size) for ref in (down_ref, tgate_ref, tup_ref)]
+            for source, pieces in arrived:
+                base = (at_ref[0] ^ source) * FS
+                todo = list(segments)
+                for piece in pieces:
+                    ref, to = refs.pop(0), 0
+                    while to < piece.shape[0]:
+                        target, at, size = todo.pop(0)
+                        take = min(size, piece.shape[0] - to)
+                        target[pl.ds(pl.multiple_of(base + at, 16), take), :] = ref[to:to + take, :]
+                        to += take
+                        if take < size:
+                            todo.insert(0, (target, at + take, size - take))
 
         def turn(i, carry):
             cut = pl.ds(pl.multiple_of(i * 128, 128), 128)
@@ -417,7 +427,7 @@
 
         lax.fori_loop(0, 14, turn, 0)
 
-    args = [a for g in groups for a in g[2]]
+    args = [piece for _, arrived in groups for _, pieces in arrived for piece in pieces]
     outs = [sds((512, 4 * FS), BF), sds((512, 4 * FS), BF), sds((4 * FS, 512), BF)]
     scratch = [pltpu.VMEM((4 * FS, 512), BF), pltpu.VMEM((4 * FS, 512), BF)]
     return call(kernel, outs, (depth_at,), *args, scratch=scratch, hbm_out=(0, 1, 2), limit=24)
@@ -430,27 +440,32 @@
     count = len(CHUNKS)
 
     both = pack_call(tokens, cotangent)
-    both = join_call([both] + [send_zl(both, k) for k in (1, 2, 3)])
-    near = [send_y(both, k) for k in (1, -1, 2)]
+    both = join_call([both, send_zl(both, 1)])
+    both = join_call([both, send_zl(both, 2)])
+    near = [send_y(both, k) for k in (1, 2, 3)]
     weights = prepare_call(depth_at, w_gate, w_up, w_down)
     both = join_call([both] + near)
     both = join_call([both, send_core(both)])
     chunks = [(at, size, weights[2 * i], weights[2 * i + 1]) for i, (at, size) in enumerate(CHUNKS)]
 
     received = []
-    for n, (at, size, wgu, wd) in enumerate(chunks):
-        groups = [(2,), (1,), (-1,)] if n == 0 else [(2, 1, -1)]
+
+    def partials(n):
+        _, size, wgu, wd = chunks[n]
         arrived = []
-        for ks in groups:
+        for ks in [(2,), (1,), (-1,)] if n == 0 else [(2, 1, -1)]:
             parts = partial_call(x_at, ks, both, gain, wgu, wd, size, n == 0)
             arrived += [send_x(part, k) for k, part in zip(ks, parts)]
         received.append(arrived)
+
     halves = []
-    for n, (at, size, wgu, wd) in enumerate(chunks):
+
+    def row_sum(n):
+        _, size, wgu, wd = chunks[n]
         total, message = sum_call(x_at, both, gain, wgu, wd, received[n], size, n == 0)
         halves.append((total, send_zh(message)))
+
     pieces = []
-    grads = []
 
     def middle(n, inv):
         _, size, _, _ = chunks[n]
@@ -458,37 +473,55 @@
         pieces.append([mine] + [send_x(mine, k) for k in (2, 1, -1)])
         return inv
 
-    def weight_grad(n):
-        at, size, _, _ = chunks[n]
-        grad = weight_grad_call(x_at, pieces[n], both, gain, size)
-        grads.append((at, size, grad, send_y(grad, 1), send_y(grad, -1)))
-
-    def relay(n):
-        at, size, grad, prev, after = grads[n]
-        half = 3 * size // 2
-        return at, size, [grad, prev, after, send_y(prev[:half], 1), send_y(after[half:], -1)]
+    def weight_grad(ns):
+        grad = weight_grad_call(
+            x_at, [pieces[n] for n in ns], [CHUNKS[n][1] for n in ns], both, gain)
+        arrived = [(0, [grad])]
+        return [CHUNKS[n] for n in ns], arrived
+
+    def spread(group, ks):
+        for k in ks:
+            group[1].append((k, [send_y(group[1][0][1][0], k)]))
+
+    def relay(group):
+        near = {source: pieces[0] for source, pieces in group[1]}
+        half = near[0].shape[0] // 2
+        group[1].append((2, [send_y(near[1][:half], 3), send_y(near[3][half:], 1)]))
 
     def back(n, before):
         _, size, wgu, wd = chunks[n]
         return back_call(x_at, pieces[n], wgu, wd, before, both, size, n == count - 1)
 
+    partials(0)
+    partials(1)
+    row_sum(0)
+    partials(2)
+    row_sum(1)
     inv = middle(0, None)
-    weight_grad(0)
+    row_sum(2)
     middle(1, inv)
-    *before, inv = back(0, None)
-    groups = [relay(0)]
-    own, gain_part, inner, message = back(1, before)
+    *before, own_inv = back(0, None)
+    middle(2, inv)
+    early = weight_grad((0, 1))
+    spread(early, (1, 3))
+    before = back(1, before)
+    own, gain_part, inner, message = back(2, before)
     message = send_core(message)
-    weight_grad(1)
+    late = weight_grad((2,))
     strips = [[(128 * a + 32 * j, 32) for a in range(4)] for j in range(4)]
-    own, gain_part, inner, *messages = fold_call(own, gain_part, inner, [message], [0], strips)
-    messages = [send_zl(m, -k) for k, m in zip((1, 2, 3), messages)]
-    groups.append(relay(1))
-    strips = [[(32 * j, 32)] for j in range(4)]
-    own, gain_part, inner, *messages = fold_call(own, gain_part, inner, messages, [32, 64, 96], strips)
-    messages = [send_y(m, k) for k, m in zip((-1, 1, 2), messages)]
-    output, grad_tokens, gain_grad = final_call(own, gain_part, inner, inv, messages, tokens, cotangent, gain)
-    out_gate, out_up, out_down = assemble_call(depth_at, groups)
+    own, gain_part, inner, *messages = fold_call(own, gain_part, inner, [message], [None], strips)
+    messages = [send_zl(m, k) for k, m in zip((1, 2, 3), messages)]
+    relay(early)
+    spread(late, (1, 3, 2))
+    turns = [lambda v, lanes=lanes: turn_left(v, lanes) for lanes in (32, 64, 96)]
+    own, gain_part, inner, *messages = fold_call(
+        own, gain_part, inner, messages, turns, [[(0, 64)], [(64, 64)]])
+    message = send_y(messages[0], 2)
+    own, gain_part, inner, *messages = fold_call(
+        own, gain_part, inner, [message], [upper_half], [[(0, 32)], [(32, 32)]])
+    message = send_y(messages[0], 1)
+    out_gate, out_up, out_down = assemble_call(depth_at, [early, late])
+    output, grad_tokens, gain_grad = final_call(own, gain_part, inner, own_inv, message, tokens, cotangent, gain)
     return output, grad_tokens, gain_grad[0], out_gate, out_up, out_down
 
 

time: 178 us -> 194 us (1.090)
  the two profiles are of different devices: /device:TPU:1 before, /device:TPU:32 now
where the time goes in v3:
time: 194 us
  waiting for transfers between devices  108 us (56%)
  starting transfers between devices  67 us (35%)
  Pallas kernels  17.8 us (9%)
    ppermute x40, waiting for transfers between devices, send(): return lax.ppermute(v, axis, perm)  108 us
    ppermute x40, starting transfers between devices, send(): return lax.ppermute(v, axis, perm)  67 us
    pallas_call x27, Pallas kernels, call(): return run(*scalars, *placed)  17.8 us
  transfers between devices with their start and end apart: 40, of which 24 were waited for; matrix products, arithmetic and copies ran while one was open for 0% of the time, Pallas kernels for 7%

profile of v3, /device:TPU:32, one launch (start us, length us, event | category | flops | bytes accessed | tf_op | source)
XLA Modules:
  0.0 193.7 jit_solution(2403128657801267096)
XLA Ops:
  0.6 0.8 shard_map.109.refs_0_
  1.4 1.8 collective-permute-start
  3.2 2.4 %collective-permute-done.refs_1_ = bf16[32,1024]{1,0:T(8,128)(2,1)S(1)} collective-permute-done((bf16[32,1024]{1,0:T(8,128)(2,1)S(1)}, bf16[32,1024]{1,0:T(8,128)(2,1)S(1)}, u32[]{:S(2)}, u32[]{:S(2)}) %collective-permute-start) | collective-permute-done | bytes 65568 | tf_op jit(solution)/shard_map/ppermute | solution.py:38
  5.7 3.4 %collective-permute-start.1 = (bf16[64,1024]{1,0:T(8,128)(2,1)S(1)}, bf16[64,1024]{1,0:T(8,128)(2,1)S(1)}, u32[]{:S(2)}, u32[]{:S(2)}) collective-permute-start(bf16[64,1024]{1,0:T(8,128)(2,1)S(1)} %shard_map.110.refs_0_), channel_id=1, source_target_pairs={{0,16},{4,20},{8,24},{12,28},{16,0},{20,4},{24,8},{28,12},{1,17},{... | collective-permute-start | bytes 393224 | tf_op jit(solution)/shard_map/ppermute | solution.py:38
  9.1 4.1 %collective-permute-done.1.refs_1_ = bf16[64,1024]{1,0:T(8,128)(2,1)S(1)} collective-permute-done((bf16[64,1024]{1,0:T(8,128)(2,1)S(1)}, bf16[64,1024]{1,0:T(8,128)(2,1)S(1)}, u32[]{:S(2)}, u32[]{:S(2)}) %collective-permute-start.1) | collective-permute-done | bytes 131104 | tf_op jit(solution)/shard_map/ppermute | solution.py:38
  13.2 1.7 collective-permute-start.2
  14.9 2.9 %collective-permute-start.3 = (bf16[128,1024]{1,0:T(8,128)(2,1)S(1)}, bf16[128,1024]{1,0:T(8,128)(2,1)S(1)}, u32[]{:S(2)}, u32[]{:S(2)}) collective-permute-start(bf16[128,1024]{1,0:T(8,128)(2,1)S(1)} %shard_map.111.refs_0_), channel_id=1, source_target_pairs={{0,2},{1,3},{2,0},{3,1},{4,6},{5,7},{6,4},{7,5},{8,10},{9,11},{10,... | collective-permute-start | bytes 786440 | tf_op jit(solution)/shard_map/ppermute | solution.py:38
  18.0 4.5 %collective-permute-done.2.refs_1_ = bf16[128,1024]{1,0:T(8,128)(2,1)S(1)} collective-permute-done((bf16[128,1024]{1,0:T(8,128)(2,1)S(1)}, bf16[128,1024]{1,0:T(8,128)(2,1)S(1)}, u32[]{:S(2)}, u32[]{:S(2)}) %collective-permute-start.2) | collective-permute-done | bytes 262176 | tf_op jit(solution)/shard_map/ppermute | solution.py:38
  22.5 6.5 %collective-permute-done.3.refs_2_ = bf16[128,1024]{1,0:T(8,128)(2,1)S(1)} collective-permute-done((bf16[128,1024]{1,0:T(8,128)(2,1)S(1)}, bf16[128,1024]{1,0:T(8,128)(2,1)S(1)}, u32[]{:S(2)}, u32[]{:S(2)}) %collective-permute-start.3) | collective-permute-done | bytes 262176 | tf_op jit(solution)/shard_map/ppermute | solution.py:38
  29.0 2.6 %collective-permute-done.4.refs_3_ = bf16[128,1024]{1,0:T(8,128)(2,1)S(1)} collective-permute-done((bf16[128,1024]{1,0:T(8,128)(2,1)S(1)}, bf16[128,1024]{1,0:T(8,128)(2,1)S(1)}, u32[]{:S(2)}, u32[]{:S(2)}) %collective-permute-start.4) | collective-permute-done | bytes 262176 | tf_op jit(solution)/shard_map/ppermute | solution.py:38
  31.7 1.6 shard_map.114
  33.3 1.0 collective-permute-done.5.refs_1_
  34.5 0.7 shard_map.123
  35.3 3.1 %collective-permute-start.17 = (bf16[480,256]{1,0:T(8,128)(2,1)S(1)}, bf16[480,256]{1,0:T(8,128)(2,1)S(1)}, u32[]{:S(2)}, u32[]{:S(2)}) collective-permute-start(bf16[480,256]{1,0:T(8,128)(2,1)S(1)} %get-tuple-element.69), channel_id=1, source_target_pairs={{0,128},{32,160},{64,192},{96,224},{128,0},{160,32},{192,64},{224,... | collective-permute-start | bytes 737288 | tf_op jit(solution)/shard_map/ppermute | solution.py:38
  38.4 0.6 collective-permute-start.18
  39.0 2.6 %collective-permute-start.19 = (bf16[480,256]{1,0:T(8,128)(2,1)S(1)}, bf16[480,256]{1,0:T(8,128)(2,1)S(1)}, u32[]{:S(2)}, u32[]{:S(2)}) collective-permute-start(bf16[480,256]{1,0:T(8,128)(2,1)S(1)} %get-tuple-element.71), channel_id=1, source_target_pairs={{0,192},{32,224},{64,0},{96,32},{128,64},{160,96},{192,128},{224,1... | collective-permute-start | bytes 737288 | tf_op jit(solution)/shard_map/ppermute | solution.py:38
  42.6 0.9 collective-permute-start.11
  43.9 1.8 collective-permute-done.17.a_ref
  45.7 2.7 %collective-permute-start.12 = (bf16[400,256]{1,0:T(8,128)(2,1)S(1)}, bf16[400,256]{1,0:T(8,128)(2,1)S(1)}, u32[]{:S(2)}, u32[]{:S(2)}) collective-permute-start(bf16[400,256]{1,0:T(8,128)(2,1)S(1)} %shard_map.119), channel_id=1, source_target_pairs={{0,192},{32,224},{64,0},{96,32},{128,64},{160,96},{192,128},{224,1... | collective-permute-start | bytes 614408 | tf_op jit(solution)/shard_map/ppermute | solution.py:38
  48.5 2.6 %collective-permute-done.18.b_ref = bf16[480,256]{1,0:T(8,128)(2,1)S(1)} collective-permute-done((bf16[480,256]{1,0:T(8,128)(2,1)S(1)}, bf16[480,256]{1,0:T(8,128)(2,1)S(1)}, u32[]{:S(2)}, u32[]{:S(2)}) %collective-permute-start.18) | collective-permute-done | bytes 245792 | tf_op jit(solution)/shard_map/ppermute | solution.py:38
  51.5 4.6 %collective-permute-start.20 = (bf16[480,256]{1,0:T(8,128)(2,1)S(1)}, bf16[480,256]{1,0:T(8,128)(2,1)S(1)}, u32[]{:S(2)}, u32[]{:S(2)}) collective-permute-start(bf16[480,256]{1,0:T(8,128)(2,1)S(1)} %get-tuple-element.73), channel_id=1, source_target_pairs={{0,32},{32,0},{64,96},{96,64},{128,160},{160,128},{192,224},{224,1... | collective-permute-start | bytes 737288 | tf_op jit(solution)/shard_map/ppermute | solution.py:38
  56.1 0.7 shard_map.115
  56.8 2.9 %collective-permute-start.6 = (bf16[480,256]{1,0:T(8,128)(2,1)S(1)}, bf16[480,256]{1,0:T(8,128)(2,1)S(1)}, u32[]{:S(2)}, u32[]{:S(2)}) collective-permute-start(bf16[480,256]{1,0:T(8,128)(2,1)S(1)} %get-tuple-element.57), channel_id=1, source_target_pairs={{0,128},{32,160},{64,192},{96,224},{128,0},{160,32},{192,64},{224,... | collective-permute-start | bytes 737288 | tf_op jit(solution)/shard_map/ppermute | solution.py:38
  59.7 0.8 collective-permute-start.7
  60.5 2.4 %collective-permute-start.8 = (bf16[480,256]{1,0:T(8,128)(2,1)S(1)}, bf16[480,256]{1,0:T(8,128)(2,1)S(1)}, u32[]{:S(2)}, u32[]{:S(2)}) collective-permute-start(bf16[480,256]{1,0:T(8,128)(2,1)S(1)} %get-tuple-element.59), channel_id=1, source_target_pairs={{0,192},{32,224},{64,0},{96,32},{128,64},{160,96},{192,128},{224,1... | collective-permute-start | bytes 737288 | tf_op jit(solution)/shard_map/ppermute | solution.py:38
  63.5 2.1 %collective-permute-start.13 = (bf16[400,256]{1,0:T(8,128)(2,1)S(1)}, bf16[400,256]{1,0:T(8,128)(2,1)S(1)}, u32[]{:S(2)}, u32[]{:S(2)}) collective-permute-start(bf16[400,256]{1,0:T(8,128)(2,1)S(1)} %get-tuple-element.65), channel_id=1, source_target_pairs={{0,32},{32,0},{64,96},{96,64},{128,160},{160,128},{192,224},{224,1... | collective-permute-start | bytes 614408 | tf_op jit(solution)/shard_map/ppermute | solution.py:38
  65.5 13.0 %collective-permute-done.13.other_ref = bf16[400,256]{1,0:T(8,128)(2,1)S(1)} collective-permute-done((bf16[400,256]{1,0:T(8,128)(2,1)S(1)}, bf16[400,256]{1,0:T(8,128)(2,1)S(1)}, u32[]{:S(2)}, u32[]{:S(2)}) %collective-permute-start.13) | collective-permute-done | bytes 204832 | tf_op jit(solution)/shard_map/ppermute | solution.py:38
  78.9 0.8 collective-permute-start.21
  80.1 4.0 %collective-permute-start.9 = (bf16[480,256]{1,0:T(8,128)(2,1)S(1)}, bf16[480,256]{1,0:T(8,128)(2,1)S(1)}, u32[]{:S(2)}, u32[]{:S(2)}) collective-permute-start(bf16[480,256]{1,0:T(8,128)(2,1)S(1)} %get-tuple-element.61), channel_id=1, source_target_pairs={{0,32},{32,0},{64,96},{96,64},{128,160},{160,128},{192,224},{224,1... | collective-permute-start | bytes 737288 | tf_op jit(solution)/shard_map/ppermute | solution.py:38
  84.2 2.8 %collective-permute-start.24 = (bf16[416,256]{1,0:T(8,128)(2,1)S(1)}, bf16[416,256]{1,0:T(8,128)(2,1)S(1)}, u32[]{:S(2)}, u32[]{:S(2)}) collective-permute-start(bf16[416,256]{1,0:T(8,128)(2,1)S(1)} %get-tuple-element.74.a_ref.refs_0_), channel_id=1, source_target_pairs={{0,128},{32,160},{64,192},{96,224},{128,0},{160,32},{192,64},{224,... | collective-permute-start | bytes 638984 | tf_op jit(solution)/shard_map/ppermute | solution.py:38
  87.0 1.5 collective-permute-start.25
  88.5 1.8 collective-permute-start.26
  90.2 4.0 %collective-permute-done.9.other_ref = bf16[480,256]{1,0:T(8,128)(2,1)S(1)} collective-permute-done((bf16[480,256]{1,0:T(8,128)(2,1)S(1)}, bf16[480,256]{1,0:T(8,128)(2,1)S(1)}, u32[]{:S(2)}, u32[]{:S(2)}) %collective-permute-start.9) | collective-permute-done | bytes 245792 | tf_op jit(solution)/shard_map/ppermute | solution.py:38
  94.2 3.3 %collective-permute-start.22 = (bf16[496,256]{1,0:T(8,128)(2,1)S(1)}, bf16[496,256]{1,0:T(8,128)(2,1)S(1)}, u32[]{:S(2)}, u32[]{:S(2)}) collective-permute-start(bf16[496,256]{1,0:T(8,128)(2,1)S(1)} %shard_map.125.a_ref.refs_4_), channel_id=1, source_target_pairs={{0,64},{32,96},{64,128},{96,160},{128,192},{160,224},{192,0},{224,... | collective-permute-start | bytes 761864 | tf_op jit(solution)/shard_map/ppermute | solution.py:38
  97.6 0.7 collective-permute-start.23
  98.3 1.6 collective-permute-start.14
  99.8 1.3 collective-permute-start.15
  101.2 1.9 collective-permute-start.16
  103.1 0.7 shard_map.126
  103.8 1.6 collective-permute-done.22.c_ref.refs_6_
  105.4 1.3 collective-permute-done.23.d_ref.refs_7_
  106.7 1.0 shard_map.127
  107.7 4.2 %collective-permute-done.14.b_ref.refs_1_ = bf16[496,256]{1,0:T(8,128)(2,1)S(1)} collective-permute-done((bf16[496,256]{1,0:T(8,128)(2,1)S(1)}, bf16[496,256]{1,0:T(8,128)(2,1)S(1)}, u32[]{:S(2)}, u32[]{:S(2)}) %collective-permute-start.14) | collective-permute-done | bytes 253984 | tf_op jit(solution)/shard_map/ppermute | solution.py:38
  111.9 3.3 %collective-permute-done.15.c_ref.refs_2_ = bf16[496,256]{1,0:T(8,128)(2,1)S(1)} collective-permute-done((bf16[496,256]{1,0:T(8,128)(2,1)S(1)}, bf16[496,256]{1,0:T(8,128)(2,1)S(1)}, u32[]{:S(2)}, u32[]{:S(2)}) %collective-permute-start.15) | collective-permute-done | bytes 253984 | tf_op jit(solution)/shard_map/ppermute | solution.py:38
  115.2 1.2 collective-permute-done.16.d_ref.refs_3_
  116.4 1.3 shard_map.128
  118.0 1.1 shard_map.133.refs_0_
  119.7 1.1 collective-permute-done.27.refs_0_
  121.2 3.4 %collective-permute-start.30 = (bf16[144,1024]{1,0:T(8,128)(2,1)S(1)}, bf16[144,1024]{1,0:T(8,128)(2,1)S(1)}, u32[]{:S(2)}, u32[]{:S(2)}) collective-permute-start(bf16[144,1024]{1,0:T(8,128)(2,1)S(1)} %get-tuple-element.88), channel_id=1, source_target_pairs={{0,24},{4,28},{8,16},{12,20},{16,8},{20,12},{24,0},{28,4},{1,25},{... | collective-permute-start | bytes 884744 | tf_op jit(solution)/shard_map/ppermute | solution.py:38
  124.5 6.4 %collective-permute-done.28.refs_0_ = bf16[144,1024]{1,0:T(8,128)(2,1)S(1)} collective-permute-done((bf16[144,1024]{1,0:T(8,128)(2,1)S(1)}, bf16[144,1024]{1,0:T(8,128)(2,1)S(1)}, u32[]{:S(2)}, u32[]{:S(2)}) %collective-permute-start.28) | collective-permute-done | bytes 294944 | tf_op jit(solution)/shard_map/ppermute | solution.py:38
  130.9 3.6 %collective-permute-done.29.refs_1_ = bf16[144,1024]{1,0:T(8,128)(2,1)S(1)} collective-permute-done((bf16[144,1024]{1,0:T(8,128)(2,1)S(1)}, bf16[144,1024]{1,0:T(8,128)(2,1)S(1)}, u32[]{:S(2)}, u32[]{:S(2)}) %collective-permute-start.29) | collective-permute-done | bytes 294944 | tf_op jit(solution)/shard_map/ppermute | solution.py:38
  134.5 15.8 %collective-permute-done.30.refs_2_ = bf16[144,1024]{1,0:T(8,128)(2,1)S(1)} collective-permute-done((bf16[144,1024]{1,0:T(8,128)(2,1)S(1)}, bf16[144,1024]{1,0:T(8,128)(2,1)S(1)}, u32[]{:S(2)}, u32[]{:S(2)}) %collective-permute-start.30) | collective-permute-done | bytes 294944 | tf_op jit(solution)/shard_map/ppermute | solution.py:38
  150.5 2.5 %collective-permute-start.31 = (bf16[80,1024]{1,0:T(8,128)(2,1)S(1)}, bf16[80,1024]{1,0:T(8,128)(2,1)S(1)}, u32[]{:S(2)}, u32[]{:S(2)}) collective-permute-start(bf16[80,1024]{1,0:T(8,128)(2,1)S(1)} %get-tuple-element.92), channel_id=1, source_target_pairs={{0,2},{1,3},{2,0},{3,1},{4,6},{5,7},{6,4},{7,5},{8,10},{9,11},{10,... | collective-permute-start | bytes 491528 | tf_op jit(solution)/shard_map/ppermute | solution.py:38
  153.0 0.7 shard_map.134.refs_5_
  154.2 1.3 collective-permute-start.38
  155.4 2.4 %collective-permute-start.39 = (bf16[480,512]{1,0:T(8,128)(2,1)S(1)}, bf16[480,512]{1,0:T(8,128)(2,1)S(1)}, u32[]{:S(2)}, u32[]{:S(2)}) collective-permute-start(bf16[480,512]{1,0:T(8,128)(2,1)S(1)} %shard_map.134.refs_5_), channel_id=1, source_target_pairs={{0,2},{1,3},{2,0},{3,1},{4,6},{5,7},{6,4},{7,5},{8,10},{9,11},{10,... | collective-permute-start | bytes 1474568 | tf_op jit(solution)/shard_map/ppermute | solution.py:38
  157.9 1.0 collective-permute-start.35
  159.1 0.6 collective-permute-start.36
  159.8 9.0 %collective-permute-done.37.refs_6_ = bf16[480,512]{1,0:T(8,128)(2,1)S(1)} collective-permute-done((bf16[480,512]{1,0:T(8,128)(2,1)S(1)}, bf16[480,512]{1,0:T(8,128)(2,1)S(1)}, u32[]{:S(2)}, u32[]{:S(2)}) %collective-permute-start.37) | collective-permute-done | bytes 491552 | tf_op jit(solution)/shard_map/ppermute | solution.py:38
  168.9 1.7 collective-permute-start.32
  170.6 9.4 %collective-permute-done.38.refs_7_ = bf16[480,512]{1,0:T(8,128)(2,1)S(1)} collective-permute-done((bf16[480,512]{1,0:T(8,128)(2,1)S(1)}, bf16[480,512]{1,0:T(8,128)(2,1)S(1)}, u32[]{:S(2)}, u32[]{:S(2)}) %collective-permute-start.38) | collective-permute-done | bytes 491552 | tf_op jit(solution)/shard_map/ppermute | solution.py:38
  180.2 8.1 %collective-permute-done.35.refs_3_ = bf16[432,512]{1,0:T(8,128)(2,1)S(1)} collective-permute-done((bf16[432,512]{1,0:T(8,128)(2,1)S(1)}, bf16[432,512]{1,0:T(8,128)(2,1)S(1)}, u32[]{:S(2)}, u32[]{:S(2)}) %collective-permute-start.35) | collective-permute-done | bytes 442400 | tf_op jit(solution)/shard_map/ppermute | solution.py:38
  188.4 4.5 %shard_map.135 = (bf16[512,1792]{1,0:T(8,128)(2,1)}, bf16[512,1792]{1,0:T(8,128)(2,1)}, bf16[1792,512]{1,0:T(8,128)(2,1)}) custom-call(s32[1]{0:T(128)} %bitcast.2.at_ref, bf16[864,512]{1,0:T(8,128)(2,1)S(1)} %shard_map.133.refs_0_, bf16[864,512]{1,0:T(8,128)(2,1)S(1)} %collective-permute-done.33.refs_1_, ...), custom_call_target="tpu_custom_call" | custom-call | tf_op jit(solution)/shard_map/pallas_call | solution.py:98
  192.8 0.9 shard_map.132
  (51 shorter events, 6.2 us)
Async XLA Ops:
  1.4 4.3 %collective-permute-start = (bf16[32,1024]{1,0:T(8,128)(2,1)S(1)}, bf16[32,1024]{1,0:T(8,128)(2,1)S(1)}, u32[]{:S(2)}, u32[]{:S(2)}) collective-permute-start(bf16[32,1024]{1,0:T(8,128)(2,1)S(1)} %shard_map.109.refs_0_), channel_id=1, source_target_pairs={{0,8},{4,12},{8,0},{12,4},{16,24},{20,28},{24,16},{28,20},{1,9},{5... | collective-permute-start | bytes 196616 | tf_op jit(solution)/shard_map/ppermute | solution.py:38
  5.7 7.5 %collective-permute-start.1 = (bf16[64,1024]{1,0:T(8,128)(2,1)S(1)}, bf16[64,1024]{1,0:T(8,128)(2,1)S(1)}, u32[]{:S(2)}, u32[]{:S(2)}) collective-permute-start(bf16[64,1024]{1,0:T(8,128)(2,1)S(1)} %shard_map.110.refs_0_), channel_id=1, source_target_pairs={{0,16},{4,20},{8,24},{12,28},{16,0},{20,4},{24,8},{28,12},{1,17},{... | collective-permute-start | bytes 393224 | tf_op jit(solution)/shard_map/ppermute | solution.py:38
  13.2 9.3 %collective-permute-start.2 = (bf16[128,1024]{1,0:T(8,128)(2,1)S(1)}, bf16[128,1024]{1,0:T(8,128)(2,1)S(1)}, u32[]{:S(2)}, u32[]{:S(2)}) collective-permute-start(bf16[128,1024]{1,0:T(8,128)(2,1)S(1)} %shard_map.111.refs_0_), channel_id=1, source_target_pairs={{0,1},{1,0},{2,3},{3,2},{4,5},{5,4},{6,7},{7,6},{8,9},{9,8},{10,11... | collective-permute-start | bytes 786440 | tf_op jit(solution)/shard_map/ppermute | solution.py:38
  14.9 14.1 %collective-permute-start.3 = (bf16[128,1024]{1,0:T(8,128)(2,1)S(1)}, bf16[128,1024]{1,0:T(8,128)(2,1)S(1)}, u32[]{:S(2)}, u32[]{:S(2)}) collective-permute-start(bf16[128,1024]{1,0:T(8,128)(2,1)S(1)} %shard_map.111.refs_0_), channel_id=1, source_target_pairs={{0,2},{1,3},{2,0},{3,1},{4,6},{5,7},{6,4},{7,5},{8,10},{9,11},{10,... | collective-permute-start | bytes 786440 | tf_op jit(solution)/shard_map/ppermute | solution.py:38
  17.8 13.8 %collective-permute-start.4 = (bf16[128,1024]{1,0:T(8,128)(2,1)S(1)}, bf16[128,1024]{1,0:T(8,128)(2,1)S(1)}, u32[]{:S(2)}, u32[]{:S(2)}) collective-permute-start(bf16[128,1024]{1,0:T(8,128)(2,1)S(1)} %shard_map.111.refs_0_), channel_id=1, source_target_pairs={{0,3},{1,2},{2,1},{3,0},{4,7},{5,6},{6,5},{7,4},{8,11},{9,10},{10,... | collective-permute-start | bytes 786440 | tf_op jit(solution)/shard_map/ppermute | solution.py:38
  31.6 2.7 %collective-permute-start.5 = (bf16[512,1024]{1,0:T(8,128)(2,1)S(1)}, bf16[512,1024]{1,0:T(8,128)(2,1)S(1)}, u32[]{:S(2)}, u32[]{:S(2)}) collective-permute-start(bf16[512,1024]{1,0:T(8,128)(2,1)S(1)} %shard_map.112.refs_0_), channel_id=1, source_target_pairs={{0,4},{4,0},{8,12},{12,8},{16,20},{20,16},{24,28},{28,24},{1,5},{5... | collective-permute-start | bytes 3145736 | tf_op jit(solution)/shard_map/ppermute | solution.py:38
  33.3 1.2 copy-start
  35.3 10.5 %collective-permute-start.17 = (bf16[480,256]{1,0:T(8,128)(2,1)S(1)}, bf16[480,256]{1,0:T(8,128)(2,1)S(1)}, u32[]{:S(2)}, u32[]{:S(2)}) collective-permute-start(bf16[480,256]{1,0:T(8,128)(2,1)S(1)} %get-tuple-element.69), channel_id=1, source_target_pairs={{0,128},{32,160},{64,192},{96,224},{128,0},{160,32},{192,64},{224,... | collective-permute-start | bytes 737288 | tf_op jit(solution)/shard_map/ppermute | solution.py:38
  38.4 12.7 %collective-permute-start.18 = (bf16[480,256]{1,0:T(8,128)(2,1)S(1)}, bf16[480,256]{1,0:T(8,128)(2,1)S(1)}, u32[]{:S(2)}, u32[]{:S(2)}) collective-permute-start(bf16[480,256]{1,0:T(8,128)(2,1)S(1)} %get-tuple-element.70), channel_id=1, source_target_pairs={{0,64},{32,96},{64,128},{96,160},{128,192},{160,224},{192,0},{224,... | collective-permute-start | bytes 737288 | tf_op jit(solution)/shard_map/ppermute | solution.py:38
  39.0 12.1 %collective-permute-start.19 = (bf16[480,256]{1,0:T(8,128)(2,1)S(1)}, bf16[480,256]{1,0:T(8,128)(2,1)S(1)}, u32[]{:S(2)}, u32[]{:S(2)}) collective-permute-start(bf16[480,256]{1,0:T(8,128)(2,1)S(1)} %get-tuple-element.71), channel_id=1, source_target_pairs={{0,192},{32,224},{64,0},{96,32},{128,64},{160,96},{192,128},{224,1... | collective-permute-start | bytes 737288 | tf_op jit(solution)/shard_map/ppermute | solution.py:38
  42.0 17.6 %collective-permute-start.10 = (bf16[400,256]{1,0:T(8,128)(2,1)S(1)}, bf16[400,256]{1,0:T(8,128)(2,1)S(1)}, u32[]{:S(2)}, u32[]{:S(2)}) collective-permute-start(bf16[400,256]{1,0:T(8,128)(2,1)S(1)} %shard_map.117), channel_id=1, source_target_pairs={{0,128},{32,160},{64,192},{96,224},{128,0},{160,32},{192,64},{224,... | collective-permute-start | bytes 614408 | tf_op jit(solution)/shard_map/ppermute | solution.py:38
  42.6 17.9 %collective-permute-start.11 = (bf16[400,256]{1,0:T(8,128)(2,1)S(1)}, bf16[400,256]{1,0:T(8,128)(2,1)S(1)}, u32[]{:S(2)}, u32[]{:S(2)}) collective-permute-start(bf16[400,256]{1,0:T(8,128)(2,1)S(1)} %shard_map.118), channel_id=1, source_target_pairs={{0,64},{32,96},{64,128},{96,160},{128,192},{160,224},{192,0},{224,... | collective-permute-start | bytes 614408 | tf_op jit(solution)/shard_map/ppermute | solution.py:38
  45.7 17.2 %collective-permute-start.12 = (bf16[400,256]{1,0:T(8,128)(2,1)S(1)}, bf16[400,256]{1,0:T(8,128)(2,1)S(1)}, u32[]{:S(2)}, u32[]{:S(2)}) collective-permute-start(bf16[400,256]{1,0:T(8,128)(2,1)S(1)} %shard_map.119), channel_id=1, source_target_pairs={{0,192},{32,224},{64,0},{96,32},{128,64},{160,96},{192,128},{224,1... | collective-permute-start | bytes 614408 | tf_op jit(solution)/shard_map/ppermute | solution.py:38
  51.5 27.3 %collective-permute-start.20 = (bf16[480,256]{1,0:T(8,128)(2,1)S(1)}, bf16[480,256]{1,0:T(8,128)(2,1)S(1)}, u32[]{:S(2)}, u32[]{:S(2)}) collective-permute-start(bf16[480,256]{1,0:T(8,128)(2,1)S(1)} %get-tuple-element.73), channel_id=1, source_target_pairs={{0,32},{32,0},{64,96},{96,64},{128,160},{160,128},{192,224},{224,1... | collective-permute-start | bytes 737288 | tf_op jit(solution)/shard_map/ppermute | solution.py:38
  56.8 22.9 %collective-permute-start.6 = (bf16[480,256]{1,0:T(8,128)(2,1)S(1)}, bf16[480,256]{1,0:T(8,128)(2,1)S(1)}, u32[]{:S(2)}, u32[]{:S(2)}) collective-permute-start(bf16[480,256]{1,0:T(8,128)(2,1)S(1)} %get-tuple-element.57), channel_id=1, source_target_pairs={{0,128},{32,160},{64,192},{96,224},{128,0},{160,32},{192,64},{224,... | collective-permute-start | bytes 737288 | tf_op jit(solution)/shard_map/ppermute | solution.py:38
  59.7 20.1 %collective-permute-start.7 = (bf16[480,256]{1,0:T(8,128)(2,1)S(1)}, bf16[480,256]{1,0:T(8,128)(2,1)S(1)}, u32[]{:S(2)}, u32[]{:S(2)}) collective-permute-start(bf16[480,256]{1,0:T(8,128)(2,1)S(1)} %get-tuple-element.58), channel_id=1, source_target_pairs={{0,64},{32,96},{64,128},{96,160},{128,192},{160,224},{192,0},{224,... | collective-permute-start | bytes 737288 | tf_op jit(solution)/shard_map/ppermute | solution.py:38
  60.5 19.2 %collective-permute-start.8 = (bf16[480,256]{1,0:T(8,128)(2,1)S(1)}, bf16[480,256]{1,0:T(8,128)(2,1)S(1)}, u32[]{:S(2)}, u32[]{:S(2)}) collective-permute-start(bf16[480,256]{1,0:T(8,128)(2,1)S(1)} %get-tuple-element.59), channel_id=1, source_target_pairs={{0,192},{32,224},{64,0},{96,32},{128,64},{160,96},{192,128},{224,1... | collective-permute-start | bytes 737288 | tf_op jit(solution)/shard_map/ppermute | solution.py:38
  63.5 15.1 %collective-permute-start.13 = (bf16[400,256]{1,0:T(8,128)(2,1)S(1)}, bf16[400,256]{1,0:T(8,128)(2,1)S(1)}, u32[]{:S(2)}, u32[]{:S(2)}) collective-permute-start(bf16[400,256]{1,0:T(8,128)(2,1)S(1)} %get-tuple-element.65), channel_id=1, source_target_pairs={{0,32},{32,0},{64,96},{96,64},{128,160},{160,128},{192,224},{224,1... | collective-permute-start | bytes 614408 | tf_op jit(solution)/shard_map/ppermute | solution.py:38
  78.9 22.3 %collective-permute-start.21 = (bf16[496,256]{1,0:T(8,128)(2,1)S(1)}, bf16[496,256]{1,0:T(8,128)(2,1)S(1)}, u32[]{:S(2)}, u32[]{:S(2)}) collective-permute-start(bf16[496,256]{1,0:T(8,128)(2,1)S(1)} %shard_map.125.a_ref.refs_4_), channel_id=1, source_target_pairs={{0,128},{32,160},{64,192},{96,224},{128,0},{160,32},{192,64},{224,... | collective-permute-start | bytes 761864 | tf_op jit(solution)/shard_map/ppermute | solution.py:38
  80.1 14.0 %collective-permute-start.9 = (bf16[480,256]{1,0:T(8,128)(2,1)S(1)}, bf16[480,256]{1,0:T(8,128)(2,1)S(1)}, u32[]{:S(2)}, u32[]{:S(2)}) collective-permute-start(bf16[480,256]{1,0:T(8,128)(2,1)S(1)} %get-tuple-element.61), channel_id=1, source_target_pairs={{0,32},{32,0},{64,96},{96,64},{128,160},{160,128},{192,224},{224,1... | collective-permute-start | bytes 737288 | tf_op jit(solution)/shard_map/ppermute | solution.py:38
  84.2 13.5 %collective-permute-start.24 = (bf16[416,256]{1,0:T(8,128)(2,1)S(1)}, bf16[416,256]{1,0:T(8,128)(2,1)S(1)}, u32[]{:S(2)}, u32[]{:S(2)}) collective-permute-start(bf16[416,256]{1,0:T(8,128)(2,1)S(1)} %get-tuple-element.74.a_ref.refs_0_), channel_id=1, source_target_pairs={{0,128},{32,160},{64,192},{96,224},{128,0},{160,32},{192,64},{224,... | collective-permute-start | bytes 638984 | tf_op jit(solution)/shard_map/ppermute | solution.py:38
  87.0 11.3 %collective-permute-start.25 = (bf16[416,256]{1,0:T(8,128)(2,1)S(1)}, bf16[416,256]{1,0:T(8,128)(2,1)S(1)}, u32[]{:S(2)}, u32[]{:S(2)}) collective-permute-start(bf16[416,256]{1,0:T(8,128)(2,1)S(1)} %get-tuple-element.74.a_ref.refs_0_), channel_id=1, source_target_pairs={{0,64},{32,96},{64,128},{96,160},{128,192},{160,224},{192,0},{224,... | collective-permute-start | bytes 638984 | tf_op jit(solution)/shard_map/ppermute | solution.py:38
  88.5 11.4 %collective-permute-start.26 = (bf16[416,256]{1,0:T(8,128)(2,1)S(1)}, bf16[416,256]{1,0:T(8,128)(2,1)S(1)}, u32[]{:S(2)}, u32[]{:S(2)}) collective-permute-start(bf16[416,256]{1,0:T(8,128)(2,1)S(1)} %get-tuple-element.74.a_ref.refs_0_), channel_id=1, source_target_pairs={{0,192},{32,224},{64,0},{96,32},{128,64},{160,96},{192,128},{224,1... | collective-permute-start | bytes 638984 | tf_op jit(solution)/shard_map/ppermute | solution.py:38
  94.2 11.2 %collective-permute-start.22 = (bf16[496,256]{1,0:T(8,128)(2,1)S(1)}, bf16[496,256]{1,0:T(8,128)(2,1)S(1)}, u32[]{:S(2)}, u32[]{:S(2)}) collective-permute-start(bf16[496,256]{1,0:T(8,128)(2,1)S(1)} %shard_map.125.a_ref.refs_4_), channel_id=1, source_target_pairs={{0,64},{32,96},{64,128},{96,160},{128,192},{160,224},{192,0},{224,... | collective-permute-start | bytes 761864 | tf_op jit(solution)/shard_map/ppermute | solution.py:38
  97.6 9.1 %collective-permute-start.23 = (bf16[496,256]{1,0:T(8,128)(2,1)S(1)}, bf16[496,256]{1,0:T(8,128)(2,1)S(1)}, u32[]{:S(2)}, u32[]{:S(2)}) collective-permute-start(bf16[496,256]{1,0:T(8,128)(2,1)S(1)} %shard_map.125.a_ref.refs_4_), channel_id=1, source_target_pairs={{0,192},{32,224},{64,0},{96,32},{128,64},{160,96},{192,128},{224,1... | collective-permute-start | bytes 761864 | tf_op jit(solution)/shard_map/ppermute | solution.py:38
  98.3 13.7 %collective-permute-start.14 = (bf16[496,256]{1,0:T(8,128)(2,1)S(1)}, bf16[496,256]{1,0:T(8,128)(2,1)S(1)}, u32[]{:S(2)}, u32[]{:S(2)}) collective-permute-start(bf16[496,256]{1,0:T(8,128)(2,1)S(1)} %shard_map.122.a_ref.refs_0_), channel_id=1, source_target_pairs={{0,128},{32,160},{64,192},{96,224},{128,0},{160,32},{192,64},{224,... | collective-permute-start | bytes 761864 | tf_op jit(solution)/shard_map/ppermute | solution.py:38
  99.8 15.4 %collective-permute-start.15 = (bf16[496,256]{1,0:T(8,128)(2,1)S(1)}, bf16[496,256]{1,0:T(8,128)(2,1)S(1)}, u32[]{:S(2)}, u32[]{:S(2)}) collective-permute-start(bf16[496,256]{1,0:T(8,128)(2,1)S(1)} %shard_map.122.a_ref.refs_0_), channel_id=1, source_target_pairs={{0,64},{32,96},{64,128},{96,160},{128,192},{160,224},{192,0},{224,... | collective-permute-start | bytes 761864 | tf_op jit(solution)/shard_map/ppermute | solution.py:38
  101.2 15.2 %collective-permute-start.16 = (bf16[496,256]{1,0:T(8,128)(2,1)S(1)}, bf16[496,256]{1,0:T(8,128)(2,1)S(1)}, u32[]{:S(2)}, u32[]{:S(2)}) collective-permute-start(bf16[496,256]{1,0:T(8,128)(2,1)S(1)} %shard_map.122.a_ref.refs_0_), channel_id=1, source_target_pairs={{0,192},{32,224},{64,0},{96,32},{128,64},{160,96},{192,128},{224,1... | collective-permute-start | bytes 761864 | tf_op jit(solution)/shard_map/ppermute | solution.py:38
  117.7 3.0 %collective-permute-start.27 = (bf16[528,1024]{1,0:T(8,128)(2,1)S(1)}, bf16[528,1024]{1,0:T(8,128)(2,1)S(1)}, u32[]{:S(2)}, u32[]{:S(2)}) collective-permute-start(bf16[528,1024]{1,0:T(8,128)(2,1)S(1)} %get-tuple-element.82), channel_id=1, source_target_pairs={{0,4},{4,0},{8,12},{12,8},{16,20},{20,16},{24,28},{28,24},{1,5},{5... | collective-permute-start | bytes 3244040 | tf_op jit(solution)/shard_map/ppermute | solution.py:38
  119.2 36.3 %collective-permute-start.33 = (bf16[864,512]{1,0:T(8,128)(2,1)S(1)}, bf16[864,512]{1,0:T(8,128)(2,1)S(1)}, u32[]{:S(2)}, u32[]{:S(2)}) collective-permute-start(bf16[864,512]{1,0:T(8,128)(2,1)S(1)} %shard_map.133.refs_0_), channel_id=1, source_target_pairs={{0,1},{1,0},{2,3},{3,2},{4,5},{5,4},{6,7},{7,6},{8,9},{9,8},{10,11... | collective-permute-start | bytes 2654216 | tf_op jit(solution)/shard_map/ppermute | solution.py:38
  119.3 38.6 %collective-permute-start.34 = (bf16[864,512]{1,0:T(8,128)(2,1)S(1)}, bf16[864,512]{1,0:T(8,128)(2,1)S(1)}, u32[]{:S(2)}, u32[]{:S(2)}) collective-permute-start(bf16[864,512]{1,0:T(8,128)(2,1)S(1)} %shard_map.133.refs_0_), channel_id=1, source_target_pairs={{0,3},{1,2},{2,1},{3,0},{4,7},{5,6},{6,5},{7,4},{8,11},{9,10},{10,... | collective-permute-start | bytes 2654216 | tf_op jit(solution)/shard_map/ppermute | solution.py:38
  121.0 10.0 %collective-permute-start.28 = (bf16[144,1024]{1,0:T(8,128)(2,1)S(1)}, bf16[144,1024]{1,0:T(8,128)(2,1)S(1)}, u32[]{:S(2)}, u32[]{:S(2)}) collective-permute-start(bf16[144,1024]{1,0:T(8,128)(2,1)S(1)} %get-tuple-element.86), channel_id=1, source_target_pairs={{0,8},{4,12},{8,0},{12,4},{16,24},{20,28},{24,16},{28,20},{1,9},{5... | collective-permute-start | bytes 884744 | tf_op jit(solution)/shard_map/ppermute | solution.py:38
  121.1 13.4 %collective-permute-start.29 = (bf16[144,1024]{1,0:T(8,128)(2,1)S(1)}, bf16[144,1024]{1,0:T(8,128)(2,1)S(1)}, u32[]{:S(2)}, u32[]{:S(2)}) collective-permute-start(bf16[144,1024]{1,0:T(8,128)(2,1)S(1)} %get-tuple-element.87), channel_id=1, source_target_pairs={{0,16},{4,20},{8,24},{12,28},{16,0},{20,4},{24,8},{28,12},{1,17},{... | collective-permute-start | bytes 884744 | tf_op jit(solution)/shard_map/ppermute | solution.py:38
  121.2 29.1 %collective-permute-start.30 = (bf16[144,1024]{1,0:T(8,128)(2,1)S(1)}, bf16[144,1024]{1,0:T(8,128)(2,1)S(1)}, u32[]{:S(2)}, u32[]{:S(2)}) collective-permute-start(bf16[144,1024]{1,0:T(8,128)(2,1)S(1)} %get-tuple-element.88), channel_id=1, source_target_pairs={{0,24},{4,28},{8,16},{12,20},{16,8},{20,12},{24,0},{28,4},{1,25},{... | collective-permute-start | bytes 884744 | tf_op jit(solution)/shard_map/ppermute | solution.py:38
  150.5 8.7 %collective-permute-start.31 = (bf16[80,1024]{1,0:T(8,128)(2,1)S(1)}, bf16[80,1024]{1,0:T(8,128)(2,1)S(1)}, u32[]{:S(2)}, u32[]{:S(2)}) collective-permute-start(bf16[80,1024]{1,0:T(8,128)(2,1)S(1)} %get-tuple-element.92), channel_id=1, source_target_pairs={{0,2},{1,3},{2,0},{3,1},{4,6},{5,7},{6,4},{7,5},{8,10},{9,11},{10,... | collective-permute-start | bytes 491528 | tf_op jit(solution)/shard_map/ppermute | solution.py:38
  153.7 15.2 %collective-permute-start.37 = (bf16[480,512]{1,0:T(8,128)(2,1)S(1)}, bf16[480,512]{1,0:T(8,128)(2,1)S(1)}, u32[]{:S(2)}, u32[]{:S(2)}) collective-permute-start(bf16[480,512]{1,0:T(8,128)(2,1)S(1)} %shard_map.134.refs_5_), channel_id=1, source_target_pairs={{0,1},{1,0},{2,3},{3,2},{4,5},{5,4},{6,7},{7,6},{8,9},{9,8},{10,11... | collective-permute-start | bytes 1474568 | tf_op jit(solution)/shard_map/ppermute | solution.py:38
  154.2 25.8 %collective-permute-start.38 = (bf16[480,512]{1,0:T(8,128)(2,1)S(1)}, bf16[480,512]{1,0:T(8,128)(2,1)S(1)}, u32[]{:S(2)}, u32[]{:S(2)}) collective-permute-start(bf16[480,512]{1,0:T(8,128)(2,1)S(1)} %shard_map.134.refs_5_), channel_id=1, source_target_pairs={{0,3},{1,2},{2,1},{3,0},{4,7},{5,6},{6,5},{7,4},{8,11},{9,10},{10,... | collective-permute-start | bytes 1474568 | tf_op jit(solution)/shard_map/ppermute | solution.py:38
  155.4 24.8 %collective-permute-start.39 = (bf16[480,512]{1,0:T(8,128)(2,1)S(1)}, bf16[480,512]{1,0:T(8,128)(2,1)S(1)}, u32[]{:S(2)}, u32[]{:S(2)}) collective-permute-start(bf16[480,512]{1,0:T(8,128)(2,1)S(1)} %shard_map.134.refs_5_), channel_id=1, source_target_pairs={{0,2},{1,3},{2,0},{3,1},{4,6},{5,7},{6,4},{7,5},{8,10},{9,11},{10,... | collective-permute-start | bytes 1474568 | tf_op jit(solution)/shard_map/ppermute | solution.py:38
  157.9 30.4 %collective-permute-start.35 = (bf16[432,512]{1,0:T(8,128)(2,1)S(1)}, bf16[432,512]{1,0:T(8,128)(2,1)S(1)}, u32[]{:S(2)}, u32[]{:S(2)}) collective-permute-start(bf16[432,512]{1,0:T(8,128)(2,1)S(1)} %slice.8), channel_id=1, source_target_pairs={{0,3},{1,2},{2,1},{3,0},{4,7},{5,6},{6,5},{7,4},{8,11},{9,10},{10,... | collective-permute-start | bytes 1327112 | tf_op jit(solution)/shard_map/ppermute | solution.py:38
  159.1 29.2 %collective-permute-start.36 = (bf16[432,512]{1,0:T(8,128)(2,1)S(1)}, bf16[432,512]{1,0:T(8,128)(2,1)S(1)}, u32[]{:S(2)}, u32[]{:S(2)}) collective-permute-start(bf16[432,512]{1,0:T(8,128)(2,1)S(1)} %slice.9), channel_id=1, source_target_pairs={{0,1},{1,0},{2,3},{3,2},{4,5},{5,4},{6,7},{7,6},{8,9},{9,8},{10,11... | collective-permute-start | bytes 1327112 | tf_op jit(solution)/shard_map/ppermute | solution.py:38
  168.9 24.0 %copy-start.1 = (bf16[32,512]{1,0:T(8,128)(2,1)S(1)}, bf16[32,512]{1,0:T(8,128)(2,1)}, u32[]{:S(2)}) copy-start(bf16[32,512]{1,0:T(8,128)(2,1)} %tok_ref.3) | copy-start | bytes 98308
  168.9 24.0 %copy-start.2 = (bf16[32,512]{1,0:T(8,128)(2,1)S(1)}, bf16[32,512]{1,0:T(8,128)(2,1)}, u32[]{:S(2)}) copy-start(bf16[32,512]{1,0:T(8,128)(2,1)} %cot_ref.3) | copy-start | bytes 98308
  168.9 24.0 %collective-permute-start.32 = (bf16[48,1024]{1,0:T(8,128)(2,1)S(1)}, bf16[48,1024]{1,0:T(8,128)(2,1)S(1)}, u32[]{:S(2)}, u32[]{:S(2)}) collective-permute-start(bf16[48,1024]{1,0:T(8,128)(2,1)S(1)} %get-tuple-element.97), channel_id=1, source_target_pairs={{0,1},{1,0},{2,3},{3,2},{4,5},{5,4},{6,7},{7,6},{8,9},{9,8},{10,11... | collective-permute-start | bytes 294920 | tf_op jit(solution)/shard_map/ppermute | solution.py:38

commit v4 on v3

--- a/solution.py
+++ b/solution.py
@@ -266,16 +266,16 @@
 
 
 def write_extra(ref, rows, gain_part, inner):
-    gain_hi, gain_lo = split(gain_part)
-    inner_hi, inner_lo = split(inner)
-    ref[rows:, :512] = jnp.concatenate([gain_hi, inner_hi], axis=0)
-    ref[rows:, 512:] = jnp.concatenate([gain_lo, inner_lo], axis=0)
+    upper = lax.broadcasted_iota(jnp.int32, (8, 512), 0) < 4
+    hi, lo = split(jnp.where(upper, gain_part, inner))
+    ref[rows:, :512] = hi
+    ref[rows:, 512:] = lo
 
 
 def read_extra(ref, rows):
     extra = ref[rows:, :].astype(F32)
     extra = extra[:, :512] + extra[:, 512:]
-    return extra[:8, :], extra[8:, :]
+    return jnp.broadcast_to(extra[:1, :], (8, 512)), jnp.broadcast_to(extra[4:5, :], (8, 512))
 
 
 def read_pair(ref, at):
@@ -325,7 +325,7 @@
     args = list(pieces) + [wgu, wd, both] + ([] if first else list(before))
     acc, inner = sds((1024, 1024), F32), sds((8, 1024), F32)
     if last:
-        outs = [sds((512, 1024), F32), sds((8, 512), F32), sds((8, 512), F32), sds((528, 1024), BF)]
+        outs = [sds((512, 1024), F32), sds((8, 512), F32), sds((8, 512), F32), sds((520, 1024), BF)]
         scratch = [pltpu.VMEM(acc.shape, F32), pltpu.VMEM(inner.shape, F32)]
         return call(kernel, outs, (x_at,), *args, scratch=scratch)
     if first:
@@ -370,7 +370,7 @@
             write_extra(ref, keep, gain_sum, inner_sum)
 
     outs = [sds((keep, 1024), F32), sds((8, 512), F32), sds((8, 512), F32)]
-    outs += [sds((keep + 16, 1024), BF)] * (len(strips) - 1)
+    outs += [sds((keep + 8, 1024), BF)] * (len(strips) - 1)
     return call(kernel, outs, (), own, gain_part, inner, *messages)
 
 
@@ -440,8 +440,7 @@
     count = len(CHUNKS)
 
     both = pack_call(tokens, cotangent)
-    both = join_call([both, send_zl(both, 1)])
-    both = join_call([both, send_zl(both, 2)])
+    both = join_call([both] + [send_zl(both, k) for k in (1, 2, 3)])
     near = [send_y(both, k) for k in (1, 2, 3)]
     weights = prepare_call(depth_at, w_gate, w_up, w_down)
     both = join_call([both] + near)
@@ -482,11 +481,6 @@
     def spread(group, ks):
         for k in ks:
             group[1].append((k, [send_y(group[1][0][1][0], k)]))
-
-    def relay(group):
-        near = {source: pieces[0] for source, pieces in group[1]}
-        half = near[0].shape[0] // 2
-        group[1].append((2, [send_y(near[1][:half], 3), send_y(near[3][half:], 1)]))
 
     def back(n, before):
         _, size, wgu, wd = chunks[n]
@@ -500,27 +494,28 @@
     inv = middle(0, None)
     row_sum(2)
     middle(1, inv)
+    groups = [weight_grad((0,))]
+    spread(groups[0], (2, 1, 3))
     *before, own_inv = back(0, None)
     middle(2, inv)
-    early = weight_grad((0, 1))
-    spread(early, (1, 3))
+    groups.append(weight_grad((1,)))
+    spread(groups[1], (2, 1, 3))
     before = back(1, before)
     own, gain_part, inner, message = back(2, before)
     message = send_core(message)
-    late = weight_grad((2,))
+    groups.append(weight_grad((2,)))
     strips = [[(128 * a + 32 * j, 32) for a in range(4)] for j in range(4)]
     own, gain_part, inner, *messages = fold_call(own, gain_part, inner, [message], [None], strips)
     messages = [send_zl(m, k) for k, m in zip((1, 2, 3), messages)]
-    relay(early)
-    spread(late, (1, 3, 2))
+    spread(groups[2], (2, 1, 3))
     turns = [lambda v, lanes=lanes: turn_left(v, lanes) for lanes in (32, 64, 96)]
     own, gain_part, inner, *messages = fold_call(
         own, gain_part, inner, messages, turns, [[(0, 64)], [(64, 64)]])
     message = send_y(messages[0], 2)
+    out_gate, out_up, out_down = assemble_call(depth_at, groups)
     own, gain_part, inner, *messages = fold_call(
         own, gain_part, inner, [message], [upper_half], [[(0, 32)], [(32, 32)]])
     message = send_y(messages[0], 1)
-    out_gate, out_up, out_down = assemble_call(depth_at, [early, late])
     output, grad_tokens, gain_grad = final_call(own, gain_part, inner, own_inv, message, tokens, cotangent, gain)
     return output, grad_tokens, gain_grad[0], out_gate, out_up, out_down
 

time: 194 us -> 196 us (1.010)
  the two profiles are of different devices: /device:TPU:32 before, /device:TPU:1 now
where the time goes in v4:
time: 196 us
  waiting for transfers between devices  114 us (58%)
  starting transfers between devices  63.7 us (32%)
  Pallas kernels  18 us (9%)
    ppermute x43, waiting for transfers between devices, send(): return lax.ppermute(v, axis, perm)  114 us
    ppermute x43, starting transfers between devices, send(): return lax.ppermute(v, axis, perm)  63.7 us
    pallas_call x27, Pallas kernels, call(): return run(*scalars, *placed)  18 us
  transfers between devices with their start and end apart: 43, of which 26 were waited for; matrix products, arithmetic and copies ran while one was open for 0% of the time, Pallas kernels for 7%

profile of v4, /device:TPU:1, one launch (start us, length us, event | category | flops | bytes accessed | tf_op | source)
XLA Modules:
  0.0 196.1 jit_solution(16351616285585622008)
XLA Ops:
  0.6 0.8 shard_map.109.refs_0_
  1.4 2.5 %collective-permute-start = (bf16[32,1024]{1,0:T(8,128)(2,1)S(1)}, bf16[32,1024]{1,0:T(8,128)(2,1)S(1)}, u32[]{:S(2)}, u32[]{:S(2)}) collective-permute-start(bf16[32,1024]{1,0:T(8,128)(2,1)S(1)} %shard_map.109.refs_0_), channel_id=1, source_target_pairs={{0,8},{4,12},{8,0},{12,4},{16,24},{20,28},{24,16},{28,20},{1,9},{5... | collective-permute-start | bytes 196616 | tf_op jit(solution)/shard_map/ppermute | solution.py:38
  3.9 3.0 %collective-permute-start.1 = (bf16[32,1024]{1,0:T(8,128)(2,1)S(1)}, bf16[32,1024]{1,0:T(8,128)(2,1)S(1)}, u32[]{:S(2)}, u32[]{:S(2)}) collective-permute-start(bf16[32,1024]{1,0:T(8,128)(2,1)S(1)} %shard_map.109.refs_0_), channel_id=1, source_target_pairs={{0,16},{4,20},{8,24},{12,28},{16,0},{20,4},{24,8},{28,12},{1,17},{... | collective-permute-start | bytes 196616 | tf_op jit(solution)/shard_map/ppermute | solution.py:38
  6.9 2.6 %collective-permute-done.1.refs_2_ = bf16[32,1024]{1,0:T(8,128)(2,1)S(1)} collective-permute-done((bf16[32,1024]{1,0:T(8,128)(2,1)S(1)}, bf16[32,1024]{1,0:T(8,128)(2,1)S(1)}, u32[]{:S(2)}, u32[]{:S(2)}) %collective-permute-start.1) | collective-permute-done | bytes 65568 | tf_op jit(solution)/shard_map/ppermute | solution.py:38
  9.5 2.3 %collective-permute-done.2.refs_3_ = bf16[32,1024]{1,0:T(8,128)(2,1)S(1)} collective-permute-done((bf16[32,1024]{1,0:T(8,128)(2,1)S(1)}, bf16[32,1024]{1,0:T(8,128)(2,1)S(1)}, u32[]{:S(2)}, u32[]{:S(2)}) %collective-permute-start.2) | collective-permute-done | bytes 65568 | tf_op jit(solution)/shard_map/ppermute | solution.py:38
  11.8 1.5 collective-permute-start.3
  13.3 2.6 %collective-permute-start.4 = (bf16[128,1024]{1,0:T(8,128)(2,1)S(1)}, bf16[128,1024]{1,0:T(8,128)(2,1)S(1)}, u32[]{:S(2)}, u32[]{:S(2)}) collective-permute-start(bf16[128,1024]{1,0:T(8,128)(2,1)S(1)} %shard_map.110.refs_0_), channel_id=1, source_target_pairs={{0,2},{1,3},{2,0},{3,1},{4,6},{5,7},{6,4},{7,5},{8,10},{9,11},{10,... | collective-permute-start | bytes 786440 | tf_op jit(solution)/shard_map/ppermute | solution.py:38
  15.9 1.2 collective-permute-done.3.refs_1_
  17.1 8.5 %collective-permute-done.4.refs_2_ = bf16[128,1024]{1,0:T(8,128)(2,1)S(1)} collective-permute-done((bf16[128,1024]{1,0:T(8,128)(2,1)S(1)}, bf16[128,1024]{1,0:T(8,128)(2,1)S(1)}, u32[]{:S(2)}, u32[]{:S(2)}) %collective-permute-start.4) | collective-permute-done | bytes 262176 | tf_op jit(solution)/shard_map/ppermute | solution.py:38
  25.6 3.7 %collective-permute-done.5.refs_3_ = bf16[128,1024]{1,0:T(8,128)(2,1)S(1)} collective-permute-done((bf16[128,1024]{1,0:T(8,128)(2,1)S(1)}, bf16[128,1024]{1,0:T(8,128)(2,1)S(1)}, u32[]{:S(2)}, u32[]{:S(2)}) %collective-permute-start.5) | collective-permute-done | bytes 262176 | tf_op jit(solution)/shard_map/ppermute | solution.py:38
  29.4 2.2 %collective-permute-start.6 = (bf16[512,1024]{1,0:T(8,128)(2,1)S(1)}, bf16[512,1024]{1,0:T(8,128)(2,1)S(1)}, u32[]{:S(2)}, u32[]{:S(2)}) collective-permute-start(bf16[512,1024]{1,0:T(8,128)(2,1)S(1)} %shard_map.111.refs_0_), channel_id=1, source_target_pairs={{0,4},{4,0},{8,12},{12,8},{16,20},{20,16},{24,28},{28,24},{1,5},{5... | collective-permute-start | bytes 3145736 | tf_op jit(solution)/shard_map/ppermute | solution.py:38
  31.6 1.6 shard_map.113
  33.2 0.7 collective-permute-done.6.refs_1_
  34.0 0.7 shard_map.122
  34.8 2.8 %collective-permute-start.18 = (bf16[480,256]{1,0:T(8,128)(2,1)S(1)}, bf16[480,256]{1,0:T(8,128)(2,1)S(1)}, u32[]{:S(2)}, u32[]{:S(2)}) collective-permute-start(bf16[480,256]{1,0:T(8,128)(2,1)S(1)} %get-tuple-element.69), channel_id=1, source_target_pairs={{0,128},{32,160},{64,192},{96,224},{128,0},{160,32},{192,64},{224,... | collective-permute-start | bytes 737288 | tf_op jit(solution)/shard_map/ppermute | solution.py:38
  37.9 2.4 %collective-permute-start.20 = (bf16[480,256]{1,0:T(8,128)(2,1)S(1)}, bf16[480,256]{1,0:T(8,128)(2,1)S(1)}, u32[]{:S(2)}, u32[]{:S(2)}) collective-permute-start(bf16[480,256]{1,0:T(8,128)(2,1)S(1)} %get-tuple-element.71), channel_id=1, source_target_pairs={{0,192},{32,224},{64,0},{96,32},{128,64},{160,96},{192,128},{224,1... | collective-permute-start | bytes 737288 | tf_op jit(solution)/shard_map/ppermute | solution.py:38
  42.3 1.2 collective-permute-done.18.a_ref
  43.5 2.5 %collective-permute-start.13 = (bf16[400,256]{1,0:T(8,128)(2,1)S(1)}, bf16[400,256]{1,0:T(8,128)(2,1)S(1)}, u32[]{:S(2)}, u32[]{:S(2)}) collective-permute-start(bf16[400,256]{1,0:T(8,128)(2,1)S(1)} %shard_map.118), channel_id=1, source_target_pairs={{0,192},{32,224},{64,0},{96,32},{128,64},{160,96},{192,128},{224,1... | collective-permute-start | bytes 614408 | tf_op jit(solution)/shard_map/ppermute | solution.py:38
  46.0 4.2 %collective-permute-done.19.b_ref = bf16[480,256]{1,0:T(8,128)(2,1)S(1)} collective-permute-done((bf16[480,256]{1,0:T(8,128)(2,1)S(1)}, bf16[480,256]{1,0:T(8,128)(2,1)S(1)}, u32[]{:S(2)}, u32[]{:S(2)}) %collective-permute-start.19) | collective-permute-done | bytes 245792 | tf_op jit(solution)/shard_map/ppermute | solution.py:38
  50.6 4.7 %collective-permute-start.21 = (bf16[480,256]{1,0:T(8,128)(2,1)S(1)}, bf16[480,256]{1,0:T(8,128)(2,1)S(1)}, u32[]{:S(2)}, u32[]{:S(2)}) collective-permute-start(bf16[480,256]{1,0:T(8,128)(2,1)S(1)} %get-tuple-element.73), channel_id=1, source_target_pairs={{0,32},{32,0},{64,96},{96,64},{128,160},{160,128},{192,224},{224,1... | collective-permute-start | bytes 737288 | tf_op jit(solution)/shard_map/ppermute | solution.py:38
  55.3 0.7 shard_map.114
  56.0 0.7 collective-permute-start.7
  56.8 2.6 %collective-permute-start.8 = (bf16[480,256]{1,0:T(8,128)(2,1)S(1)}, bf16[480,256]{1,0:T(8,128)(2,1)S(1)}, u32[]{:S(2)}, u32[]{:S(2)}) collective-permute-start(bf16[480,256]{1,0:T(8,128)(2,1)S(1)} %get-tuple-element.58), channel_id=1, source_target_pairs={{0,64},{32,96},{64,128},{96,160},{128,192},{160,224},{192,0},{224,... | collective-permute-start | bytes 737288 | tf_op jit(solution)/shard_map/ppermute | solution.py:38
  60.5 3.7 %collective-permute-start.14 = (bf16[400,256]{1,0:T(8,128)(2,1)S(1)}, bf16[400,256]{1,0:T(8,128)(2,1)S(1)}, u32[]{:S(2)}, u32[]{:S(2)}) collective-permute-start(bf16[400,256]{1,0:T(8,128)(2,1)S(1)} %get-tuple-element.65), channel_id=1, source_target_pairs={{0,32},{32,0},{64,96},{96,64},{128,160},{160,128},{192,224},{224,1... | collective-permute-start | bytes 614408 | tf_op jit(solution)/shard_map/ppermute | solution.py:38
  64.2 15.4 %collective-permute-done.14.other_ref = bf16[400,256]{1,0:T(8,128)(2,1)S(1)} collective-permute-done((bf16[400,256]{1,0:T(8,128)(2,1)S(1)}, bf16[400,256]{1,0:T(8,128)(2,1)S(1)}, u32[]{:S(2)}, u32[]{:S(2)}) %collective-permute-start.14) | collective-permute-done | bytes 204832 | tf_op jit(solution)/shard_map/ppermute | solution.py:38
  80.5 1.7 collective-permute-start.10
  82.2 2.9 %collective-permute-start.25 = (bf16[416,256]{1,0:T(8,128)(2,1)S(1)}, bf16[416,256]{1,0:T(8,128)(2,1)S(1)}, u32[]{:S(2)}, u32[]{:S(2)}) collective-permute-start(bf16[416,256]{1,0:T(8,128)(2,1)S(1)} %get-tuple-element.74.a_ref.refs_0_), channel_id=1, source_target_pairs={{0,128},{32,160},{64,192},{96,224},{128,0},{160,32},{192,64},{224,... | collective-permute-start | bytes 638984 | tf_op jit(solution)/shard_map/ppermute | solution.py:38
  85.1 1.2 collective-permute-start.26
  86.3 1.5 collective-permute-start.27
  87.8 6.8 %collective-permute-done.10.other_ref = bf16[480,256]{1,0:T(8,128)(2,1)S(1)} collective-permute-done((bf16[480,256]{1,0:T(8,128)(2,1)S(1)}, bf16[480,256]{1,0:T(8,128)(2,1)S(1)}, u32[]{:S(2)}, u32[]{:S(2)}) %collective-permute-start.10) | collective-permute-done | bytes 245792 | tf_op jit(solution)/shard_map/ppermute | solution.py:38
  94.6 2.6 %collective-permute-start.23 = (bf16[496,256]{1,0:T(8,128)(2,1)S(1)}, bf16[496,256]{1,0:T(8,128)(2,1)S(1)}, u32[]{:S(2)}, u32[]{:S(2)}) collective-permute-start(bf16[496,256]{1,0:T(8,128)(2,1)S(1)} %shard_map.124.a_ref.refs_0_), channel_id=1, source_target_pairs={{0,64},{32,96},{64,128},{96,160},{128,192},{160,224},{192,0},{224,... | collective-permute-start | bytes 761864 | tf_op jit(solution)/shard_map/ppermute | solution.py:38
  97.4 2.7 %collective-permute-start.24 = (bf16[496,256]{1,0:T(8,128)(2,1)S(1)}, bf16[496,256]{1,0:T(8,128)(2,1)S(1)}, u32[]{:S(2)}, u32[]{:S(2)}) collective-permute-start(bf16[496,256]{1,0:T(8,128)(2,1)S(1)} %shard_map.124.a_ref.refs_0_), channel_id=1, source_target_pairs={{0,192},{32,224},{64,0},{96,32},{128,64},{160,96},{192,128},{224,1... | collective-permute-start | bytes 761864 | tf_op jit(solution)/shard_map/ppermute | solution.py:38
  100.1 1.3 collective-permute-start.15
  101.4 0.8 collective-permute-start.16
  102.1 1.9 collective-permute-start.17
  104.1 0.7 shard_map.125
  104.8 1.0 collective-permute-done.23.c_ref.refs_2_
  105.8 1.4 collective-permute-done.24.d_ref.refs_3_
  107.3 1.0 shard_map.126
  108.3 3.9 %collective-permute-done.15.b_ref.refs_1_ = bf16[496,256]{1,0:T(8,128)(2,1)S(1)} collective-permute-done((bf16[496,256]{1,0:T(8,128)(2,1)S(1)}, bf16[496,256]{1,0:T(8,128)(2,1)S(1)}, u32[]{:S(2)}, u32[]{:S(2)}) %collective-permute-start.15) | collective-permute-done | bytes 253984 | tf_op jit(solution)/shard_map/ppermute | solution.py:38
  112.2 4.5 %collective-permute-done.16.c_ref.refs_2_ = bf16[496,256]{1,0:T(8,128)(2,1)S(1)} collective-permute-done((bf16[496,256]{1,0:T(8,128)(2,1)S(1)}, bf16[496,256]{1,0:T(8,128)(2,1)S(1)}, u32[]{:S(2)}, u32[]{:S(2)}) %collective-permute-start.16) | collective-permute-done | bytes 253984 | tf_op jit(solution)/shard_map/ppermute | solution.py:38
  116.7 1.3 shard_map.127
  118.0 1.2 collective-permute-start.28
  119.2 2.3 %collective-permute-done.28.refs_0_ = bf16[520,1024]{1,0:T(8,128)(2,1)S(1)} collective-permute-done((bf16[520,1024]{1,0:T(8,128)(2,1)S(1)}, bf16[520,1024]{1,0:T(8,128)(2,1)S(1)}, u32[]{:S(2)}, u32[]{:S(2)}) %collective-permute-start.28) | collective-permute-done | bytes 1064992 | tf_op jit(solution)/shard_map/ppermute | solution.py:38
  121.8 2.8 %collective-permute-start.30 = (bf16[136,1024]{1,0:T(8,128)(2,1)S(1)}, bf16[136,1024]{1,0:T(8,128)(2,1)S(1)}, u32[]{:S(2)}, u32[]{:S(2)}) collective-permute-start(bf16[136,1024]{1,0:T(8,128)(2,1)S(1)} %get-tuple-element.87), channel_id=1, source_target_pairs={{0,16},{4,20},{8,24},{12,28},{16,0},{20,4},{24,8},{28,12},{1,17},{... | collective-permute-start | bytes 835592 | tf_op jit(solution)/shard_map/ppermute | solution.py:38
  124.6 0.7 shard_map.133.refs_4_
  126.1 3.0 %collective-permute-start.34 = (bf16[384,512]{1,0:T(8,128)(2,1)S(1)}, bf16[384,512]{1,0:T(8,128)(2,1)S(1)}, u32[]{:S(2)}, u32[]{:S(2)}) collective-permute-start(bf16[384,512]{1,0:T(8,128)(2,1)S(1)} %shard_map.132.refs_0_), channel_id=1, source_target_pairs={{0,2},{1,3},{2,0},{3,1},{4,6},{5,7},{6,4},{7,5},{8,10},{9,11},{10,... | collective-permute-start | bytes 1179656 | tf_op jit(solution)/shard_map/ppermute | solution.py:38
  129.1 0.7 collective-permute-start.31
  129.8 5.4 %collective-permute-done.29.refs_0_ = bf16[136,1024]{1,0:T(8,128)(2,1)S(1)} collective-permute-done((bf16[136,1024]{1,0:T(8,128)(2,1)S(1)}, bf16[136,1024]{1,0:T(8,128)(2,1)S(1)}, u32[]{:S(2)}, u32[]{:S(2)}) %collective-permute-start.29) | collective-permute-done | bytes 278560 | tf_op jit(solution)/shard_map/ppermute | solution.py:38
  135.2 7.7 %collective-permute-done.31.refs_2_ = bf16[136,1024]{1,0:T(8,128)(2,1)S(1)} collective-permute-done((bf16[136,1024]{1,0:T(8,128)(2,1)S(1)}, bf16[136,1024]{1,0:T(8,128)(2,1)S(1)}, u32[]{:S(2)}, u32[]{:S(2)}) %collective-permute-start.31) | collective-permute-done | bytes 278560 | tf_op jit(solution)/shard_map/ppermute | solution.py:38
  143.3 4.0 %collective-permute-done.34.refs_1_ = bf16[384,512]{1,0:T(8,128)(2,1)S(1)} collective-permute-done((bf16[384,512]{1,0:T(8,128)(2,1)S(1)}, bf16[384,512]{1,0:T(8,128)(2,1)S(1)}, u32[]{:S(2)}, u32[]{:S(2)}) %collective-permute-start.34) | collective-permute-done | bytes 393248 | tf_op jit(solution)/shard_map/ppermute | solution.py:38
  148.0 5.3 %collective-permute-done.35.refs_2_ = bf16[384,512]{1,0:T(8,128)(2,1)S(1)} collective-permute-done((bf16[384,512]{1,0:T(8,128)(2,1)S(1)}, bf16[384,512]{1,0:T(8,128)(2,1)S(1)}, u32[]{:S(2)}, u32[]{:S(2)}) %collective-permute-start.35) | collective-permute-done | bytes 393248 | tf_op jit(solution)/shard_map/ppermute | solution.py:38
  153.3 2.7 %collective-permute-start.39 = (bf16[480,512]{1,0:T(8,128)(2,1)S(1)}, bf16[480,512]{1,0:T(8,128)(2,1)S(1)}, u32[]{:S(2)}, u32[]{:S(2)}) collective-permute-start(bf16[480,512]{1,0:T(8,128)(2,1)S(1)} %shard_map.133.refs_4_), channel_id=1, source_target_pairs={{0,3},{1,2},{2,1},{3,0},{4,7},{5,6},{6,5},{7,4},{8,11},{9,10},{10,... | collective-permute-start | bytes 1474568 | tf_op jit(solution)/shard_map/ppermute | solution.py:38
  156.4 1.5 collective-permute-start.40
  157.9 0.9 collective-permute-done.32.refs_0_
  158.9 0.8 collective-permute-start.42
  159.7 7.3 %collective-permute-done.38.refs_6_ = bf16[480,512]{1,0:T(8,128)(2,1)S(1)} collective-permute-done((bf16[480,512]{1,0:T(8,128)(2,1)S(1)}, bf16[480,512]{1,0:T(8,128)(2,1)S(1)}, u32[]{:S(2)}, u32[]{:S(2)}) %collective-permute-start.38) | collective-permute-done | bytes 491552 | tf_op jit(solution)/shard_map/ppermute | solution.py:38
  167.0 1.2 collective-permute-start.33
  168.2 1.8 collective-permute-done.39.refs_7_
  170.0 10.0 %collective-permute-done.40.refs_9_ = bf16[480,512]{1,0:T(8,128)(2,1)S(1)} collective-permute-done((bf16[480,512]{1,0:T(8,128)(2,1)S(1)}, bf16[480,512]{1,0:T(8,128)(2,1)S(1)}, u32[]{:S(2)}, u32[]{:S(2)}) %collective-permute-start.40) | collective-permute-done | bytes 491552 | tf_op jit(solution)/shard_map/ppermute | solution.py:38
  180.0 8.2 %collective-permute-done.41.refs_10_ = bf16[480,512]{1,0:T(8,128)(2,1)S(1)} collective-permute-done((bf16[480,512]{1,0:T(8,128)(2,1)S(1)}, bf16[480,512]{1,0:T(8,128)(2,1)S(1)}, u32[]{:S(2)}, u32[]{:S(2)}) %collective-permute-start.41) | collective-permute-done | bytes 491552 | tf_op jit(solution)/shard_map/ppermute | solution.py:38
  188.1 2.6 %collective-permute-done.42.refs_11_ = bf16[480,512]{1,0:T(8,128)(2,1)S(1)} collective-permute-done((bf16[480,512]{1,0:T(8,128)(2,1)S(1)}, bf16[480,512]{1,0:T(8,128)(2,1)S(1)}, u32[]{:S(2)}, u32[]{:S(2)}) %collective-permute-start.42) | collective-permute-done | bytes 491552 | tf_op jit(solution)/shard_map/ppermute | solution.py:38
  190.7 4.5 %shard_map.135 = (bf16[512,1792]{1,0:T(8,128)(2,1)}, bf16[512,1792]{1,0:T(8,128)(2,1)}, bf16[1792,512]{1,0:T(8,128)(2,1)}) custom-call(s32[1]{0:T(128)} %bitcast.2.at_ref, bf16[384,512]{1,0:T(8,128)(2,1)S(1)} %shard_map.132.refs_0_, bf16[384,512]{1,0:T(8,128)(2,1)S(1)} %collective-permute-done.34.refs_1_, ...), custom_call_target="tpu_custom_call" | custom-call | tf_op jit(solution)/shard_map/pallas_call | solution.py:98
  195.2 0.9 shard_map.131
  (55 shorter events, 7.6 us)
Async XLA Ops:
  1.4 5.5 %collective-permute-start = (bf16[32,1024]{1,0:T(8,128)(2,1)S(1)}, bf16[32,1024]{1,0:T(8,128)(2,1)S(1)}, u32[]{:S(2)}, u32[]{:S(2)}) collective-permute-start(bf16[32,1024]{1,0:T(8,128)(2,1)S(1)} %shard_map.109.refs_0_), channel_id=1, source_target_pairs={{0,8},{4,12},{8,0},{12,4},{16,24},{20,28},{24,16},{28,20},{1,9},{5... | collective-permute-start | bytes 196616 | tf_op jit(solution)/shard_map/ppermute | solution.py:38
  3.9 5.6 %collective-permute-start.1 = (bf16[32,1024]{1,0:T(8,128)(2,1)S(1)}, bf16[32,1024]{1,0:T(8,128)(2,1)S(1)}, u32[]{:S(2)}, u32[]{:S(2)}) collective-permute-start(bf16[32,1024]{1,0:T(8,128)(2,1)S(1)} %shard_map.109.refs_0_), channel_id=1, source_target_pairs={{0,16},{4,20},{8,24},{12,28},{16,0},{20,4},{24,8},{28,12},{1,17},{... | collective-permute-start | bytes 196616 | tf_op jit(solution)/shard_map/ppermute | solution.py:38
  6.9 4.9 %collective-permute-start.2 = (bf16[32,1024]{1,0:T(8,128)(2,1)S(1)}, bf16[32,1024]{1,0:T(8,128)(2,1)S(1)}, u32[]{:S(2)}, u32[]{:S(2)}) collective-permute-start(bf16[32,1024]{1,0:T(8,128)(2,1)S(1)} %shard_map.109.refs_0_), channel_id=1, source_target_pairs={{0,24},{4,28},{8,16},{12,20},{16,8},{20,12},{24,0},{28,4},{1,25},{... | collective-permute-start | bytes 196616 | tf_op jit(solution)/shard_map/ppermute | solution.py:38
  11.8 5.3 %collective-permute-start.3 = (bf16[128,1024]{1,0:T(8,128)(2,1)S(1)}, bf16[128,1024]{1,0:T(8,128)(2,1)S(1)}, u32[]{:S(2)}, u32[]{:S(2)}) collective-permute-start(bf16[128,1024]{1,0:T(8,128)(2,1)S(1)} %shard_map.110.refs_0_), channel_id=1, source_target_pairs={{0,1},{1,0},{2,3},{3,2},{4,5},{5,4},{6,7},{7,6},{8,9},{9,8},{10,11... | collective-permute-start | bytes 786440 | tf_op jit(solution)/shard_map/ppermute | solution.py:38
  13.3 12.3 %collective-permute-start.4 = (bf16[128,1024]{1,0:T(8,128)(2,1)S(1)}, bf16[128,1024]{1,0:T(8,128)(2,1)S(1)}, u32[]{:S(2)}, u32[]{:S(2)}) collective-permute-start(bf16[128,1024]{1,0:T(8,128)(2,1)S(1)} %shard_map.110.refs_0_), channel_id=1, source_target_pairs={{0,2},{1,3},{2,0},{3,1},{4,6},{5,7},{6,4},{7,5},{8,10},{9,11},{10,... | collective-permute-start | bytes 786440 | tf_op jit(solution)/shard_map/ppermute | solution.py:38
  15.9 13.4 %collective-permute-start.5 = (bf16[128,1024]{1,0:T(8,128)(2,1)S(1)}, bf16[128,1024]{1,0:T(8,128)(2,1)S(1)}, u32[]{:S(2)}, u32[]{:S(2)}) collective-permute-start(bf16[128,1024]{1,0:T(8,128)(2,1)S(1)} %shard_map.110.refs_0_), channel_id=1, source_target_pairs={{0,3},{1,2},{2,1},{3,0},{4,7},{5,6},{6,5},{7,4},{8,11},{9,10},{10,... | collective-permute-start | bytes 786440 | tf_op jit(solution)/shard_map/ppermute | solution.py:38
  29.4 4.5 %collective-permute-start.6 = (bf16[512,1024]{1,0:T(8,128)(2,1)S(1)}, bf16[512,1024]{1,0:T(8,128)(2,1)S(1)}, u32[]{:S(2)}, u32[]{:S(2)}) collective-permute-start(bf16[512,1024]{1,0:T(8,128)(2,1)S(1)} %shard_map.111.refs_0_), channel_id=1, source_target_pairs={{0,4},{4,0},{8,12},{12,8},{16,20},{20,16},{24,28},{28,24},{1,5},{5... | collective-permute-start | bytes 3145736 | tf_op jit(solution)/shard_map/ppermute | solution.py:38
  33.2 0.9 copy-start
  34.8 8.8 %collective-permute-start.18 = (bf16[480,256]{1,0:T(8,128)(2,1)S(1)}, bf16[480,256]{1,0:T(8,128)(2,1)S(1)}, u32[]{:S(2)}, u32[]{:S(2)}) collective-permute-start(bf16[480,256]{1,0:T(8,128)(2,1)S(1)} %get-tuple-element.69), channel_id=1, source_target_pairs={{0,128},{32,160},{64,192},{96,224},{128,0},{160,32},{192,64},{224,... | collective-permute-start | bytes 737288 | tf_op jit(solution)/shard_map/ppermute | solution.py:38
  37.6 12.6 %collective-permute-start.19 = (bf16[480,256]{1,0:T(8,128)(2,1)S(1)}, bf16[480,256]{1,0:T(8,128)(2,1)S(1)}, u32[]{:S(2)}, u32[]{:S(2)}) collective-permute-start(bf16[480,256]{1,0:T(8,128)(2,1)S(1)} %get-tuple-element.70), channel_id=1, source_target_pairs={{0,64},{32,96},{64,128},{96,160},{128,192},{160,224},{192,0},{224,... | collective-permute-start | bytes 737288 | tf_op jit(solution)/shard_map/ppermute | solution.py:38
  37.9 12.3 %collective-permute-start.20 = (bf16[480,256]{1,0:T(8,128)(2,1)S(1)}, bf16[480,256]{1,0:T(8,128)(2,1)S(1)}, u32[]{:S(2)}, u32[]{:S(2)}) collective-permute-start(bf16[480,256]{1,0:T(8,128)(2,1)S(1)} %get-tuple-element.71), channel_id=1, source_target_pairs={{0,192},{32,224},{64,0},{96,32},{128,64},{160,96},{192,128},{224,1... | collective-permute-start | bytes 737288 | tf_op jit(solution)/shard_map/ppermute | solution.py:38
  40.7 16.0 %collective-permute-start.11 = (bf16[400,256]{1,0:T(8,128)(2,1)S(1)}, bf16[400,256]{1,0:T(8,128)(2,1)S(1)}, u32[]{:S(2)}, u32[]{:S(2)}) collective-permute-start(bf16[400,256]{1,0:T(8,128)(2,1)S(1)} %shard_map.116), channel_id=1, source_target_pairs={{0,128},{32,160},{64,192},{96,224},{128,0},{160,32},{192,64},{224,... | collective-permute-start | bytes 614408 | tf_op jit(solution)/shard_map/ppermute | solution.py:38
  41.3 18.1 %collective-permute-start.12 = (bf16[400,256]{1,0:T(8,128)(2,1)S(1)}, bf16[400,256]{1,0:T(8,128)(2,1)S(1)}, u32[]{:S(2)}, u32[]{:S(2)}) collective-permute-start(bf16[400,256]{1,0:T(8,128)(2,1)S(1)} %shard_map.117), channel_id=1, source_target_pairs={{0,64},{32,96},{64,128},{96,160},{128,192},{160,224},{192,0},{224,... | collective-permute-start | bytes 614408 | tf_op jit(solution)/shard_map/ppermute | solution.py:38
  43.5 16.4 %collective-permute-start.13 = (bf16[400,256]{1,0:T(8,128)(2,1)S(1)}, bf16[400,256]{1,0:T(8,128)(2,1)S(1)}, u32[]{:S(2)}, u32[]{:S(2)}) collective-permute-start(bf16[400,256]{1,0:T(8,128)(2,1)S(1)} %shard_map.118), channel_id=1, source_target_pairs={{0,192},{32,224},{64,0},{96,32},{128,64},{160,96},{192,128},{224,1... | collective-permute-start | bytes 614408 | tf_op jit(solution)/shard_map/ppermute | solution.py:38
  50.6 29.2 %collective-permute-start.21 = (bf16[480,256]{1,0:T(8,128)(2,1)S(1)}, bf16[480,256]{1,0:T(8,128)(2,1)S(1)}, u32[]{:S(2)}, u32[]{:S(2)}) collective-permute-start(bf16[480,256]{1,0:T(8,128)(2,1)S(1)} %get-tuple-element.73), channel_id=1, source_target_pairs={{0,32},{32,0},{64,96},{96,64},{128,160},{160,128},{192,224},{224,1... | collective-permute-start | bytes 737288 | tf_op jit(solution)/shard_map/ppermute | solution.py:38
  56.0 24.0 %collective-permute-start.7 = (bf16[480,256]{1,0:T(8,128)(2,1)S(1)}, bf16[480,256]{1,0:T(8,128)(2,1)S(1)}, u32[]{:S(2)}, u32[]{:S(2)}) collective-permute-start(bf16[480,256]{1,0:T(8,128)(2,1)S(1)} %get-tuple-element.57), channel_id=1, source_target_pairs={{0,128},{32,160},{64,192},{96,224},{128,0},{160,32},{192,64},{224,... | collective-permute-start | bytes 737288 | tf_op jit(solution)/shard_map/ppermute | solution.py:38
  56.8 23.3 %collective-permute-start.8 = (bf16[480,256]{1,0:T(8,128)(2,1)S(1)}, bf16[480,256]{1,0:T(8,128)(2,1)S(1)}, u32[]{:S(2)}, u32[]{:S(2)}) collective-permute-start(bf16[480,256]{1,0:T(8,128)(2,1)S(1)} %get-tuple-element.58), channel_id=1, source_target_pairs={{0,64},{32,96},{64,128},{96,160},{128,192},{160,224},{192,0},{224,... | collective-permute-start | bytes 737288 | tf_op jit(solution)/shard_map/ppermute | solution.py:38
  59.4 20.7 %collective-permute-start.9 = (bf16[480,256]{1,0:T(8,128)(2,1)S(1)}, bf16[480,256]{1,0:T(8,128)(2,1)S(1)}, u32[]{:S(2)}, u32[]{:S(2)}) collective-permute-start(bf16[480,256]{1,0:T(8,128)(2,1)S(1)} %get-tuple-element.59), channel_id=1, source_target_pairs={{0,192},{32,224},{64,0},{96,32},{128,64},{160,96},{192,128},{224,1... | collective-permute-start | bytes 737288 | tf_op jit(solution)/shard_map/ppermute | solution.py:38
  60.5 19.1 %collective-permute-start.14 = (bf16[400,256]{1,0:T(8,128)(2,1)S(1)}, bf16[400,256]{1,0:T(8,128)(2,1)S(1)}, u32[]{:S(2)}, u32[]{:S(2)}) collective-permute-start(bf16[400,256]{1,0:T(8,128)(2,1)S(1)} %get-tuple-element.65), channel_id=1, source_target_pairs={{0,32},{32,0},{64,96},{96,64},{128,160},{160,128},{192,224},{224,1... | collective-permute-start | bytes 614408 | tf_op jit(solution)/shard_map/ppermute | solution.py:38
  79.9 22.2 %collective-permute-start.22 = (bf16[496,256]{1,0:T(8,128)(2,1)S(1)}, bf16[496,256]{1,0:T(8,128)(2,1)S(1)}, u32[]{:S(2)}, u32[]{:S(2)}) collective-permute-start(bf16[496,256]{1,0:T(8,128)(2,1)S(1)} %shard_map.124.a_ref.refs_0_), channel_id=1, source_target_pairs={{0,128},{32,160},{64,192},{96,224},{128,0},{160,32},{192,64},{224,... | collective-permute-start | bytes 761864 | tf_op jit(solution)/shard_map/ppermute | solution.py:38
  80.5 14.1 %collective-permute-start.10 = (bf16[480,256]{1,0:T(8,128)(2,1)S(1)}, bf16[480,256]{1,0:T(8,128)(2,1)S(1)}, u32[]{:S(2)}, u32[]{:S(2)}) collective-permute-start(bf16[480,256]{1,0:T(8,128)(2,1)S(1)} %get-tuple-element.61), channel_id=1, source_target_pairs={{0,32},{32,0},{64,96},{96,64},{128,160},{160,128},{192,224},{224,1... | collective-permute-start | bytes 737288 | tf_op jit(solution)/shard_map/ppermute | solution.py:38
  82.2 15.2 %collective-permute-start.25 = (bf16[416,256]{1,0:T(8,128)(2,1)S(1)}, bf16[416,256]{1,0:T(8,128)(2,1)S(1)}, u32[]{:S(2)}, u32[]{:S(2)}) collective-permute-start(bf16[416,256]{1,0:T(8,128)(2,1)S(1)} %get-tuple-element.74.a_ref.refs_0_), channel_id=1, source_target_pairs={{0,128},{32,160},{64,192},{96,224},{128,0},{160,32},{192,64},{224,... | collective-permute-start | bytes 638984 | tf_op jit(solution)/shard_map/ppermute | solution.py:38
  85.1 15.0 %collective-permute-start.26 = (bf16[416,256]{1,0:T(8,128)(2,1)S(1)}, bf16[416,256]{1,0:T(8,128)(2,1)S(1)}, u32[]{:S(2)}, u32[]{:S(2)}) collective-permute-start(bf16[416,256]{1,0:T(8,128)(2,1)S(1)} %get-tuple-element.74.a_ref.refs_0_), channel_id=1, source_target_pairs={{0,64},{32,96},{64,128},{96,160},{128,192},{160,224},{192,0},{224,... | collective-permute-start | bytes 638984 | tf_op jit(solution)/shard_map/ppermute | solution.py:38
  86.3 15.1 %collective-permute-start.27 = (bf16[416,256]{1,0:T(8,128)(2,1)S(1)}, bf16[416,256]{1,0:T(8,128)(2,1)S(1)}, u32[]{:S(2)}, u32[]{:S(2)}) collective-permute-start(bf16[416,256]{1,0:T(8,128)(2,1)S(1)} %get-tuple-element.74.a_ref.refs_0_), channel_id=1, source_target_pairs={{0,192},{32,224},{64,0},{96,32},{128,64},{160,96},{192,128},{224,1... | collective-permute-start | bytes 638984 | tf_op jit(solution)/shard_map/ppermute | solution.py:38
  94.6 11.3 %collective-permute-start.23 = (bf16[496,256]{1,0:T(8,128)(2,1)S(1)}, bf16[496,256]{1,0:T(8,128)(2,1)S(1)}, u32[]{:S(2)}, u32[]{:S(2)}) collective-permute-start(bf16[496,256]{1,0:T(8,128)(2,1)S(1)} %shard_map.124.a_ref.refs_0_), channel_id=1, source_target_pairs={{0,64},{32,96},{64,128},{96,160},{128,192},{160,224},{192,0},{224,... | collective-permute-start | bytes 761864 | tf_op jit(solution)/shard_map/ppermute | solution.py:38
  97.4 9.9 %collective-permute-start.24 = (bf16[496,256]{1,0:T(8,128)(2,1)S(1)}, bf16[496,256]{1,0:T(8,128)(2,1)S(1)}, u32[]{:S(2)}, u32[]{:S(2)}) collective-permute-start(bf16[496,256]{1,0:T(8,128)(2,1)S(1)} %shard_map.124.a_ref.refs_0_), channel_id=1, source_target_pairs={{0,192},{32,224},{64,0},{96,32},{128,64},{160,96},{192,128},{224,1... | collective-permute-start | bytes 761864 | tf_op jit(solution)/shard_map/ppermute | solution.py:38
  100.1 12.1 %collective-permute-start.15 = (bf16[496,256]{1,0:T(8,128)(2,1)S(1)}, bf16[496,256]{1,0:T(8,128)(2,1)S(1)}, u32[]{:S(2)}, u32[]{:S(2)}) collective-permute-start(bf16[496,256]{1,0:T(8,128)(2,1)S(1)} %shard_map.121.a_ref.refs_0_), channel_id=1, source_target_pairs={{0,128},{32,160},{64,192},{96,224},{128,0},{160,32},{192,64},{224,... | collective-permute-start | bytes 761864 | tf_op jit(solution)/shard_map/ppermute | solution.py:38
  101.4 15.3 %collective-permute-start.16 = (bf16[496,256]{1,0:T(8,128)(2,1)S(1)}, bf16[496,256]{1,0:T(8,128)(2,1)S(1)}, u32[]{:S(2)}, u32[]{:S(2)}) collective-permute-start(bf16[496,256]{1,0:T(8,128)(2,1)S(1)} %shard_map.121.a_ref.refs_0_), channel_id=1, source_target_pairs={{0,64},{32,96},{64,128},{96,160},{128,192},{160,224},{192,0},{224,... | collective-permute-start | bytes 761864 | tf_op jit(solution)/shard_map/ppermute | solution.py:38
  102.1 14.6 %collective-permute-start.17 = (bf16[496,256]{1,0:T(8,128)(2,1)S(1)}, bf16[496,256]{1,0:T(8,128)(2,1)S(1)}, u32[]{:S(2)}, u32[]{:S(2)}) collective-permute-start(bf16[496,256]{1,0:T(8,128)(2,1)S(1)} %shard_map.121.a_ref.refs_0_), channel_id=1, source_target_pairs={{0,192},{32,224},{64,0},{96,32},{128,64},{160,96},{192,128},{224,1... | collective-permute-start | bytes 761864 | tf_op jit(solution)/shard_map/ppermute | solution.py:38
  118.0 3.5 %collective-permute-start.28 = (bf16[520,1024]{1,0:T(8,128)(2,1)S(1)}, bf16[520,1024]{1,0:T(8,128)(2,1)S(1)}, u32[]{:S(2)}, u32[]{:S(2)}) collective-permute-start(bf16[520,1024]{1,0:T(8,128)(2,1)S(1)} %get-tuple-element.82), channel_id=1, source_target_pairs={{0,4},{4,0},{8,12},{12,8},{16,20},{20,16},{24,28},{28,24},{1,5},{5... | collective-permute-start | bytes 3194888 | tf_op jit(solution)/shard_map/ppermute | solution.py:38
  121.7 13.5 %collective-permute-start.29 = (bf16[136,1024]{1,0:T(8,128)(2,1)S(1)}, bf16[136,1024]{1,0:T(8,128)(2,1)S(1)}, u32[]{:S(2)}, u32[]{:S(2)}) collective-permute-start(bf16[136,1024]{1,0:T(8,128)(2,1)S(1)} %get-tuple-element.86), channel_id=1, source_target_pairs={{0,8},{4,12},{8,0},{12,4},{16,24},{20,28},{24,16},{28,20},{1,9},{5... | collective-permute-start | bytes 835592 | tf_op jit(solution)/shard_map/ppermute | solution.py:38
  121.8 13.4 %collective-permute-start.30 = (bf16[136,1024]{1,0:T(8,128)(2,1)S(1)}, bf16[136,1024]{1,0:T(8,128)(2,1)S(1)}, u32[]{:S(2)}, u32[]{:S(2)}) collective-permute-start(bf16[136,1024]{1,0:T(8,128)(2,1)S(1)} %get-tuple-element.87), channel_id=1, source_target_pairs={{0,16},{4,20},{8,24},{12,28},{16,0},{20,4},{24,8},{28,12},{1,17},{... | collective-permute-start | bytes 835592 | tf_op jit(solution)/shard_map/ppermute | solution.py:38
  125.4 32.6 %collective-permute-start.37 = (bf16[480,512]{1,0:T(8,128)(2,1)S(1)}, bf16[480,512]{1,0:T(8,128)(2,1)S(1)}, u32[]{:S(2)}, u32[]{:S(2)}) collective-permute-start(bf16[480,512]{1,0:T(8,128)(2,1)S(1)} %shard_map.133.refs_4_), channel_id=1, source_target_pairs={{0,2},{1,3},{2,0},{3,1},{4,6},{5,7},{6,4},{7,5},{8,10},{9,11},{10,... | collective-permute-start | bytes 1474568 | tf_op jit(solution)/shard_map/ppermute | solution.py:38
  126.1 21.2 %collective-permute-start.34 = (bf16[384,512]{1,0:T(8,128)(2,1)S(1)}, bf16[384,512]{1,0:T(8,128)(2,1)S(1)}, u32[]{:S(2)}, u32[]{:S(2)}) collective-permute-start(bf16[384,512]{1,0:T(8,128)(2,1)S(1)} %shard_map.132.refs_0_), channel_id=1, source_target_pairs={{0,2},{1,3},{2,0},{3,1},{4,6},{5,7},{6,4},{7,5},{8,10},{9,11},{10,... | collective-permute-start | bytes 1179656 | tf_op jit(solution)/shard_map/ppermute | solution.py:38
  129.1 13.9 %collective-permute-start.31 = (bf16[136,1024]{1,0:T(8,128)(2,1)S(1)}, bf16[136,1024]{1,0:T(8,128)(2,1)S(1)}, u32[]{:S(2)}, u32[]{:S(2)}) collective-permute-start(bf16[136,1024]{1,0:T(8,128)(2,1)S(1)} %get-tuple-element.88), channel_id=1, source_target_pairs={{0,24},{4,28},{8,16},{12,20},{16,8},{20,12},{24,0},{28,4},{1,25},{... | collective-permute-start | bytes 835592 | tf_op jit(solution)/shard_map/ppermute | solution.py:38
  135.2 18.1 %collective-permute-start.35 = (bf16[384,512]{1,0:T(8,128)(2,1)S(1)}, bf16[384,512]{1,0:T(8,128)(2,1)S(1)}, u32[]{:S(2)}, u32[]{:S(2)}) collective-permute-start(bf16[384,512]{1,0:T(8,128)(2,1)S(1)} %shard_map.132.refs_0_), channel_id=1, source_target_pairs={{0,1},{1,0},{2,3},{3,2},{4,5},{5,4},{6,7},{7,6},{8,9},{9,8},{10,11... | collective-permute-start | bytes 1179656 | tf_op jit(solution)/shard_map/ppermute | solution.py:38
  135.2 21.1 %collective-permute-start.36 = (bf16[384,512]{1,0:T(8,128)(2,1)S(1)}, bf16[384,512]{1,0:T(8,128)(2,1)S(1)}, u32[]{:S(2)}, u32[]{:S(2)}) collective-permute-start(bf16[384,512]{1,0:T(8,128)(2,1)S(1)} %shard_map.132.refs_0_), channel_id=1, source_target_pairs={{0,3},{1,2},{2,1},{3,0},{4,7},{5,6},{6,5},{7,4},{8,11},{9,10},{10,... | collective-permute-start | bytes 1179656 | tf_op jit(solution)/shard_map/ppermute | solution.py:38
  143.2 15.7 %collective-permute-start.32 = (bf16[72,1024]{1,0:T(8,128)(2,1)S(1)}, bf16[72,1024]{1,0:T(8,128)(2,1)S(1)}, u32[]{:S(2)}, u32[]{:S(2)}) collective-permute-start(bf16[72,1024]{1,0:T(8,128)(2,1)S(1)} %get-tuple-element.92), channel_id=1, source_target_pairs={{0,2},{1,3},{2,0},{3,1},{4,6},{5,7},{6,4},{7,5},{8,10},{9,11},{10,... | collective-permute-start | bytes 442376 | tf_op jit(solution)/shard_map/ppermute | solution.py:38
  147.3 19.7 %collective-permute-start.38 = (bf16[480,512]{1,0:T(8,128)(2,1)S(1)}, bf16[480,512]{1,0:T(8,128)(2,1)S(1)}, u32[]{:S(2)}, u32[]{:S(2)}) collective-permute-start(bf16[480,512]{1,0:T(8,128)(2,1)S(1)} %shard_map.133.refs_4_), channel_id=1, source_target_pairs={{0,1},{1,0},{2,3},{3,2},{4,5},{5,4},{6,7},{7,6},{8,9},{9,8},{10,11... | collective-permute-start | bytes 1474568 | tf_op jit(solution)/shard_map/ppermute | solution.py:38
  153.3 16.6 %collective-permute-start.39 = (bf16[480,512]{1,0:T(8,128)(2,1)S(1)}, bf16[480,512]{1,0:T(8,128)(2,1)S(1)}, u32[]{:S(2)}, u32[]{:S(2)}) collective-permute-start(bf16[480,512]{1,0:T(8,128)(2,1)S(1)} %shard_map.133.refs_4_), channel_id=1, source_target_pairs={{0,3},{1,2},{2,1},{3,0},{4,7},{5,6},{6,5},{7,4},{8,11},{9,10},{10,... | collective-permute-start | bytes 1474568 | tf_op jit(solution)/shard_map/ppermute | solution.py:38
  156.4 23.6 %collective-permute-start.40 = (bf16[480,512]{1,0:T(8,128)(2,1)S(1)}, bf16[480,512]{1,0:T(8,128)(2,1)S(1)}, u32[]{:S(2)}, u32[]{:S(2)}) collective-permute-start(bf16[480,512]{1,0:T(8,128)(2,1)S(1)} %shard_map.134.refs_8_), channel_id=1, source_target_pairs={{0,2},{1,3},{2,0},{3,1},{4,6},{5,7},{6,4},{7,5},{8,10},{9,11},{10,... | collective-permute-start | bytes 1474568 | tf_op jit(solution)/shard_map/ppermute | solution.py:38
  157.9 30.2 %collective-permute-start.41 = (bf16[480,512]{1,0:T(8,128)(2,1)S(1)}, bf16[480,512]{1,0:T(8,128)(2,1)S(1)}, u32[]{:S(2)}, u32[]{:S(2)}) collective-permute-start(bf16[480,512]{1,0:T(8,128)(2,1)S(1)} %shard_map.134.refs_8_), channel_id=1, source_target_pairs={{0,1},{1,0},{2,3},{3,2},{4,5},{5,4},{6,7},{7,6},{8,9},{9,8},{10,11... | collective-permute-start | bytes 1474568 | tf_op jit(solution)/shard_map/ppermute | solution.py:38
  158.9 31.9 %collective-permute-start.42 = (bf16[480,512]{1,0:T(8,128)(2,1)S(1)}, bf16[480,512]{1,0:T(8,128)(2,1)S(1)}, u32[]{:S(2)}, u32[]{:S(2)}) collective-permute-start(bf16[480,512]{1,0:T(8,128)(2,1)S(1)} %shard_map.134.refs_8_), channel_id=1, source_target_pairs={{0,3},{1,2},{2,1},{3,0},{4,7},{5,6},{6,5},{7,4},{8,11},{9,10},{10,... | collective-permute-start | bytes 1474568 | tf_op jit(solution)/shard_map/ppermute | solution.py:38
  167.0 28.2 %copy-start.1 = (bf16[32,512]{1,0:T(8,128)(2,1)S(1)}, bf16[32,512]{1,0:T(8,128)(2,1)}, u32[]{:S(2)}) copy-start(bf16[32,512]{1,0:T(8,128)(2,1)} %tok_ref.3) | copy-start | bytes 98308
  167.0 28.2 %copy-start.2 = (bf16[32,512]{1,0:T(8,128)(2,1)S(1)}, bf16[32,512]{1,0:T(8,128)(2,1)}, u32[]{:S(2)}) copy-start(bf16[32,512]{1,0:T(8,128)(2,1)} %cot_ref.3) | copy-start | bytes 98308
  167.0 28.2 %collective-permute-start.33 = (bf16[40,1024]{1,0:T(8,128)(2,1)S(1)}, bf16[40,1024]{1,0:T(8,128)(2,1)S(1)}, u32[]{:S(2)}, u32[]{:S(2)}) collective-permute-start(bf16[40,1024]{1,0:T(8,128)(2,1)S(1)} %get-tuple-element.97), channel_id=1, source_target_pairs={{0,1},{1,0},{2,3},{3,2},{4,5},{5,4},{6,7},{7,6},{8,9},{9,8},{10,11... | collective-permute-start | bytes 245768 | tf_op jit(solution)/shard_map/ppermute | solution.py:38

commit v5 on v4

--- a/solution.py
+++ b/solution.py
@@ -482,6 +482,11 @@
         for k in ks:
             group[1].append((k, [send_y(group[1][0][1][0], k)]))
 
+    def relay(group):
+        near = {source: pieces[0] for source, pieces in group[1]}
+        half = near[0].shape[0] // 2
+        group[1].append((2, [send_y(near[1][:half], 3), send_y(near[3][half:], 1)]))
+
     def back(n, before):
         _, size, wgu, wd = chunks[n]
         return back_call(x_at, pieces[n], wgu, wd, before, both, size, n == count - 1)
@@ -499,7 +504,7 @@
     *before, own_inv = back(0, None)
     middle(2, inv)
     groups.append(weight_grad((1,)))
-    spread(groups[1], (2, 1, 3))
+    spread(groups[1], (1, 3))
     before = back(1, before)
     own, gain_part, inner, message = back(2, before)
     message = send_core(message)
@@ -507,15 +512,16 @@
     strips = [[(128 * a + 32 * j, 32) for a in range(4)] for j in range(4)]
     own, gain_part, inner, *messages = fold_call(own, gain_part, inner, [message], [None], strips)
     messages = [send_zl(m, k) for k, m in zip((1, 2, 3), messages)]
+    relay(groups[1])
     spread(groups[2], (2, 1, 3))
     turns = [lambda v, lanes=lanes: turn_left(v, lanes) for lanes in (32, 64, 96)]
     own, gain_part, inner, *messages = fold_call(
         own, gain_part, inner, messages, turns, [[(0, 64)], [(64, 64)]])
     message = send_y(messages[0], 2)
-    out_gate, out_up, out_down = assemble_call(depth_at, groups)
     own, gain_part, inner, *messages = fold_call(
         own, gain_part, inner, [message], [upper_half], [[(0, 32)], [(32, 32)]])
     message = send_y(messages[0], 1)
+    out_gate, out_up, out_down = assemble_call(depth_at, groups)
     output, grad_tokens, gain_grad = final_call(own, gain_part, inner, own_inv, message, tokens, cotangent, gain)
     return output, grad_tokens, gain_grad[0], out_gate, out_up, out_down
 

time: 196 us -> 195 us (level)
  waiting for transfers between devices: 114 us -> 108 us
  starting transfers between devices: 63.7 us -> 67.6 us
    ppermute x43 -> x44, waiting for transfers between devices: 114 us -> 108 us  [send(): return lax.ppermute(v, axis, perm)]
    ppermute x43 -> x44, starting transfers between devices: 63.7 us -> 67.6 us  [send(): return lax.ppermute(v, axis, perm)]
  transfers between devices with their start and end apart: 43 -> 44, of which waited for: 26 -> 22; matrix products, arithmetic and copies ran while one was open for 0% -> 0% of each run, Pallas kernels for 7% -> 7%
where the time goes in v5:
time: 195 us
  waiting for transfers between devices  108 us (55%)
  starting transfers between devices  67.6 us (35%)
  Pallas kernels  18 us (9%)
    ppermute x44, waiting for transfers between devices, send(): return lax.ppermute(v, axis, perm)  108 us
    ppermute x44, starting transfers between devices, send(): return lax.ppermute(v, axis, perm)  67.6 us
    pallas_call x27, Pallas kernels, call(): return run(*scalars, *placed)  18 us
  transfers between devices with their start and end apart: 44, of which 22 were waited for; matrix products, arithmetic and copies ran while one was open for 0% of the time, Pallas kernels for 7%

profile of v5, /device:TPU:1, one launch (start us, length us, event | category | flops | bytes accessed | tf_op | source)
XLA Modules:
  0.0 194.5 jit_solution(2313411090113435285)
XLA Ops:
  0.6 0.8 shard_map.109.refs_0_
  1.4 2.5 %collective-permute-start = (bf16[32,1024]{1,0:T(8,128)(2,1)S(1)}, bf16[32,1024]{1,0:T(8,128)(2,1)S(1)}, u32[]{:S(2)}, u32[]{:S(2)}) collective-permute-start(bf16[32,1024]{1,0:T(8,128)(2,1)S(1)} %shard_map.109.refs_0_), channel_id=1, source_target_pairs={{0,8},{4,12},{8,0},{12,4},{16,24},{20,28},{24,16},{28,20},{1,9},{5... | collective-permute-start | bytes 196616 | tf_op jit(solution)/shard_map/ppermute | solution.py:38
  3.9 3.0 %collective-permute-start.1 = (bf16[32,1024]{1,0:T(8,128)(2,1)S(1)}, bf16[32,1024]{1,0:T(8,128)(2,1)S(1)}, u32[]{:S(2)}, u32[]{:S(2)}) collective-permute-start(bf16[32,1024]{1,0:T(8,128)(2,1)S(1)} %shard_map.109.refs_0_), channel_id=1, source_target_pairs={{0,16},{4,20},{8,24},{12,28},{16,0},{20,4},{24,8},{28,12},{1,17},{... | collective-permute-start | bytes 196616 | tf_op jit(solution)/shard_map/ppermute | solution.py:38
  6.9 2.6 %collective-permute-done.1.refs_2_ = bf16[32,1024]{1,0:T(8,128)(2,1)S(1)} collective-permute-done((bf16[32,1024]{1,0:T(8,128)(2,1)S(1)}, bf16[32,1024]{1,0:T(8,128)(2,1)S(1)}, u32[]{:S(2)}, u32[]{:S(2)}) %collective-permute-start.1) | collective-permute-done | bytes 65568 | tf_op jit(solution)/shard_map/ppermute | solution.py:38
  9.5 2.3 %collective-permute-done.2.refs_3_ = bf16[32,1024]{1,0:T(8,128)(2,1)S(1)} collective-permute-done((bf16[32,1024]{1,0:T(8,128)(2,1)S(1)}, bf16[32,1024]{1,0:T(8,128)(2,1)S(1)}, u32[]{:S(2)}, u32[]{:S(2)}) %collective-permute-start.2) | collective-permute-done | bytes 65568 | tf_op jit(solution)/shard_map/ppermute | solution.py:38
  11.8 1.5 collective-permute-start.3
  13.3 2.6 %collective-permute-start.4 = (bf16[128,1024]{1,0:T(8,128)(2,1)S(1)}, bf16[128,1024]{1,0:T(8,128)(2,1)S(1)}, u32[]{:S(2)}, u32[]{:S(2)}) collective-permute-start(bf16[128,1024]{1,0:T(8,128)(2,1)S(1)} %shard_map.110.refs_0_), channel_id=1, source_target_pairs={{0,2},{1,3},{2,0},{3,1},{4,6},{5,7},{6,4},{7,5},{8,10},{9,11},{10,... | collective-permute-start | bytes 786440 | tf_op jit(solution)/shard_map/ppermute | solution.py:38
  15.9 1.2 collective-permute-done.3.refs_1_
  17.1 8.5 %collective-permute-done.4.refs_2_ = bf16[128,1024]{1,0:T(8,128)(2,1)S(1)} collective-permute-done((bf16[128,1024]{1,0:T(8,128)(2,1)S(1)}, bf16[128,1024]{1,0:T(8,128)(2,1)S(1)}, u32[]{:S(2)}, u32[]{:S(2)}) %collective-permute-start.4) | collective-permute-done | bytes 262176 | tf_op jit(solution)/shard_map/ppermute | solution.py:38
  25.6 3.7 %collective-permute-done.5.refs_3_ = bf16[128,1024]{1,0:T(8,128)(2,1)S(1)} collective-permute-done((bf16[128,1024]{1,0:T(8,128)(2,1)S(1)}, bf16[128,1024]{1,0:T(8,128)(2,1)S(1)}, u32[]{:S(2)}, u32[]{:S(2)}) %collective-permute-start.5) | collective-permute-done | bytes 262176 | tf_op jit(solution)/shard_map/ppermute | solution.py:38
  29.4 2.2 %collective-permute-start.6 = (bf16[512,1024]{1,0:T(8,128)(2,1)S(1)}, bf16[512,1024]{1,0:T(8,128)(2,1)S(1)}, u32[]{:S(2)}, u32[]{:S(2)}) collective-permute-start(bf16[512,1024]{1,0:T(8,128)(2,1)S(1)} %shard_map.111.refs_0_), channel_id=1, source_target_pairs={{0,4},{4,0},{8,12},{12,8},{16,20},{20,16},{24,28},{28,24},{1,5},{5... | collective-permute-start | bytes 3145736 | tf_op jit(solution)/shard_map/ppermute | solution.py:38
  31.6 1.6 shard_map.113
  33.2 0.7 collective-permute-done.6.refs_1_
  34.0 0.7 shard_map.122
  34.8 2.8 %collective-permute-start.18 = (bf16[480,256]{1,0:T(8,128)(2,1)S(1)}, bf16[480,256]{1,0:T(8,128)(2,1)S(1)}, u32[]{:S(2)}, u32[]{:S(2)}) collective-permute-start(bf16[480,256]{1,0:T(8,128)(2,1)S(1)} %get-tuple-element.69), channel_id=1, source_target_pairs={{0,128},{32,160},{64,192},{96,224},{128,0},{160,32},{192,64},{224,... | collective-permute-start | bytes 737288 | tf_op jit(solution)/shard_map/ppermute | solution.py:38
  37.9 2.4 %collective-permute-start.20 = (bf16[480,256]{1,0:T(8,128)(2,1)S(1)}, bf16[480,256]{1,0:T(8,128)(2,1)S(1)}, u32[]{:S(2)}, u32[]{:S(2)}) collective-permute-start(bf16[480,256]{1,0:T(8,128)(2,1)S(1)} %get-tuple-element.71), channel_id=1, source_target_pairs={{0,192},{32,224},{64,0},{96,32},{128,64},{160,96},{192,128},{224,1... | collective-permute-start | bytes 737288 | tf_op jit(solution)/shard_map/ppermute | solution.py:38
  41.3 0.6 collective-permute-start.12
  42.3 1.2 collective-permute-done.18.a_ref
  43.5 2.5 %collective-permute-start.13 = (bf16[400,256]{1,0:T(8,128)(2,1)S(1)}, bf16[400,256]{1,0:T(8,128)(2,1)S(1)}, u32[]{:S(2)}, u32[]{:S(2)}) collective-permute-start(bf16[400,256]{1,0:T(8,128)(2,1)S(1)} %shard_map.118), channel_id=1, source_target_pairs={{0,192},{32,224},{64,0},{96,32},{128,64},{160,96},{192,128},{224,1... | collective-permute-start | bytes 614408 | tf_op jit(solution)/shard_map/ppermute | solution.py:38
  46.0 4.2 %collective-permute-done.19.b_ref = bf16[480,256]{1,0:T(8,128)(2,1)S(1)} collective-permute-done((bf16[480,256]{1,0:T(8,128)(2,1)S(1)}, bf16[480,256]{1,0:T(8,128)(2,1)S(1)}, u32[]{:S(2)}, u32[]{:S(2)}) %collective-permute-start.19) | collective-permute-done | bytes 245792 | tf_op jit(solution)/shard_map/ppermute | solution.py:38
  50.6 4.7 %collective-permute-start.21 = (bf16[480,256]{1,0:T(8,128)(2,1)S(1)}, bf16[480,256]{1,0:T(8,128)(2,1)S(1)}, u32[]{:S(2)}, u32[]{:S(2)}) collective-permute-start(bf16[480,256]{1,0:T(8,128)(2,1)S(1)} %get-tuple-element.73), channel_id=1, source_target_pairs={{0,32},{32,0},{64,96},{96,64},{128,160},{160,128},{192,224},{224,1... | collective-permute-start | bytes 737288 | tf_op jit(solution)/shard_map/ppermute | solution.py:38
  55.3 0.7 shard_map.114
  56.0 0.7 collective-permute-start.7
  56.8 2.6 %collective-permute-start.8 = (bf16[480,256]{1,0:T(8,128)(2,1)S(1)}, bf16[480,256]{1,0:T(8,128)(2,1)S(1)}, u32[]{:S(2)}, u32[]{:S(2)}) collective-permute-start(bf16[480,256]{1,0:T(8,128)(2,1)S(1)} %get-tuple-element.58), channel_id=1, source_target_pairs={{0,64},{32,96},{64,128},{96,160},{128,192},{160,224},{192,0},{224,... | collective-permute-start | bytes 737288 | tf_op jit(solution)/shard_map/ppermute | solution.py:38
  60.5 3.7 %collective-permute-start.14 = (bf16[400,256]{1,0:T(8,128)(2,1)S(1)}, bf16[400,256]{1,0:T(8,128)(2,1)S(1)}, u32[]{:S(2)}, u32[]{:S(2)}) collective-permute-start(bf16[400,256]{1,0:T(8,128)(2,1)S(1)} %get-tuple-element.65), channel_id=1, source_target_pairs={{0,32},{32,0},{64,96},{96,64},{128,160},{160,128},{192,224},{224,1... | collective-permute-start | bytes 614408 | tf_op jit(solution)/shard_map/ppermute | solution.py:38
  64.2 15.4 %collective-permute-done.14.other_ref = bf16[400,256]{1,0:T(8,128)(2,1)S(1)} collective-permute-done((bf16[400,256]{1,0:T(8,128)(2,1)S(1)}, bf16[400,256]{1,0:T(8,128)(2,1)S(1)}, u32[]{:S(2)}, u32[]{:S(2)}) %collective-permute-start.14) | collective-permute-done | bytes 204832 | tf_op jit(solution)/shard_map/ppermute | solution.py:38
  80.5 1.7 collective-permute-start.10
  82.1 2.9 %collective-permute-start.25 = (bf16[416,256]{1,0:T(8,128)(2,1)S(1)}, bf16[416,256]{1,0:T(8,128)(2,1)S(1)}, u32[]{:S(2)}, u32[]{:S(2)}) collective-permute-start(bf16[416,256]{1,0:T(8,128)(2,1)S(1)} %get-tuple-element.74.a_ref.refs_0_), channel_id=1, source_target_pairs={{0,128},{32,160},{64,192},{96,224},{128,0},{160,32},{192,64},{224,... | collective-permute-start | bytes 638984 | tf_op jit(solution)/shard_map/ppermute | solution.py:38
  85.1 1.2 collective-permute-start.26
  86.2 1.5 collective-permute-start.27
  87.8 6.8 %collective-permute-done.10.other_ref = bf16[480,256]{1,0:T(8,128)(2,1)S(1)} collective-permute-done((bf16[480,256]{1,0:T(8,128)(2,1)S(1)}, bf16[480,256]{1,0:T(8,128)(2,1)S(1)}, u32[]{:S(2)}, u32[]{:S(2)}) %collective-permute-start.10) | collective-permute-done | bytes 245792 | tf_op jit(solution)/shard_map/ppermute | solution.py:38
  94.6 2.6 %collective-permute-start.23 = (bf16[496,256]{1,0:T(8,128)(2,1)S(1)}, bf16[496,256]{1,0:T(8,128)(2,1)S(1)}, u32[]{:S(2)}, u32[]{:S(2)}) collective-permute-start(bf16[496,256]{1,0:T(8,128)(2,1)S(1)} %shard_map.124.a_ref.refs_0_), channel_id=1, source_target_pairs={{0,64},{32,96},{64,128},{96,160},{128,192},{160,224},{192,0},{224,... | collective-permute-start | bytes 761864 | tf_op jit(solution)/shard_map/ppermute | solution.py:38
  97.3 2.7 %collective-permute-start.24 = (bf16[496,256]{1,0:T(8,128)(2,1)S(1)}, bf16[496,256]{1,0:T(8,128)(2,1)S(1)}, u32[]{:S(2)}, u32[]{:S(2)}) collective-permute-start(bf16[496,256]{1,0:T(8,128)(2,1)S(1)} %shard_map.124.a_ref.refs_0_), channel_id=1, source_target_pairs={{0,192},{32,224},{64,0},{96,32},{128,64},{160,96},{192,128},{224,1... | collective-permute-start | bytes 761864 | tf_op jit(solution)/shard_map/ppermute | solution.py:38
  100.1 1.3 collective-permute-start.15
  101.4 0.8 collective-permute-start.16
  102.1 1.9 collective-permute-start.17
  104.0 0.7 shard_map.125
  104.8 1.0 collective-permute-done.23.c_ref.refs_2_
  105.8 1.4 collective-permute-done.24.d_ref.refs_3_
  107.3 1.0 shard_map.126
  108.3 3.9 %collective-permute-done.15.b_ref.refs_1_ = bf16[496,256]{1,0:T(8,128)(2,1)S(1)} collective-permute-done((bf16[496,256]{1,0:T(8,128)(2,1)S(1)}, bf16[496,256]{1,0:T(8,128)(2,1)S(1)}, u32[]{:S(2)}, u32[]{:S(2)}) %collective-permute-start.15) | collective-permute-done | bytes 253984 | tf_op jit(solution)/shard_map/ppermute | solution.py:38
  112.2 4.5 %collective-permute-done.16.c_ref.refs_2_ = bf16[496,256]{1,0:T(8,128)(2,1)S(1)} collective-permute-done((bf16[496,256]{1,0:T(8,128)(2,1)S(1)}, bf16[496,256]{1,0:T(8,128)(2,1)S(1)}, u32[]{:S(2)}, u32[]{:S(2)}) %collective-permute-start.16) | collective-permute-done | bytes 253984 | tf_op jit(solution)/shard_map/ppermute | solution.py:38
  116.7 1.3 shard_map.127
  118.0 1.2 collective-permute-start.28
  120.5 0.7 shard_map.133.refs_4_
  121.2 1.1 collective-permute-start.37
  122.2 1.8 collective-permute-start.38
  124.3 7.7 %collective-permute-done.34.refs_1_ = bf16[384,512]{1,0:T(8,128)(2,1)S(1)} collective-permute-done((bf16[384,512]{1,0:T(8,128)(2,1)S(1)}, bf16[384,512]{1,0:T(8,128)(2,1)S(1)}, u32[]{:S(2)}, u32[]{:S(2)}) %collective-permute-start.34) | collective-permute-done | bytes 393248 | tf_op jit(solution)/shard_map/ppermute | solution.py:38
  132.1 6.0 %collective-permute-done.35.refs_2_ = bf16[384,512]{1,0:T(8,128)(2,1)S(1)} collective-permute-done((bf16[384,512]{1,0:T(8,128)(2,1)S(1)}, bf16[384,512]{1,0:T(8,128)(2,1)S(1)}, u32[]{:S(2)}, u32[]{:S(2)}) %collective-permute-start.35) | collective-permute-done | bytes 393248 | tf_op jit(solution)/shard_map/ppermute | solution.py:38
  138.1 2.5 %collective-permute-start.31 = (bf16[136,1024]{1,0:T(8,128)(2,1)S(1)}, bf16[136,1024]{1,0:T(8,128)(2,1)S(1)}, u32[]{:S(2)}, u32[]{:S(2)}) collective-permute-start(bf16[136,1024]{1,0:T(8,128)(2,1)S(1)} %get-tuple-element.88), channel_id=1, source_target_pairs={{0,24},{4,28},{8,16},{12,20},{16,8},{20,12},{24,0},{28,4},{1,25},{... | collective-permute-start | bytes 835592 | tf_op jit(solution)/shard_map/ppermute | solution.py:38
  140.7 8.0 %collective-permute-done.37.refs_5_ = bf16[480,512]{1,0:T(8,128)(2,1)S(1)} collective-permute-done((bf16[480,512]{1,0:T(8,128)(2,1)S(1)}, bf16[480,512]{1,0:T(8,128)(2,1)S(1)}, u32[]{:S(2)}, u32[]{:S(2)}) %collective-permute-start.37) | collective-permute-done | bytes 491552 | tf_op jit(solution)/shard_map/ppermute | solution.py:38
  148.6 2.7 %collective-permute-start.36 = (bf16[384,512]{1,0:T(8,128)(2,1)S(1)}, bf16[384,512]{1,0:T(8,128)(2,1)S(1)}, u32[]{:S(2)}, u32[]{:S(2)}) collective-permute-start(bf16[384,512]{1,0:T(8,128)(2,1)S(1)} %shard_map.132.refs_0_), channel_id=1, source_target_pairs={{0,3},{1,2},{2,1},{3,0},{4,7},{5,6},{6,5},{7,4},{8,11},{9,10},{10,... | collective-permute-start | bytes 1179656 | tf_op jit(solution)/shard_map/ppermute | solution.py:38
  151.3 0.7 shard_map.134.refs_9_
  152.4 0.9 collective-permute-done.30.refs_1_
  153.3 2.1 %collective-permute-start.43 = (bf16[480,512]{1,0:T(8,128)(2,1)S(1)}, bf16[480,512]{1,0:T(8,128)(2,1)S(1)}, u32[]{:S(2)}, u32[]{:S(2)}) collective-permute-start(bf16[480,512]{1,0:T(8,128)(2,1)S(1)} %shard_map.134.refs_9_), channel_id=1, source_target_pairs={{0,3},{1,2},{2,1},{3,0},{4,7},{5,6},{6,5},{7,4},{8,11},{9,10},{10,... | collective-permute-start | bytes 1474568 | tf_op jit(solution)/shard_map/ppermute | solution.py:38
  155.6 1.3 collective-permute-start.32
  156.9 13.3 %collective-permute-done.36.refs_3_ = bf16[384,512]{1,0:T(8,128)(2,1)S(1)} collective-permute-done((bf16[384,512]{1,0:T(8,128)(2,1)S(1)}, bf16[384,512]{1,0:T(8,128)(2,1)S(1)}, u32[]{:S(2)}, u32[]{:S(2)}) %collective-permute-start.36) | collective-permute-done | bytes 393248 | tf_op jit(solution)/shard_map/ppermute | solution.py:38
  170.2 2.8 %collective-permute-start.39 = (bf16[240,512]{1,0:T(8,128)(2,1)S(1)}, bf16[240,512]{1,0:T(8,128)(2,1)S(1)}, u32[]{:S(2)}, u32[]{:S(2)}) collective-permute-start(bf16[240,512]{1,0:T(8,128)(2,1)S(1)} %slice.8), channel_id=1, source_target_pairs={{0,3},{1,2},{2,1},{3,0},{4,7},{5,6},{6,5},{7,4},{8,11},{9,10},{10,... | collective-permute-start | bytes 737288 | tf_op jit(solution)/shard_map/ppermute | solution.py:38
  173.0 5.8 %collective-permute-done.32.refs_0_ = bf16[72,1024]{1,0:T(8,128)(2,1)S(1)} collective-permute-done((bf16[72,1024]{1,0:T(8,128)(2,1)S(1)}, bf16[72,1024]{1,0:T(8,128)(2,1)S(1)}, u32[]{:S(2)}, u32[]{:S(2)}) %collective-permute-start.32) | collective-permute-done | bytes 147488 | tf_op jit(solution)/shard_map/ppermute | solution.py:38
  178.8 1.5 collective-permute-start.33
  180.4 3.5 %collective-permute-done.43.refs_12_ = bf16[480,512]{1,0:T(8,128)(2,1)S(1)} collective-permute-done((bf16[480,512]{1,0:T(8,128)(2,1)S(1)}, bf16[480,512]{1,0:T(8,128)(2,1)S(1)}, u32[]{:S(2)}, u32[]{:S(2)}) %collective-permute-start.43) | collective-permute-done | bytes 491552 | tf_op jit(solution)/shard_map/ppermute | solution.py:38
  183.9 5.3 %collective-permute-done.39.refs_7_ = bf16[240,512]{1,0:T(8,128)(2,1)S(1)} collective-permute-done((bf16[240,512]{1,0:T(8,128)(2,1)S(1)}, bf16[240,512]{1,0:T(8,128)(2,1)S(1)}, u32[]{:S(2)}, u32[]{:S(2)}) %collective-permute-start.39) | collective-permute-done | bytes 245792 | tf_op jit(solution)/shard_map/ppermute | solution.py:38
  189.1 4.5 %shard_map.135 = (bf16[512,1792]{1,0:T(8,128)(2,1)}, bf16[512,1792]{1,0:T(8,128)(2,1)}, bf16[1792,512]{1,0:T(8,128)(2,1)}) custom-call(s32[1]{0:T(128)} %bitcast.2.at_ref, bf16[384,512]{1,0:T(8,128)(2,1)S(1)} %shard_map.132.refs_0_, bf16[384,512]{1,0:T(8,128)(2,1)S(1)} %collective-permute-done.34.refs_1_, ...), custom_call_target="tpu_custom_call" | custom-call | tf_op jit(solution)/shard_map/pallas_call | solution.py:98
  193.6 0.9 shard_map.131
  (59 shorter events, 6.7 us)
Async XLA Ops:
  1.4 5.5 %collective-permute-start = (bf16[32,1024]{1,0:T(8,128)(2,1)S(1)}, bf16[32,1024]{1,0:T(8,128)(2,1)S(1)}, u32[]{:S(2)}, u32[]{:S(2)}) collective-permute-start(bf16[32,1024]{1,0:T(8,128)(2,1)S(1)} %shard_map.109.refs_0_), channel_id=1, source_target_pairs={{0,8},{4,12},{8,0},{12,4},{16,24},{20,28},{24,16},{28,20},{1,9},{5... | collective-permute-start | bytes 196616 | tf_op jit(solution)/shard_map/ppermute | solution.py:38
  3.9 5.6 %collective-permute-start.1 = (bf16[32,1024]{1,0:T(8,128)(2,1)S(1)}, bf16[32,1024]{1,0:T(8,128)(2,1)S(1)}, u32[]{:S(2)}, u32[]{:S(2)}) collective-permute-start(bf16[32,1024]{1,0:T(8,128)(2,1)S(1)} %shard_map.109.refs_0_), channel_id=1, source_target_pairs={{0,16},{4,20},{8,24},{12,28},{16,0},{20,4},{24,8},{28,12},{1,17},{... | collective-permute-start | bytes 196616 | tf_op jit(solution)/shard_map/ppermute | solution.py:38
  6.9 4.9 %collective-permute-start.2 = (bf16[32,1024]{1,0:T(8,128)(2,1)S(1)}, bf16[32,1024]{1,0:T(8,128)(2,1)S(1)}, u32[]{:S(2)}, u32[]{:S(2)}) collective-permute-start(bf16[32,1024]{1,0:T(8,128)(2,1)S(1)} %shard_map.109.refs_0_), channel_id=1, source_target_pairs={{0,24},{4,28},{8,16},{12,20},{16,8},{20,12},{24,0},{28,4},{1,25},{... | collective-permute-start | bytes 196616 | tf_op jit(solution)/shard_map/ppermute | solution.py:38
  11.8 5.3 %collective-permute-start.3 = (bf16[128,1024]{1,0:T(8,128)(2,1)S(1)}, bf16[128,1024]{1,0:T(8,128)(2,1)S(1)}, u32[]{:S(2)}, u32[]{:S(2)}) collective-permute-start(bf16[128,1024]{1,0:T(8,128)(2,1)S(1)} %shard_map.110.refs_0_), channel_id=1, source_target_pairs={{0,1},{1,0},{2,3},{3,2},{4,5},{5,4},{6,7},{7,6},{8,9},{9,8},{10,11... | collective-permute-start | bytes 786440 | tf_op jit(solution)/shard_map/ppermute | solution.py:38
  13.3 12.3 %collective-permute-start.4 = (bf16[128,1024]{1,0:T(8,128)(2,1)S(1)}, bf16[128,1024]{1,0:T(8,128)(2,1)S(1)}, u32[]{:S(2)}, u32[]{:S(2)}) collective-permute-start(bf16[128,1024]{1,0:T(8,128)(2,1)S(1)} %shard_map.110.refs_0_), channel_id=1, source_target_pairs={{0,2},{1,3},{2,0},{3,1},{4,6},{5,7},{6,4},{7,5},{8,10},{9,11},{10,... | collective-permute-start | bytes 786440 | tf_op jit(solution)/shard_map/ppermute | solution.py:38
  15.9 13.4 %collective-permute-start.5 = (bf16[128,1024]{1,0:T(8,128)(2,1)S(1)}, bf16[128,1024]{1,0:T(8,128)(2,1)S(1)}, u32[]{:S(2)}, u32[]{:S(2)}) collective-permute-start(bf16[128,1024]{1,0:T(8,128)(2,1)S(1)} %shard_map.110.refs_0_), channel_id=1, source_target_pairs={{0,3},{1,2},{2,1},{3,0},{4,7},{5,6},{6,5},{7,4},{8,11},{9,10},{10,... | collective-permute-start | bytes 786440 | tf_op jit(solution)/shard_map/ppermute | solution.py:38
  29.4 4.5 %collective-permute-start.6 = (bf16[512,1024]{1,0:T(8,128)(2,1)S(1)}, bf16[512,1024]{1,0:T(8,128)(2,1)S(1)}, u32[]{:S(2)}, u32[]{:S(2)}) collective-permute-start(bf16[512,1024]{1,0:T(8,128)(2,1)S(1)} %shard_map.111.refs_0_), channel_id=1, source_target_pairs={{0,4},{4,0},{8,12},{12,8},{16,20},{20,16},{24,28},{28,24},{1,5},{5... | collective-permute-start | bytes 3145736 | tf_op jit(solution)/shard_map/ppermute | solution.py:38
  33.2 0.9 copy-start
  34.8 8.8 %collective-permute-start.18 = (bf16[480,256]{1,0:T(8,128)(2,1)S(1)}, bf16[480,256]{1,0:T(8,128)(2,1)S(1)}, u32[]{:S(2)}, u32[]{:S(2)}) collective-permute-start(bf16[480,256]{1,0:T(8,128)(2,1)S(1)} %get-tuple-element.69), channel_id=1, source_target_pairs={{0,128},{32,160},{64,192},{96,224},{128,0},{160,32},{192,64},{224,... | collective-permute-start | bytes 737288 | tf_op jit(solution)/shard_map/ppermute | solution.py:38
  37.6 12.6 %collective-permute-start.19 = (bf16[480,256]{1,0:T(8,128)(2,1)S(1)}, bf16[480,256]{1,0:T(8,128)(2,1)S(1)}, u32[]{:S(2)}, u32[]{:S(2)}) collective-permute-start(bf16[480,256]{1,0:T(8,128)(2,1)S(1)} %get-tuple-element.70), channel_id=1, source_target_pairs={{0,64},{32,96},{64,128},{96,160},{128,192},{160,224},{192,0},{224,... | collective-permute-start | bytes 737288 | tf_op jit(solution)/shard_map/ppermute | solution.py:38
  37.9 12.3 %collective-permute-start.20 = (bf16[480,256]{1,0:T(8,128)(2,1)S(1)}, bf16[480,256]{1,0:T(8,128)(2,1)S(1)}, u32[]{:S(2)}, u32[]{:S(2)}) collective-permute-start(bf16[480,256]{1,0:T(8,128)(2,1)S(1)} %get-tuple-element.71), channel_id=1, source_target_pairs={{0,192},{32,224},{64,0},{96,32},{128,64},{160,96},{192,128},{224,1... | collective-permute-start | bytes 737288 | tf_op jit(solution)/shard_map/ppermute | solution.py:38
  40.7 16.0 %collective-permute-start.11 = (bf16[400,256]{1,0:T(8,128)(2,1)S(1)}, bf16[400,256]{1,0:T(8,128)(2,1)S(1)}, u32[]{:S(2)}, u32[]{:S(2)}) collective-permute-start(bf16[400,256]{1,0:T(8,128)(2,1)S(1)} %shard_map.116), channel_id=1, source_target_pairs={{0,128},{32,160},{64,192},{96,224},{128,0},{160,32},{192,64},{224,... | collective-permute-start | bytes 614408 | tf_op jit(solution)/shard_map/ppermute | solution.py:38
  41.3 18.1 %collective-permute-start.12 = (bf16[400,256]{1,0:T(8,128)(2,1)S(1)}, bf16[400,256]{1,0:T(8,128)(2,1)S(1)}, u32[]{:S(2)}, u32[]{:S(2)}) collective-permute-start(bf16[400,256]{1,0:T(8,128)(2,1)S(1)} %shard_map.117), channel_id=1, source_target_pairs={{0,64},{32,96},{64,128},{96,160},{128,192},{160,224},{192,0},{224,... | collective-permute-start | bytes 614408 | tf_op jit(solution)/shard_map/ppermute | solution.py:38
  43.5 16.4 %collective-permute-start.13 = (bf16[400,256]{1,0:T(8,128)(2,1)S(1)}, bf16[400,256]{1,0:T(8,128)(2,1)S(1)}, u32[]{:S(2)}, u32[]{:S(2)}) collective-permute-start(bf16[400,256]{1,0:T(8,128)(2,1)S(1)} %shard_map.118), channel_id=1, source_target_pairs={{0,192},{32,224},{64,0},{96,32},{128,64},{160,96},{192,128},{224,1... | collective-permute-start | bytes 614408 | tf_op jit(solution)/shard_map/ppermute | solution.py:38
  50.6 29.2 %collective-permute-start.21 = (bf16[480,256]{1,0:T(8,128)(2,1)S(1)}, bf16[480,256]{1,0:T(8,128)(2,1)S(1)}, u32[]{:S(2)}, u32[]{:S(2)}) collective-permute-start(bf16[480,256]{1,0:T(8,128)(2,1)S(1)} %get-tuple-element.73), channel_id=1, source_target_pairs={{0,32},{32,0},{64,96},{96,64},{128,160},{160,128},{192,224},{224,1... | collective-permute-start | bytes 737288 | tf_op jit(solution)/shard_map/ppermute | solution.py:38
  56.0 24.0 %collective-permute-start.7 = (bf16[480,256]{1,0:T(8,128)(2,1)S(1)}, bf16[480,256]{1,0:T(8,128)(2,1)S(1)}, u32[]{:S(2)}, u32[]{:S(2)}) collective-permute-start(bf16[480,256]{1,0:T(8,128)(2,1)S(1)} %get-tuple-element.57), channel_id=1, source_target_pairs={{0,128},{32,160},{64,192},{96,224},{128,0},{160,32},{192,64},{224,... | collective-permute-start | bytes 737288 | tf_op jit(solution)/shard_map/ppermute | solution.py:38
  56.8 23.3 %collective-permute-start.8 = (bf16[480,256]{1,0:T(8,128)(2,1)S(1)}, bf16[480,256]{1,0:T(8,128)(2,1)S(1)}, u32[]{:S(2)}, u32[]{:S(2)}) collective-permute-start(bf16[480,256]{1,0:T(8,128)(2,1)S(1)} %get-tuple-element.58), channel_id=1, source_target_pairs={{0,64},{32,96},{64,128},{96,160},{128,192},{160,224},{192,0},{224,... | collective-permute-start | bytes 737288 | tf_op jit(solution)/shard_map/ppermute | solution.py:38
  59.4 20.7 %collective-permute-start.9 = (bf16[480,256]{1,0:T(8,128)(2,1)S(1)}, bf16[480,256]{1,0:T(8,128)(2,1)S(1)}, u32[]{:S(2)}, u32[]{:S(2)}) collective-permute-start(bf16[480,256]{1,0:T(8,128)(2,1)S(1)} %get-tuple-element.59), channel_id=1, source_target_pairs={{0,192},{32,224},{64,0},{96,32},{128,64},{160,96},{192,128},{224,1... | collective-permute-start | bytes 737288 | tf_op jit(solution)/shard_map/ppermute | solution.py:38
  60.5 19.1 %collective-permute-start.14 = (bf16[400,256]{1,0:T(8,128)(2,1)S(1)}, bf16[400,256]{1,0:T(8,128)(2,1)S(1)}, u32[]{:S(2)}, u32[]{:S(2)}) collective-permute-start(bf16[400,256]{1,0:T(8,128)(2,1)S(1)} %get-tuple-element.65), channel_id=1, source_target_pairs={{0,32},{32,0},{64,96},{96,64},{128,160},{160,128},{192,224},{224,1... | collective-permute-start | bytes 614408 | tf_op jit(solution)/shard_map/ppermute | solution.py:38
  79.9 22.2 %collective-permute-start.22 = (bf16[496,256]{1,0:T(8,128)(2,1)S(1)}, bf16[496,256]{1,0:T(8,128)(2,1)S(1)}, u32[]{:S(2)}, u32[]{:S(2)}) collective-permute-start(bf16[496,256]{1,0:T(8,128)(2,1)S(1)} %shard_map.124.a_ref.refs_0_), channel_id=1, source_target_pairs={{0,128},{32,160},{64,192},{96,224},{128,0},{160,32},{192,64},{224,... | collective-permute-start | bytes 761864 | tf_op jit(solution)/shard_map/ppermute | solution.py:38
  80.5 14.1 %collective-permute-start.10 = (bf16[480,256]{1,0:T(8,128)(2,1)S(1)}, bf16[480,256]{1,0:T(8,128)(2,1)S(1)}, u32[]{:S(2)}, u32[]{:S(2)}) collective-permute-start(bf16[480,256]{1,0:T(8,128)(2,1)S(1)} %get-tuple-element.61), channel_id=1, source_target_pairs={{0,32},{32,0},{64,96},{96,64},{128,160},{160,128},{192,224},{224,1... | collective-permute-start | bytes 737288 | tf_op jit(solution)/shard_map/ppermute | solution.py:38
  82.1 15.2 %collective-permute-start.25 = (bf16[416,256]{1,0:T(8,128)(2,1)S(1)}, bf16[416,256]{1,0:T(8,128)(2,1)S(1)}, u32[]{:S(2)}, u32[]{:S(2)}) collective-permute-start(bf16[416,256]{1,0:T(8,128)(2,1)S(1)} %get-tuple-element.74.a_ref.refs_0_), channel_id=1, source_target_pairs={{0,128},{32,160},{64,192},{96,224},{128,0},{160,32},{192,64},{224,... | collective-permute-start | bytes 638984 | tf_op jit(solution)/shard_map/ppermute | solution.py:38
  85.1 15.0 %collective-permute-start.26 = (bf16[416,256]{1,0:T(8,128)(2,1)S(1)}, bf16[416,256]{1,0:T(8,128)(2,1)S(1)}, u32[]{:S(2)}, u32[]{:S(2)}) collective-permute-start(bf16[416,256]{1,0:T(8,128)(2,1)S(1)} %get-tuple-element.74.a_ref.refs_0_), channel_id=1, source_target_pairs={{0,64},{32,96},{64,128},{96,160},{128,192},{160,224},{192,0},{224,... | collective-permute-start | bytes 638984 | tf_op jit(solution)/shard_map/ppermute | solution.py:38
  86.2 15.1 %collective-permute-start.27 = (bf16[416,256]{1,0:T(8,128)(2,1)S(1)}, bf16[416,256]{1,0:T(8,128)(2,1)S(1)}, u32[]{:S(2)}, u32[]{:S(2)}) collective-permute-start(bf16[416,256]{1,0:T(8,128)(2,1)S(1)} %get-tuple-element.74.a_ref.refs_0_), channel_id=1, source_target_pairs={{0,192},{32,224},{64,0},{96,32},{128,64},{160,96},{192,128},{224,1... | collective-permute-start | bytes 638984 | tf_op jit(solution)/shard_map/ppermute | solution.py:38
  94.6 11.3 %collective-permute-start.23 = (bf16[496,256]{1,0:T(8,128)(2,1)S(1)}, bf16[496,256]{1,0:T(8,128)(2,1)S(1)}, u32[]{:S(2)}, u32[]{:S(2)}) collective-permute-start(bf16[496,256]{1,0:T(8,128)(2,1)S(1)} %shard_map.124.a_ref.refs_0_), channel_id=1, source_target_pairs={{0,64},{32,96},{64,128},{96,160},{128,192},{160,224},{192,0},{224,... | collective-permute-start | bytes 761864 | tf_op jit(solution)/shard_map/ppermute | solution.py:38
  97.3 9.9 %collective-permute-start.24 = (bf16[496,256]{1,0:T(8,128)(2,1)S(1)}, bf16[496,256]{1,0:T(8,128)(2,1)S(1)}, u32[]{:S(2)}, u32[]{:S(2)}) collective-permute-start(bf16[496,256]{1,0:T(8,128)(2,1)S(1)} %shard_map.124.a_ref.refs_0_), channel_id=1, source_target_pairs={{0,192},{32,224},{64,0},{96,32},{128,64},{160,96},{192,128},{224,1... | collective-permute-start | bytes 761864 | tf_op jit(solution)/shard_map/ppermute | solution.py:38
  100.1 12.1 %collective-permute-start.15 = (bf16[496,256]{1,0:T(8,128)(2,1)S(1)}, bf16[496,256]{1,0:T(8,128)(2,1)S(1)}, u32[]{:S(2)}, u32[]{:S(2)}) collective-permute-start(bf16[496,256]{1,0:T(8,128)(2,1)S(1)} %shard_map.121.a_ref.refs_0_), channel_id=1, source_target_pairs={{0,128},{32,160},{64,192},{96,224},{128,0},{160,32},{192,64},{224,... | collective-permute-start | bytes 761864 | tf_op jit(solution)/shard_map/ppermute | solution.py:38
  101.4 15.3 %collective-permute-start.16 = (bf16[496,256]{1,0:T(8,128)(2,1)S(1)}, bf16[496,256]{1,0:T(8,128)(2,1)S(1)}, u32[]{:S(2)}, u32[]{:S(2)}) collective-permute-start(bf16[496,256]{1,0:T(8,128)(2,1)S(1)} %shard_map.121.a_ref.refs_0_), channel_id=1, source_target_pairs={{0,64},{32,96},{64,128},{96,160},{128,192},{160,224},{192,0},{224,... | collective-permute-start | bytes 761864 | tf_op jit(solution)/shard_map/ppermute | solution.py:38
  102.1 14.6 %collective-permute-start.17 = (bf16[496,256]{1,0:T(8,128)(2,1)S(1)}, bf16[496,256]{1,0:T(8,128)(2,1)S(1)}, u32[]{:S(2)}, u32[]{:S(2)}) collective-permute-start(bf16[496,256]{1,0:T(8,128)(2,1)S(1)} %shard_map.121.a_ref.refs_0_), channel_id=1, source_target_pairs={{0,192},{32,224},{64,0},{96,32},{128,64},{160,96},{192,128},{224,1... | collective-permute-start | bytes 761864 | tf_op jit(solution)/shard_map/ppermute | solution.py:38
  118.0 6.0 %collective-permute-start.28 = (bf16[520,1024]{1,0:T(8,128)(2,1)S(1)}, bf16[520,1024]{1,0:T(8,128)(2,1)S(1)}, u32[]{:S(2)}, u32[]{:S(2)}) collective-permute-start(bf16[520,1024]{1,0:T(8,128)(2,1)S(1)} %get-tuple-element.82), channel_id=1, source_target_pairs={{0,4},{4,0},{8,12},{12,8},{16,20},{20,16},{24,28},{28,24},{1,5},{5... | collective-permute-start | bytes 3194888 | tf_op jit(solution)/shard_map/ppermute | solution.py:38
  119.8 12.3 %collective-permute-start.34 = (bf16[384,512]{1,0:T(8,128)(2,1)S(1)}, bf16[384,512]{1,0:T(8,128)(2,1)S(1)}, u32[]{:S(2)}, u32[]{:S(2)}) collective-permute-start(bf16[384,512]{1,0:T(8,128)(2,1)S(1)} %shard_map.132.refs_0_), channel_id=1, source_target_pairs={{0,2},{1,3},{2,0},{3,1},{4,6},{5,7},{6,4},{7,5},{8,10},{9,11},{10,... | collective-permute-start | bytes 1179656 | tf_op jit(solution)/shard_map/ppermute | solution.py:38
  119.9 18.2 %collective-permute-start.35 = (bf16[384,512]{1,0:T(8,128)(2,1)S(1)}, bf16[384,512]{1,0:T(8,128)(2,1)S(1)}, u32[]{:S(2)}, u32[]{:S(2)}) collective-permute-start(bf16[384,512]{1,0:T(8,128)(2,1)S(1)} %shard_map.132.refs_0_), channel_id=1, source_target_pairs={{0,1},{1,0},{2,3},{3,2},{4,5},{5,4},{6,7},{7,6},{8,9},{9,8},{10,11... | collective-permute-start | bytes 1179656 | tf_op jit(solution)/shard_map/ppermute | solution.py:38
  121.2 27.5 %collective-permute-start.37 = (bf16[480,512]{1,0:T(8,128)(2,1)S(1)}, bf16[480,512]{1,0:T(8,128)(2,1)S(1)}, u32[]{:S(2)}, u32[]{:S(2)}) collective-permute-start(bf16[480,512]{1,0:T(8,128)(2,1)S(1)} %shard_map.133.refs_4_), channel_id=1, source_target_pairs={{0,1},{1,0},{2,3},{3,2},{4,5},{5,4},{6,7},{7,6},{8,9},{9,8},{10,11... | collective-permute-start | bytes 1474568 | tf_op jit(solution)/shard_map/ppermute | solution.py:38
  122.2 33.3 %collective-permute-start.38 = (bf16[480,512]{1,0:T(8,128)(2,1)S(1)}, bf16[480,512]{1,0:T(8,128)(2,1)S(1)}, u32[]{:S(2)}, u32[]{:S(2)}) collective-permute-start(bf16[480,512]{1,0:T(8,128)(2,1)S(1)} %shard_map.133.refs_4_), channel_id=1, source_target_pairs={{0,3},{1,2},{2,1},{3,0},{4,7},{5,6},{6,5},{7,4},{8,11},{9,10},{10,... | collective-permute-start | bytes 1474568 | tf_op jit(solution)/shard_map/ppermute | solution.py:38
  124.2 27.8 %collective-permute-start.29 = (bf16[136,1024]{1,0:T(8,128)(2,1)S(1)}, bf16[136,1024]{1,0:T(8,128)(2,1)S(1)}, u32[]{:S(2)}, u32[]{:S(2)}) collective-permute-start(bf16[136,1024]{1,0:T(8,128)(2,1)S(1)} %get-tuple-element.86), channel_id=1, source_target_pairs={{0,8},{4,12},{8,0},{12,4},{16,24},{20,28},{24,16},{28,20},{1,9},{5... | collective-permute-start | bytes 835592 | tf_op jit(solution)/shard_map/ppermute | solution.py:38
  132.1 21.2 %collective-permute-start.30 = (bf16[136,1024]{1,0:T(8,128)(2,1)S(1)}, bf16[136,1024]{1,0:T(8,128)(2,1)S(1)}, u32[]{:S(2)}, u32[]{:S(2)}) collective-permute-start(bf16[136,1024]{1,0:T(8,128)(2,1)S(1)} %get-tuple-element.87), channel_id=1, source_target_pairs={{0,16},{4,20},{8,24},{12,28},{16,0},{20,4},{24,8},{28,12},{1,17},{... | collective-permute-start | bytes 835592 | tf_op jit(solution)/shard_map/ppermute | solution.py:38
  138.1 15.2 %collective-permute-start.31 = (bf16[136,1024]{1,0:T(8,128)(2,1)S(1)}, bf16[136,1024]{1,0:T(8,128)(2,1)S(1)}, u32[]{:S(2)}, u32[]{:S(2)}) collective-permute-start(bf16[136,1024]{1,0:T(8,128)(2,1)S(1)} %get-tuple-element.88), channel_id=1, source_target_pairs={{0,24},{4,28},{8,16},{12,20},{16,8},{20,12},{24,0},{28,4},{1,25},{... | collective-permute-start | bytes 835592 | tf_op jit(solution)/shard_map/ppermute | solution.py:38
  148.6 21.5 %collective-permute-start.36 = (bf16[384,512]{1,0:T(8,128)(2,1)S(1)}, bf16[384,512]{1,0:T(8,128)(2,1)S(1)}, u32[]{:S(2)}, u32[]{:S(2)}) collective-permute-start(bf16[384,512]{1,0:T(8,128)(2,1)S(1)} %shard_map.132.refs_0_), channel_id=1, source_target_pairs={{0,3},{1,2},{2,1},{3,0},{4,7},{5,6},{6,5},{7,4},{8,11},{9,10},{10,... | collective-permute-start | bytes 1179656 | tf_op jit(solution)/shard_map/ppermute | solution.py:38
  152.0 26.7 %collective-permute-start.41 = (bf16[480,512]{1,0:T(8,128)(2,1)S(1)}, bf16[480,512]{1,0:T(8,128)(2,1)S(1)}, u32[]{:S(2)}, u32[]{:S(2)}) collective-permute-start(bf16[480,512]{1,0:T(8,128)(2,1)S(1)} %shard_map.134.refs_9_), channel_id=1, source_target_pairs={{0,2},{1,3},{2,0},{3,1},{4,6},{5,7},{6,4},{7,5},{8,10},{9,11},{10,... | collective-permute-start | bytes 1474568 | tf_op jit(solution)/shard_map/ppermute | solution.py:38
  153.3 27.1 %collective-permute-start.42 = (bf16[480,512]{1,0:T(8,128)(2,1)S(1)}, bf16[480,512]{1,0:T(8,128)(2,1)S(1)}, u32[]{:S(2)}, u32[]{:S(2)}) collective-permute-start(bf16[480,512]{1,0:T(8,128)(2,1)S(1)} %shard_map.134.refs_9_), channel_id=1, source_target_pairs={{0,1},{1,0},{2,3},{3,2},{4,5},{5,4},{6,7},{7,6},{8,9},{9,8},{10,11... | collective-permute-start | bytes 1474568 | tf_op jit(solution)/shard_map/ppermute | solution.py:38
  153.3 30.6 %collective-permute-start.43 = (bf16[480,512]{1,0:T(8,128)(2,1)S(1)}, bf16[480,512]{1,0:T(8,128)(2,1)S(1)}, u32[]{:S(2)}, u32[]{:S(2)}) collective-permute-start(bf16[480,512]{1,0:T(8,128)(2,1)S(1)} %shard_map.134.refs_9_), channel_id=1, source_target_pairs={{0,3},{1,2},{2,1},{3,0},{4,7},{5,6},{6,5},{7,4},{8,11},{9,10},{10,... | collective-permute-start | bytes 1474568 | tf_op jit(solution)/shard_map/ppermute | solution.py:38
  155.6 23.2 %collective-permute-start.32 = (bf16[72,1024]{1,0:T(8,128)(2,1)S(1)}, bf16[72,1024]{1,0:T(8,128)(2,1)S(1)}, u32[]{:S(2)}, u32[]{:S(2)}) collective-permute-start(bf16[72,1024]{1,0:T(8,128)(2,1)S(1)} %get-tuple-element.92), channel_id=1, source_target_pairs={{0,2},{1,3},{2,0},{3,1},{4,6},{5,7},{6,4},{7,5},{8,10},{9,11},{10,... | collective-permute-start | bytes 442376 | tf_op jit(solution)/shard_map/ppermute | solution.py:38
  170.2 19.0 %collective-permute-start.39 = (bf16[240,512]{1,0:T(8,128)(2,1)S(1)}, bf16[240,512]{1,0:T(8,128)(2,1)S(1)}, u32[]{:S(2)}, u32[]{:S(2)}) collective-permute-start(bf16[240,512]{1,0:T(8,128)(2,1)S(1)} %slice.8), channel_id=1, source_target_pairs={{0,3},{1,2},{2,1},{3,0},{4,7},{5,6},{6,5},{7,4},{8,11},{9,10},{10,... | collective-permute-start | bytes 737288 | tf_op jit(solution)/shard_map/ppermute | solution.py:38
  178.7 10.4 %collective-permute-start.40 = (bf16[240,512]{1,0:T(8,128)(2,1)S(1)}, bf16[240,512]{1,0:T(8,128)(2,1)S(1)}, u32[]{:S(2)}, u32[]{:S(2)}) collective-permute-start(bf16[240,512]{1,0:T(8,128)(2,1)S(1)} %slice.9), channel_id=1, source_target_pairs={{0,1},{1,0},{2,3},{3,2},{4,5},{5,4},{6,7},{7,6},{8,9},{9,8},{10,11... | collective-permute-start | bytes 737288 | tf_op jit(solution)/shard_map/ppermute | solution.py:38
  178.8 14.8 %copy-start.1 = (bf16[32,512]{1,0:T(8,128)(2,1)S(1)}, bf16[32,512]{1,0:T(8,128)(2,1)}, u32[]{:S(2)}) copy-start(bf16[32,512]{1,0:T(8,128)(2,1)} %tok_ref.3) | copy-start | bytes 98308
  178.8 14.8 %copy-start.2 = (bf16[32,512]{1,0:T(8,128)(2,1)S(1)}, bf16[32,512]{1,0:T(8,128)(2,1)}, u32[]{:S(2)}) copy-start(bf16[32,512]{1,0:T(8,128)(2,1)} %cot_ref.3) | copy-start | bytes 98308
  178.8 14.8 %collective-permute-start.33 = (bf16[40,1024]{1,0:T(8,128)(2,1)S(1)}, bf16[40,1024]{1,0:T(8,128)(2,1)S(1)}, u32[]{:S(2)}, u32[]{:S(2)}) collective-permute-start(bf16[40,1024]{1,0:T(8,128)(2,1)S(1)} %get-tuple-element.97), channel_id=1, source_target_pairs={{0,1},{1,0},{2,3},{3,2},{4,5},{5,4},{6,7},{7,6},{8,9},{9,8},{10,11... | collective-permute-start | bytes 245768 | tf_op jit(solution)/shard_map/ppermute | solution.py:38

commit v6 on v5

--- a/solution.py
+++ b/solution.py
@@ -9,7 +9,7 @@
 D = 4096
 EPS = 1e-05
 FS = 448
-CHUNKS = ((0, 128), (128, 160), (288, 160))
+CHUNKS = ((0, 128), (128, 192), (320, 128))
 
 
 BF = jnp.bfloat16
@@ -509,11 +509,12 @@
     own, gain_part, inner, message = back(2, before)
     message = send_core(message)
     groups.append(weight_grad((2,)))
+    spread(groups[2], (1, 3))
     strips = [[(128 * a + 32 * j, 32) for a in range(4)] for j in range(4)]
     own, gain_part, inner, *messages = fold_call(own, gain_part, inner, [message], [None], strips)
     messages = [send_zl(m, k) for k, m in zip((1, 2, 3), messages)]
     relay(groups[1])
-    spread(groups[2], (2, 1, 3))
+    spread(groups[2], (2,))
     turns = [lambda v, lanes=lanes: turn_left(v, lanes) for lanes in (32, 64, 96)]
     own, gain_part, inner, *messages = fold_call(
         own, gain_part, inner, messages, turns, [[(0, 64)], [(64, 64)]])

time: 195 us -> 189 us (0.969)
  waiting for transfers between devices: 108 us -> 95.4 us
  starting transfers between devices: 67.6 us -> 74.4 us
    ppermute x44, waiting for transfers between devices: 108 us -> 95.4 us  [send(): return lax.ppermute(v, axis, perm)]
    ppermute x44, starting transfers between devices: 67.6 us -> 74.4 us  [send(): return lax.ppermute(v, axis, perm)]
  transfers between devices with their start and end apart: 44 -> 44, of which waited for: 22 -> 25; matrix products, arithmetic and copies ran while one was open for 0% -> 0% of each run, Pallas kernels for 7% -> 7%
where the time goes in v6:
time: 189 us
  waiting for transfers between devices  95.4 us (50%)
  starting transfers between devices  74.4 us (39%)
  Pallas kernels  17.8 us (9%)
    ppermute x44, waiting for transfers between devices, send(): return lax.ppermute(v, axis, perm)  95.4 us
    ppermute x44, starting transfers between devices, send(): return lax.ppermute(v, axis, perm)  74.4 us
    pallas_call x27, Pallas kernels, call(): return run(*scalars, *placed)  17.8 us
  transfers between devices with their start and end apart: 44, of which 25 were waited for; matrix products, arithmetic and copies ran while one was open for 0% of the time, Pallas kernels for 7%

profile of v6, /device:TPU:1, one launch (start us, length us, event | category | flops | bytes accessed | tf_op | source)
XLA Modules:
  0.0 188.6 jit_solution(13345596732771626664)
XLA Ops:
  0.6 0.8 shard_map.109.refs_0_
  1.4 2.5 %collective-permute-start = (bf16[32,1024]{1,0:T(8,128)(2,1)S(1)}, bf16[32,1024]{1,0:T(8,128)(2,1)S(1)}, u32[]{:S(2)}, u32[]{:S(2)}) collective-permute-start(bf16[32,1024]{1,0:T(8,128)(2,1)S(1)} %shard_map.109.refs_0_), channel_id=1, source_target_pairs={{0,8},{4,12},{8,0},{12,4},{16,24},{20,28},{24,16},{28,20},{1,9},{5... | collective-permute-start | bytes 196616 | tf_op jit(solution)/shard_map/ppermute | solution.py:38
  3.9 3.0 %collective-permute-start.1 = (bf16[32,1024]{1,0:T(8,128)(2,1)S(1)}, bf16[32,1024]{1,0:T(8,128)(2,1)S(1)}, u32[]{:S(2)}, u32[]{:S(2)}) collective-permute-start(bf16[32,1024]{1,0:T(8,128)(2,1)S(1)} %shard_map.109.refs_0_), channel_id=1, source_target_pairs={{0,16},{4,20},{8,24},{12,28},{16,0},{20,4},{24,8},{28,12},{1,17},{... | collective-permute-start | bytes 196616 | tf_op jit(solution)/shard_map/ppermute | solution.py:38
  6.9 2.6 %collective-permute-done.1.refs_2_ = bf16[32,1024]{1,0:T(8,128)(2,1)S(1)} collective-permute-done((bf16[32,1024]{1,0:T(8,128)(2,1)S(1)}, bf16[32,1024]{1,0:T(8,128)(2,1)S(1)}, u32[]{:S(2)}, u32[]{:S(2)}) %collective-permute-start.1) | collective-permute-done | bytes 65568 | tf_op jit(solution)/shard_map/ppermute | solution.py:38
  9.5 2.3 %collective-permute-done.2.refs_3_ = bf16[32,1024]{1,0:T(8,128)(2,1)S(1)} collective-permute-done((bf16[32,1024]{1,0:T(8,128)(2,1)S(1)}, bf16[32,1024]{1,0:T(8,128)(2,1)S(1)}, u32[]{:S(2)}, u32[]{:S(2)}) %collective-permute-start.2) | collective-permute-done | bytes 65568 | tf_op jit(solution)/shard_map/ppermute | solution.py:38
  11.8 1.5 collective-permute-start.3
  13.3 2.6 %collective-permute-start.4 = (bf16[128,1024]{1,0:T(8,128)(2,1)S(1)}, bf16[128,1024]{1,0:T(8,128)(2,1)S(1)}, u32[]{:S(2)}, u32[]{:S(2)}) collective-permute-start(bf16[128,1024]{1,0:T(8,128)(2,1)S(1)} %shard_map.110.refs_0_), channel_id=1, source_target_pairs={{0,2},{1,3},{2,0},{3,1},{4,6},{5,7},{6,4},{7,5},{8,10},{9,11},{10,... | collective-permute-start | bytes 786440 | tf_op jit(solution)/shard_map/ppermute | solution.py:38
  15.9 1.2 collective-permute-done.3.refs_1_
  17.1 8.5 %collective-permute-done.4.refs_2_ = bf16[128,1024]{1,0:T(8,128)(2,1)S(1)} collective-permute-done((bf16[128,1024]{1,0:T(8,128)(2,1)S(1)}, bf16[128,1024]{1,0:T(8,128)(2,1)S(1)}, u32[]{:S(2)}, u32[]{:S(2)}) %collective-permute-start.4) | collective-permute-done | bytes 262176 | tf_op jit(solution)/shard_map/ppermute | solution.py:38
  25.6 3.7 %collective-permute-done.5.refs_3_ = bf16[128,1024]{1,0:T(8,128)(2,1)S(1)} collective-permute-done((bf16[128,1024]{1,0:T(8,128)(2,1)S(1)}, bf16[128,1024]{1,0:T(8,128)(2,1)S(1)}, u32[]{:S(2)}, u32[]{:S(2)}) %collective-permute-start.5) | collective-permute-done | bytes 262176 | tf_op jit(solution)/shard_map/ppermute | solution.py:38
  29.4 2.2 %collective-permute-start.6 = (bf16[512,1024]{1,0:T(8,128)(2,1)S(1)}, bf16[512,1024]{1,0:T(8,128)(2,1)S(1)}, u32[]{:S(2)}, u32[]{:S(2)}) collective-permute-start(bf16[512,1024]{1,0:T(8,128)(2,1)S(1)} %shard_map.111.refs_0_), channel_id=1, source_target_pairs={{0,4},{4,0},{8,12},{12,8},{16,20},{20,16},{24,28},{28,24},{1,5},{5... | collective-permute-start | bytes 3145736 | tf_op jit(solution)/shard_map/ppermute | solution.py:38
  31.6 1.6 shard_map.113
  33.2 0.7 collective-permute-done.6.refs_1_
  34.0 0.8 shard_map.122
  34.8 2.8 %collective-permute-start.18 = (bf16[576,256]{1,0:T(8,128)(2,1)S(1)}, bf16[576,256]{1,0:T(8,128)(2,1)S(1)}, u32[]{:S(2)}, u32[]{:S(2)}) collective-permute-start(bf16[576,256]{1,0:T(8,128)(2,1)S(1)} %get-tuple-element.69), channel_id=1, source_target_pairs={{0,128},{32,160},{64,192},{96,224},{128,0},{160,32},{192,64},{224,... | collective-permute-start | bytes 884744 | tf_op jit(solution)/shard_map/ppermute | solution.py:38
  38.0 2.4 %collective-permute-start.20 = (bf16[576,256]{1,0:T(8,128)(2,1)S(1)}, bf16[576,256]{1,0:T(8,128)(2,1)S(1)}, u32[]{:S(2)}, u32[]{:S(2)}) collective-permute-start(bf16[576,256]{1,0:T(8,128)(2,1)S(1)} %get-tuple-element.71), channel_id=1, source_target_pairs={{0,192},{32,224},{64,0},{96,32},{128,64},{160,96},{192,128},{224,1... | collective-permute-start | bytes 884744 | tf_op jit(solution)/shard_map/ppermute | solution.py:38
  42.3 2.3 %collective-permute-done.18.a_ref = bf16[576,256]{1,0:T(8,128)(2,1)S(1)} collective-permute-done((bf16[576,256]{1,0:T(8,128)(2,1)S(1)}, bf16[576,256]{1,0:T(8,128)(2,1)S(1)}, u32[]{:S(2)}, u32[]{:S(2)}) %collective-permute-start.18) | collective-permute-done | bytes 294944 | tf_op jit(solution)/shard_map/ppermute | solution.py:38
  44.7 2.5 %collective-permute-start.13 = (bf16[400,256]{1,0:T(8,128)(2,1)S(1)}, bf16[400,256]{1,0:T(8,128)(2,1)S(1)}, u32[]{:S(2)}, u32[]{:S(2)}) collective-permute-start(bf16[400,256]{1,0:T(8,128)(2,1)S(1)} %shard_map.118), channel_id=1, source_target_pairs={{0,192},{32,224},{64,0},{96,32},{128,64},{160,96},{192,128},{224,1... | collective-permute-start | bytes 614408 | tf_op jit(solution)/shard_map/ppermute | solution.py:38
  47.1 5.2 %collective-permute-done.19.b_ref = bf16[576,256]{1,0:T(8,128)(2,1)S(1)} collective-permute-done((bf16[576,256]{1,0:T(8,128)(2,1)S(1)}, bf16[576,256]{1,0:T(8,128)(2,1)S(1)}, u32[]{:S(2)}, u32[]{:S(2)}) %collective-permute-start.19) | collective-permute-done | bytes 294944 | tf_op jit(solution)/shard_map/ppermute | solution.py:38
  52.8 4.7 %collective-permute-start.21 = (bf16[576,256]{1,0:T(8,128)(2,1)S(1)}, bf16[576,256]{1,0:T(8,128)(2,1)S(1)}, u32[]{:S(2)}, u32[]{:S(2)}) collective-permute-start(bf16[576,256]{1,0:T(8,128)(2,1)S(1)} %get-tuple-element.73), channel_id=1, source_target_pairs={{0,32},{32,0},{64,96},{96,64},{128,160},{160,128},{192,224},{224,1... | collective-permute-start | bytes 884744 | tf_op jit(solution)/shard_map/ppermute | solution.py:38
  57.5 2.9 %collective-permute-done.12.b_ref = bf16[400,256]{1,0:T(8,128)(2,1)S(1)} collective-permute-done((bf16[400,256]{1,0:T(8,128)(2,1)S(1)}, bf16[400,256]{1,0:T(8,128)(2,1)S(1)}, u32[]{:S(2)}, u32[]{:S(2)}) %collective-permute-start.12) | collective-permute-done | bytes 204832 | tf_op jit(solution)/shard_map/ppermute | solution.py:38
  61.0 4.9 %collective-permute-start.14 = (bf16[400,256]{1,0:T(8,128)(2,1)S(1)}, bf16[400,256]{1,0:T(8,128)(2,1)S(1)}, u32[]{:S(2)}, u32[]{:S(2)}) collective-permute-start(bf16[400,256]{1,0:T(8,128)(2,1)S(1)} %get-tuple-element.65), channel_id=1, source_target_pairs={{0,32},{32,0},{64,96},{96,64},{128,160},{160,128},{192,224},{224,1... | collective-permute-start | bytes 614408 | tf_op jit(solution)/shard_map/ppermute | solution.py:38
  65.9 0.6 shard_map.114
  66.5 1.2 collective-permute-start.7
  67.8 1.9 %collective-permute-start.8 = (bf16[384,256]{1,0:T(8,128)(2,1)S(1)}, bf16[384,256]{1,0:T(8,128)(2,1)S(1)}, u32[]{:S(2)}, u32[]{:S(2)}) collective-permute-start(bf16[384,256]{1,0:T(8,128)(2,1)S(1)} %get-tuple-element.58), channel_id=1, source_target_pairs={{0,64},{32,96},{64,128},{96,160},{128,192},{160,224},{192,0},{224,... | collective-permute-start | bytes 589832 | tf_op jit(solution)/shard_map/ppermute | solution.py:38
  69.7 0.8 collective-permute-start.9
  70.4 2.8 %collective-permute-done.14.other_ref = bf16[400,256]{1,0:T(8,128)(2,1)S(1)} collective-permute-done((bf16[400,256]{1,0:T(8,128)(2,1)S(1)}, bf16[400,256]{1,0:T(8,128)(2,1)S(1)}, u32[]{:S(2)}, u32[]{:S(2)}) %collective-permute-start.14) | collective-permute-done | bytes 204832 | tf_op jit(solution)/shard_map/ppermute | solution.py:38
  73.4 2.4 %collective-permute-start.25 = (bf16[416,256]{1,0:T(8,128)(2,1)S(1)}, bf16[416,256]{1,0:T(8,128)(2,1)S(1)}, u32[]{:S(2)}, u32[]{:S(2)}) collective-permute-start(bf16[416,256]{1,0:T(8,128)(2,1)S(1)} %get-tuple-element.74.a_ref.refs_0_), channel_id=1, source_target_pairs={{0,128},{32,160},{64,192},{96,224},{128,0},{160,32},{192,64},{224,... | collective-permute-start | bytes 638984 | tf_op jit(solution)/shard_map/ppermute | solution.py:38
  76.0 0.7 collective-permute-start.22
  76.8 3.5 %collective-permute-done.8.b_ref = bf16[384,256]{1,0:T(8,128)(2,1)S(1)} collective-permute-done((bf16[384,256]{1,0:T(8,128)(2,1)S(1)}, bf16[384,256]{1,0:T(8,128)(2,1)S(1)}, u32[]{:S(2)}, u32[]{:S(2)}) %collective-permute-start.8) | collective-permute-done | bytes 196640 | tf_op jit(solution)/shard_map/ppermute | solution.py:38
  80.6 2.5 %collective-permute-start.10 = (bf16[384,256]{1,0:T(8,128)(2,1)S(1)}, bf16[384,256]{1,0:T(8,128)(2,1)S(1)}, u32[]{:S(2)}, u32[]{:S(2)}) collective-permute-start(bf16[384,256]{1,0:T(8,128)(2,1)S(1)} %get-tuple-element.61), channel_id=1, source_target_pairs={{0,32},{32,0},{64,96},{96,64},{128,160},{160,128},{192,224},{224,1... | collective-permute-start | bytes 589832 | tf_op jit(solution)/shard_map/ppermute | solution.py:38
  83.2 1.2 collective-permute-start.26
  84.4 1.4 collective-permute-start.27
  85.8 4.5 %collective-permute-done.10.other_ref = bf16[384,256]{1,0:T(8,128)(2,1)S(1)} collective-permute-done((bf16[384,256]{1,0:T(8,128)(2,1)S(1)}, bf16[384,256]{1,0:T(8,128)(2,1)S(1)}, u32[]{:S(2)}, u32[]{:S(2)}) %collective-permute-start.10) | collective-permute-done | bytes 196640 | tf_op jit(solution)/shard_map/ppermute | solution.py:38
  90.3 1.5 collective-permute-start.23
  91.8 1.2 collective-permute-start.24
  93.2 1.5 collective-permute-done.26.c_ref.refs_2_
  94.6 1.2 collective-permute-start.15
  96.0 2.5 %collective-permute-start.17 = (bf16[400,256]{1,0:T(8,128)(2,1)S(1)}, bf16[400,256]{1,0:T(8,128)(2,1)S(1)}, u32[]{:S(2)}, u32[]{:S(2)}) collective-permute-start(bf16[400,256]{1,0:T(8,128)(2,1)S(1)} %shard_map.121.a_ref.refs_0_), channel_id=1, source_target_pairs={{0,192},{32,224},{64,0},{96,32},{128,64},{160,96},{192,128},{224,1... | collective-permute-start | bytes 614408 | tf_op jit(solution)/shard_map/ppermute | solution.py:38
  98.5 0.7 shard_map.125
  99.2 1.0 collective-permute-done.23.c_ref.refs_2_
  100.3 1.1 shard_map.126
  101.3 2.6 %collective-permute-done.15.b_ref.refs_1_ = bf16[400,256]{1,0:T(8,128)(2,1)S(1)} collective-permute-done((bf16[400,256]{1,0:T(8,128)(2,1)S(1)}, bf16[400,256]{1,0:T(8,128)(2,1)S(1)}, u32[]{:S(2)}, u32[]{:S(2)}) %collective-permute-start.15) | collective-permute-done | bytes 204832 | tf_op jit(solution)/shard_map/ppermute | solution.py:38
  104.0 4.7 %collective-permute-done.16.c_ref.refs_2_ = bf16[400,256]{1,0:T(8,128)(2,1)S(1)} collective-permute-done((bf16[400,256]{1,0:T(8,128)(2,1)S(1)}, bf16[400,256]{1,0:T(8,128)(2,1)S(1)}, u32[]{:S(2)}, u32[]{:S(2)}) %collective-permute-start.16) | collective-permute-done | bytes 204832 | tf_op jit(solution)/shard_map/ppermute | solution.py:38
  108.7 1.1 shard_map.127
  109.8 2.1 %collective-permute-start.28 = (bf16[520,1024]{1,0:T(8,128)(2,1)S(1)}, bf16[520,1024]{1,0:T(8,128)(2,1)S(1)}, u32[]{:S(2)}, u32[]{:S(2)}) collective-permute-start(bf16[520,1024]{1,0:T(8,128)(2,1)S(1)} %get-tuple-element.82), channel_id=1, source_target_pairs={{0,4},{4,0},{8,12},{12,8},{16,20},{20,16},{24,28},{28,24},{1,5},{5... | collective-permute-start | bytes 3194888 | tf_op jit(solution)/shard_map/ppermute | solution.py:38
  112.6 1.6 collective-permute-done.28.refs_0_
  114.5 7.5 %collective-permute-start.29 = (bf16[136,1024]{1,0:T(8,128)(2,1)S(1)}, bf16[136,1024]{1,0:T(8,128)(2,1)S(1)}, u32[]{:S(2)}, u32[]{:S(2)}) collective-permute-start(bf16[136,1024]{1,0:T(8,128)(2,1)S(1)} %get-tuple-element.86), channel_id=1, source_target_pairs={{0,8},{4,12},{8,0},{12,4},{16,24},{20,28},{24,16},{28,20},{1,9},{5... | collective-permute-start | bytes 835592 | tf_op jit(solution)/shard_map/ppermute | solution.py:38
  122.0 0.8 shard_map.133.refs_4_
  123.2 2.5 %collective-permute-start.42 = (bf16[384,512]{1,0:T(8,128)(2,1)S(1)}, bf16[384,512]{1,0:T(8,128)(2,1)S(1)}, u32[]{:S(2)}, u32[]{:S(2)}) collective-permute-start(bf16[384,512]{1,0:T(8,128)(2,1)S(1)} %shard_map.134.refs_9_), channel_id=1, source_target_pairs={{0,3},{1,2},{2,1},{3,0},{4,7},{5,6},{6,5},{7,4},{8,11},{9,10},{10,... | collective-permute-start | bytes 1179656 | tf_op jit(solution)/shard_map/ppermute | solution.py:38
  125.7 6.5 %collective-permute-done.29.refs_0_ = bf16[136,1024]{1,0:T(8,128)(2,1)S(1)} collective-permute-done((bf16[136,1024]{1,0:T(8,128)(2,1)S(1)}, bf16[136,1024]{1,0:T(8,128)(2,1)S(1)}, u32[]{:S(2)}, u32[]{:S(2)}) %collective-permute-start.29) | collective-permute-done | bytes 278560 | tf_op jit(solution)/shard_map/ppermute | solution.py:38
  132.2 2.3 %collective-permute-start.31 = (bf16[136,1024]{1,0:T(8,128)(2,1)S(1)}, bf16[136,1024]{1,0:T(8,128)(2,1)S(1)}, u32[]{:S(2)}, u32[]{:S(2)}) collective-permute-start(bf16[136,1024]{1,0:T(8,128)(2,1)S(1)} %get-tuple-element.88), channel_id=1, source_target_pairs={{0,24},{4,28},{8,16},{12,20},{16,8},{20,12},{24,0},{28,4},{1,25},{... | collective-permute-start | bytes 835592 | tf_op jit(solution)/shard_map/ppermute | solution.py:38
  134.5 8.9 %collective-permute-done.30.refs_1_ = bf16[136,1024]{1,0:T(8,128)(2,1)S(1)} collective-permute-done((bf16[136,1024]{1,0:T(8,128)(2,1)S(1)}, bf16[136,1024]{1,0:T(8,128)(2,1)S(1)}, u32[]{:S(2)}, u32[]{:S(2)}) %collective-permute-start.30) | collective-permute-done | bytes 278560 | tf_op jit(solution)/shard_map/ppermute | solution.py:38
  143.4 3.9 %collective-permute-start.43 = (bf16[384,512]{1,0:T(8,128)(2,1)S(1)}, bf16[384,512]{1,0:T(8,128)(2,1)S(1)}, u32[]{:S(2)}, u32[]{:S(2)}) collective-permute-start(bf16[384,512]{1,0:T(8,128)(2,1)S(1)} %shard_map.134.refs_9_), channel_id=1, source_target_pairs={{0,2},{1,3},{2,0},{3,1},{4,6},{5,7},{6,4},{7,5},{8,10},{9,11},{10,... | collective-permute-start | bytes 1179656 | tf_op jit(solution)/shard_map/ppermute | solution.py:38
  148.2 3.0 %collective-permute-start.32 = (bf16[72,1024]{1,0:T(8,128)(2,1)S(1)}, bf16[72,1024]{1,0:T(8,128)(2,1)S(1)}, u32[]{:S(2)}, u32[]{:S(2)}) collective-permute-start(bf16[72,1024]{1,0:T(8,128)(2,1)S(1)} %get-tuple-element.92), channel_id=1, source_target_pairs={{0,2},{1,3},{2,0},{3,1},{4,6},{5,7},{6,4},{7,5},{8,10},{9,11},{10,... | collective-permute-start | bytes 442376 | tf_op jit(solution)/shard_map/ppermute | solution.py:38
  151.7 3.3 %collective-permute-done.43.refs_12_ = bf16[384,512]{1,0:T(8,128)(2,1)S(1)} collective-permute-done((bf16[384,512]{1,0:T(8,128)(2,1)S(1)}, bf16[384,512]{1,0:T(8,128)(2,1)S(1)}, u32[]{:S(2)}, u32[]{:S(2)}) %collective-permute-start.43) | collective-permute-done | bytes 393248 | tf_op jit(solution)/shard_map/ppermute | solution.py:38
  155.0 1.7 collective-permute-start.39
  156.8 9.8 %collective-permute-done.32.refs_0_ = bf16[72,1024]{1,0:T(8,128)(2,1)S(1)} collective-permute-done((bf16[72,1024]{1,0:T(8,128)(2,1)S(1)}, bf16[72,1024]{1,0:T(8,128)(2,1)S(1)}, u32[]{:S(2)}, u32[]{:S(2)}) %collective-permute-start.32) | collective-permute-done | bytes 147488 | tf_op jit(solution)/shard_map/ppermute | solution.py:38
  166.7 1.5 collective-permute-start.33
  168.3 6.8 %collective-permute-done.35.refs_2_ = bf16[384,512]{1,0:T(8,128)(2,1)S(1)} collective-permute-done((bf16[384,512]{1,0:T(8,128)(2,1)S(1)}, bf16[384,512]{1,0:T(8,128)(2,1)S(1)}, u32[]{:S(2)}, u32[]{:S(2)}) %collective-permute-start.35) | collective-permute-done | bytes 393248 | tf_op jit(solution)/shard_map/ppermute | solution.py:38
  175.1 1.9 collective-permute-done.36.refs_3_
  176.9 6.3 %collective-permute-done.39.refs_7_ = bf16[288,512]{1,0:T(8,128)(2,1)S(1)} collective-permute-done((bf16[288,512]{1,0:T(8,128)(2,1)S(1)}, bf16[288,512]{1,0:T(8,128)(2,1)S(1)}, u32[]{:S(2)}, u32[]{:S(2)}) %collective-permute-start.39) | collective-permute-done | bytes 294944 | tf_op jit(solution)/shard_map/ppermute | solution.py:38
  183.2 4.5 %shard_map.135 = (bf16[512,1792]{1,0:T(8,128)(2,1)}, bf16[512,1792]{1,0:T(8,128)(2,1)}, bf16[1792,512]{1,0:T(8,128)(2,1)}) custom-call(s32[1]{0:T(128)} %bitcast.2.at_ref, bf16[384,512]{1,0:T(8,128)(2,1)S(1)} %shard_map.132.refs_0_, bf16[384,512]{1,0:T(8,128)(2,1)S(1)} %collective-permute-done.34.refs_1_, ...), custom_call_target="tpu_custom_call" | custom-call | tf_op jit(solution)/shard_map/pallas_call | solution.py:98
  187.7 0.9 shard_map.131
  (59 shorter events, 7.3 us)
Async XLA Ops:
  1.4 5.5 %collective-permute-start = (bf16[32,1024]{1,0:T(8,128)(2,1)S(1)}, bf16[32,1024]{1,0:T(8,128)(2,1)S(1)}, u32[]{:S(2)}, u32[]{:S(2)}) collective-permute-start(bf16[32,1024]{1,0:T(8,128)(2,1)S(1)} %shard_map.109.refs_0_), channel_id=1, source_target_pairs={{0,8},{4,12},{8,0},{12,4},{16,24},{20,28},{24,16},{28,20},{1,9},{5... | collective-permute-start | bytes 196616 | tf_op jit(solution)/shard_map/ppermute | solution.py:38
  3.9 5.6 %collective-permute-start.1 = (bf16[32,1024]{1,0:T(8,128)(2,1)S(1)}, bf16[32,1024]{1,0:T(8,128)(2,1)S(1)}, u32[]{:S(2)}, u32[]{:S(2)}) collective-permute-start(bf16[32,1024]{1,0:T(8,128)(2,1)S(1)} %shard_map.109.refs_0_), channel_id=1, source_target_pairs={{0,16},{4,20},{8,24},{12,28},{16,0},{20,4},{24,8},{28,12},{1,17},{... | collective-permute-start | bytes 196616 | tf_op jit(solution)/shard_map/ppermute | solution.py:38
  6.9 4.9 %collective-permute-start.2 = (bf16[32,1024]{1,0:T(8,128)(2,1)S(1)}, bf16[32,1024]{1,0:T(8,128)(2,1)S(1)}, u32[]{:S(2)}, u32[]{:S(2)}) collective-permute-start(bf16[32,1024]{1,0:T(8,128)(2,1)S(1)} %shard_map.109.refs_0_), channel_id=1, source_target_pairs={{0,24},{4,28},{8,16},{12,20},{16,8},{20,12},{24,0},{28,4},{1,25},{... | collective-permute-start | bytes 196616 | tf_op jit(solution)/shard_map/ppermute | solution.py:38
  11.8 5.3 %collective-permute-start.3 = (bf16[128,1024]{1,0:T(8,128)(2,1)S(1)}, bf16[128,1024]{1,0:T(8,128)(2,1)S(1)}, u32[]{:S(2)}, u32[]{:S(2)}) collective-permute-start(bf16[128,1024]{1,0:T(8,128)(2,1)S(1)} %shard_map.110.refs_0_), channel_id=1, source_target_pairs={{0,1},{1,0},{2,3},{3,2},{4,5},{5,4},{6,7},{7,6},{8,9},{9,8},{10,11... | collective-permute-start | bytes 786440 | tf_op jit(solution)/shard_map/ppermute | solution.py:38
  13.3 12.3 %collective-permute-start.4 = (bf16[128,1024]{1,0:T(8,128)(2,1)S(1)}, bf16[128,1024]{1,0:T(8,128)(2,1)S(1)}, u32[]{:S(2)}, u32[]{:S(2)}) collective-permute-start(bf16[128,1024]{1,0:T(8,128)(2,1)S(1)} %shard_map.110.refs_0_), channel_id=1, source_target_pairs={{0,2},{1,3},{2,0},{3,1},{4,6},{5,7},{6,4},{7,5},{8,10},{9,11},{10,... | collective-permute-start | bytes 786440 | tf_op jit(solution)/shard_map/ppermute | solution.py:38
  15.9 13.4 %collective-permute-start.5 = (bf16[128,1024]{1,0:T(8,128)(2,1)S(1)}, bf16[128,1024]{1,0:T(8,128)(2,1)S(1)}, u32[]{:S(2)}, u32[]{:S(2)}) collective-permute-start(bf16[128,1024]{1,0:T(8,128)(2,1)S(1)} %shard_map.110.refs_0_), channel_id=1, source_target_pairs={{0,3},{1,2},{2,1},{3,0},{4,7},{5,6},{6,5},{7,4},{8,11},{9,10},{10,... | collective-permute-start | bytes 786440 | tf_op jit(solution)/shard_map/ppermute | solution.py:38
  29.4 4.5 %collective-permute-start.6 = (bf16[512,1024]{1,0:T(8,128)(2,1)S(1)}, bf16[512,1024]{1,0:T(8,128)(2,1)S(1)}, u32[]{:S(2)}, u32[]{:S(2)}) collective-permute-start(bf16[512,1024]{1,0:T(8,128)(2,1)S(1)} %shard_map.111.refs_0_), channel_id=1, source_target_pairs={{0,4},{4,0},{8,12},{12,8},{16,20},{20,16},{24,28},{28,24},{1,5},{5... | collective-permute-start | bytes 3145736 | tf_op jit(solution)/shard_map/ppermute | solution.py:38
  33.2 0.9 copy-start
  34.8 9.8 %collective-permute-start.18 = (bf16[576,256]{1,0:T(8,128)(2,1)S(1)}, bf16[576,256]{1,0:T(8,128)(2,1)S(1)}, u32[]{:S(2)}, u32[]{:S(2)}) collective-permute-start(bf16[576,256]{1,0:T(8,128)(2,1)S(1)} %get-tuple-element.69), channel_id=1, source_target_pairs={{0,128},{32,160},{64,192},{96,224},{128,0},{160,32},{192,64},{224,... | collective-permute-start | bytes 884744 | tf_op jit(solution)/shard_map/ppermute | solution.py:38
  37.7 14.7 %collective-permute-start.19 = (bf16[576,256]{1,0:T(8,128)(2,1)S(1)}, bf16[576,256]{1,0:T(8,128)(2,1)S(1)}, u32[]{:S(2)}, u32[]{:S(2)}) collective-permute-start(bf16[576,256]{1,0:T(8,128)(2,1)S(1)} %get-tuple-element.70), channel_id=1, source_target_pairs={{0,64},{32,96},{64,128},{96,160},{128,192},{160,224},{192,0},{224,... | collective-permute-start | bytes 884744 | tf_op jit(solution)/shard_map/ppermute | solution.py:38
  38.0 14.4 %collective-permute-start.20 = (bf16[576,256]{1,0:T(8,128)(2,1)S(1)}, bf16[576,256]{1,0:T(8,128)(2,1)S(1)}, u32[]{:S(2)}, u32[]{:S(2)}) collective-permute-start(bf16[576,256]{1,0:T(8,128)(2,1)S(1)} %get-tuple-element.71), channel_id=1, source_target_pairs={{0,192},{32,224},{64,0},{96,32},{128,64},{160,96},{192,128},{224,1... | collective-permute-start | bytes 884744 | tf_op jit(solution)/shard_map/ppermute | solution.py:38
  41.7 15.8 %collective-permute-start.11 = (bf16[400,256]{1,0:T(8,128)(2,1)S(1)}, bf16[400,256]{1,0:T(8,128)(2,1)S(1)}, u32[]{:S(2)}, u32[]{:S(2)}) collective-permute-start(bf16[400,256]{1,0:T(8,128)(2,1)S(1)} %shard_map.116), channel_id=1, source_target_pairs={{0,128},{32,160},{64,192},{96,224},{128,0},{160,32},{192,64},{224,... | collective-permute-start | bytes 614408 | tf_op jit(solution)/shard_map/ppermute | solution.py:38
  41.8 18.7 %collective-permute-start.12 = (bf16[400,256]{1,0:T(8,128)(2,1)S(1)}, bf16[400,256]{1,0:T(8,128)(2,1)S(1)}, u32[]{:S(2)}, u32[]{:S(2)}) collective-permute-start(bf16[400,256]{1,0:T(8,128)(2,1)S(1)} %shard_map.117), channel_id=1, source_target_pairs={{0,64},{32,96},{64,128},{96,160},{128,192},{160,224},{192,0},{224,... | collective-permute-start | bytes 614408 | tf_op jit(solution)/shard_map/ppermute | solution.py:38
  44.7 15.8 %collective-permute-start.13 = (bf16[400,256]{1,0:T(8,128)(2,1)S(1)}, bf16[400,256]{1,0:T(8,128)(2,1)S(1)}, u32[]{:S(2)}, u32[]{:S(2)}) collective-permute-start(bf16[400,256]{1,0:T(8,128)(2,1)S(1)} %shard_map.118), channel_id=1, source_target_pairs={{0,192},{32,224},{64,0},{96,32},{128,64},{160,96},{192,128},{224,1... | collective-permute-start | bytes 614408 | tf_op jit(solution)/shard_map/ppermute | solution.py:38
  52.8 23.0 %collective-permute-start.21 = (bf16[576,256]{1,0:T(8,128)(2,1)S(1)}, bf16[576,256]{1,0:T(8,128)(2,1)S(1)}, u32[]{:S(2)}, u32[]{:S(2)}) collective-permute-start(bf16[576,256]{1,0:T(8,128)(2,1)S(1)} %get-tuple-element.73), channel_id=1, source_target_pairs={{0,32},{32,0},{64,96},{96,64},{128,160},{160,128},{192,224},{224,1... | collective-permute-start | bytes 884744 | tf_op jit(solution)/shard_map/ppermute | solution.py:38
  61.0 12.3 %collective-permute-start.14 = (bf16[400,256]{1,0:T(8,128)(2,1)S(1)}, bf16[400,256]{1,0:T(8,128)(2,1)S(1)}, u32[]{:S(2)}, u32[]{:S(2)}) collective-permute-start(bf16[400,256]{1,0:T(8,128)(2,1)S(1)} %get-tuple-element.65), channel_id=1, source_target_pairs={{0,32},{32,0},{64,96},{96,64},{128,160},{160,128},{192,224},{224,1... | collective-permute-start | bytes 614408 | tf_op jit(solution)/shard_map/ppermute | solution.py:38
  66.5 10.2 %collective-permute-start.7 = (bf16[384,256]{1,0:T(8,128)(2,1)S(1)}, bf16[384,256]{1,0:T(8,128)(2,1)S(1)}, u32[]{:S(2)}, u32[]{:S(2)}) collective-permute-start(bf16[384,256]{1,0:T(8,128)(2,1)S(1)} %get-tuple-element.57), channel_id=1, source_target_pairs={{0,128},{32,160},{64,192},{96,224},{128,0},{160,32},{192,64},{224,... | collective-permute-start | bytes 589832 | tf_op jit(solution)/shard_map/ppermute | solution.py:38
  67.8 12.5 %collective-permute-start.8 = (bf16[384,256]{1,0:T(8,128)(2,1)S(1)}, bf16[384,256]{1,0:T(8,128)(2,1)S(1)}, u32[]{:S(2)}, u32[]{:S(2)}) collective-permute-start(bf16[384,256]{1,0:T(8,128)(2,1)S(1)} %get-tuple-element.58), channel_id=1, source_target_pairs={{0,64},{32,96},{64,128},{96,160},{128,192},{160,224},{192,0},{224,... | collective-permute-start | bytes 589832 | tf_op jit(solution)/shard_map/ppermute | solution.py:38
  69.7 10.6 %collective-permute-start.9 = (bf16[384,256]{1,0:T(8,128)(2,1)S(1)}, bf16[384,256]{1,0:T(8,128)(2,1)S(1)}, u32[]{:S(2)}, u32[]{:S(2)}) collective-permute-start(bf16[384,256]{1,0:T(8,128)(2,1)S(1)} %get-tuple-element.59), channel_id=1, source_target_pairs={{0,192},{32,224},{64,0},{96,32},{128,64},{160,96},{192,128},{224,1... | collective-permute-start | bytes 589832 | tf_op jit(solution)/shard_map/ppermute | solution.py:38
  73.4 18.4 %collective-permute-start.25 = (bf16[416,256]{1,0:T(8,128)(2,1)S(1)}, bf16[416,256]{1,0:T(8,128)(2,1)S(1)}, u32[]{:S(2)}, u32[]{:S(2)}) collective-permute-start(bf16[416,256]{1,0:T(8,128)(2,1)S(1)} %get-tuple-element.74.a_ref.refs_0_), channel_id=1, source_target_pairs={{0,128},{32,160},{64,192},{96,224},{128,0},{160,32},{192,64},{224,... | collective-permute-start | bytes 638984 | tf_op jit(solution)/shard_map/ppermute | solution.py:38
  76.0 20.0 %collective-permute-start.22 = (bf16[592,256]{1,0:T(8,128)(2,1)S(1)}, bf16[592,256]{1,0:T(8,128)(2,1)S(1)}, u32[]{:S(2)}, u32[]{:S(2)}) collective-permute-start(bf16[592,256]{1,0:T(8,128)(2,1)S(1)} %shard_map.124.a_ref.refs_0_), channel_id=1, source_target_pairs={{0,128},{32,160},{64,192},{96,224},{128,0},{160,32},{192,64},{224,... | collective-permute-start | bytes 909320 | tf_op jit(solution)/shard_map/ppermute | solution.py:38
  80.6 9.7 %collective-permute-start.10 = (bf16[384,256]{1,0:T(8,128)(2,1)S(1)}, bf16[384,256]{1,0:T(8,128)(2,1)S(1)}, u32[]{:S(2)}, u32[]{:S(2)}) collective-permute-start(bf16[384,256]{1,0:T(8,128)(2,1)S(1)} %get-tuple-element.61), channel_id=1, source_target_pairs={{0,32},{32,0},{64,96},{96,64},{128,160},{160,128},{192,224},{224,1... | collective-permute-start | bytes 589832 | tf_op jit(solution)/shard_map/ppermute | solution.py:38
  83.2 11.5 %collective-permute-start.26 = (bf16[416,256]{1,0:T(8,128)(2,1)S(1)}, bf16[416,256]{1,0:T(8,128)(2,1)S(1)}, u32[]{:S(2)}, u32[]{:S(2)}) collective-permute-start(bf16[416,256]{1,0:T(8,128)(2,1)S(1)} %get-tuple-element.74.a_ref.refs_0_), channel_id=1, source_target_pairs={{0,64},{32,96},{64,128},{96,160},{128,192},{160,224},{192,0},{224,... | collective-permute-start | bytes 638984 | tf_op jit(solution)/shard_map/ppermute | solution.py:38
  84.4 11.4 %collective-permute-start.27 = (bf16[416,256]{1,0:T(8,128)(2,1)S(1)}, bf16[416,256]{1,0:T(8,128)(2,1)S(1)}, u32[]{:S(2)}, u32[]{:S(2)}) collective-permute-start(bf16[416,256]{1,0:T(8,128)(2,1)S(1)} %get-tuple-element.74.a_ref.refs_0_), channel_id=1, source_target_pairs={{0,192},{32,224},{64,0},{96,32},{128,64},{160,96},{192,128},{224,1... | collective-permute-start | bytes 638984 | tf_op jit(solution)/shard_map/ppermute | solution.py:38
  90.3 9.9 %collective-permute-start.23 = (bf16[592,256]{1,0:T(8,128)(2,1)S(1)}, bf16[592,256]{1,0:T(8,128)(2,1)S(1)}, u32[]{:S(2)}, u32[]{:S(2)}) collective-permute-start(bf16[592,256]{1,0:T(8,128)(2,1)S(1)} %shard_map.124.a_ref.refs_0_), channel_id=1, source_target_pairs={{0,64},{32,96},{64,128},{96,160},{128,192},{160,224},{192,0},{224,... | collective-permute-start | bytes 909320 | tf_op jit(solution)/shard_map/ppermute | solution.py:38
  91.8 8.5 %collective-permute-start.24 = (bf16[592,256]{1,0:T(8,128)(2,1)S(1)}, bf16[592,256]{1,0:T(8,128)(2,1)S(1)}, u32[]{:S(2)}, u32[]{:S(2)}) collective-permute-start(bf16[592,256]{1,0:T(8,128)(2,1)S(1)} %shard_map.124.a_ref.refs_0_), channel_id=1, source_target_pairs={{0,192},{32,224},{64,0},{96,32},{128,64},{160,96},{192,128},{224,1... | collective-permute-start | bytes 909320 | tf_op jit(solution)/shard_map/ppermute | solution.py:38
  94.6 9.3 %collective-permute-start.15 = (bf16[400,256]{1,0:T(8,128)(2,1)S(1)}, bf16[400,256]{1,0:T(8,128)(2,1)S(1)}, u32[]{:S(2)}, u32[]{:S(2)}) collective-permute-start(bf16[400,256]{1,0:T(8,128)(2,1)S(1)} %shard_map.121.a_ref.refs_0_), channel_id=1, source_target_pairs={{0,128},{32,160},{64,192},{96,224},{128,0},{160,32},{192,64},{224,... | collective-permute-start | bytes 614408 | tf_op jit(solution)/shard_map/ppermute | solution.py:38
  95.8 12.9 %collective-permute-start.16 = (bf16[400,256]{1,0:T(8,128)(2,1)S(1)}, bf16[400,256]{1,0:T(8,128)(2,1)S(1)}, u32[]{:S(2)}, u32[]{:S(2)}) collective-permute-start(bf16[400,256]{1,0:T(8,128)(2,1)S(1)} %shard_map.121.a_ref.refs_0_), channel_id=1, source_target_pairs={{0,64},{32,96},{64,128},{96,160},{128,192},{160,224},{192,0},{224,... | collective-permute-start | bytes 614408 | tf_op jit(solution)/shard_map/ppermute | solution.py:38
  96.0 12.7 %collective-permute-start.17 = (bf16[400,256]{1,0:T(8,128)(2,1)S(1)}, bf16[400,256]{1,0:T(8,128)(2,1)S(1)}, u32[]{:S(2)}, u32[]{:S(2)}) collective-permute-start(bf16[400,256]{1,0:T(8,128)(2,1)S(1)} %shard_map.121.a_ref.refs_0_), channel_id=1, source_target_pairs={{0,192},{32,224},{64,0},{96,32},{128,64},{160,96},{192,128},{224,1... | collective-permute-start | bytes 614408 | tf_op jit(solution)/shard_map/ppermute | solution.py:38
  109.8 4.4 %collective-permute-start.28 = (bf16[520,1024]{1,0:T(8,128)(2,1)S(1)}, bf16[520,1024]{1,0:T(8,128)(2,1)S(1)}, u32[]{:S(2)}, u32[]{:S(2)}) collective-permute-start(bf16[520,1024]{1,0:T(8,128)(2,1)S(1)} %get-tuple-element.82), channel_id=1, source_target_pairs={{0,4},{4,0},{8,12},{12,8},{16,20},{20,16},{24,28},{28,24},{1,5},{5... | collective-permute-start | bytes 3194888 | tf_op jit(solution)/shard_map/ppermute | solution.py:38
  112.5 10.7 %collective-permute-start.41 = (bf16[384,512]{1,0:T(8,128)(2,1)S(1)}, bf16[384,512]{1,0:T(8,128)(2,1)S(1)}, u32[]{:S(2)}, u32[]{:S(2)}) collective-permute-start(bf16[384,512]{1,0:T(8,128)(2,1)S(1)} %shard_map.134.refs_9_), channel_id=1, source_target_pairs={{0,1},{1,0},{2,3},{3,2},{4,5},{5,4},{6,7},{7,6},{8,9},{9,8},{10,11... | collective-permute-start | bytes 1179656 | tf_op jit(solution)/shard_map/ppermute | solution.py:38
  114.5 17.7 %collective-permute-start.29 = (bf16[136,1024]{1,0:T(8,128)(2,1)S(1)}, bf16[136,1024]{1,0:T(8,128)(2,1)S(1)}, u32[]{:S(2)}, u32[]{:S(2)}) collective-permute-start(bf16[136,1024]{1,0:T(8,128)(2,1)S(1)} %get-tuple-element.86), channel_id=1, source_target_pairs={{0,8},{4,12},{8,0},{12,4},{16,24},{20,28},{24,16},{28,20},{1,9},{5... | collective-permute-start | bytes 835592 | tf_op jit(solution)/shard_map/ppermute | solution.py:38
  122.8 28.4 %collective-permute-start.37 = (bf16[576,512]{1,0:T(8,128)(2,1)S(1)}, bf16[576,512]{1,0:T(8,128)(2,1)S(1)}, u32[]{:S(2)}, u32[]{:S(2)}) collective-permute-start(bf16[576,512]{1,0:T(8,128)(2,1)S(1)} %shard_map.133.refs_4_), channel_id=1, source_target_pairs={{0,1},{1,0},{2,3},{3,2},{4,5},{5,4},{6,7},{7,6},{8,9},{9,8},{10,11... | collective-permute-start | bytes 1769480 | tf_op jit(solution)/shard_map/ppermute | solution.py:38
  122.9 28.4 %collective-permute-start.38 = (bf16[576,512]{1,0:T(8,128)(2,1)S(1)}, bf16[576,512]{1,0:T(8,128)(2,1)S(1)}, u32[]{:S(2)}, u32[]{:S(2)}) collective-permute-start(bf16[576,512]{1,0:T(8,128)(2,1)S(1)} %shard_map.133.refs_4_), channel_id=1, source_target_pairs={{0,3},{1,2},{2,1},{3,0},{4,7},{5,6},{6,5},{7,4},{8,11},{9,10},{10,... | collective-permute-start | bytes 1769480 | tf_op jit(solution)/shard_map/ppermute | solution.py:38
  123.0 20.4 %collective-permute-start.30 = (bf16[136,1024]{1,0:T(8,128)(2,1)S(1)}, bf16[136,1024]{1,0:T(8,128)(2,1)S(1)}, u32[]{:S(2)}, u32[]{:S(2)}) collective-permute-start(bf16[136,1024]{1,0:T(8,128)(2,1)S(1)} %get-tuple-element.87), channel_id=1, source_target_pairs={{0,16},{4,20},{8,24},{12,28},{16,0},{20,4},{24,8},{28,12},{1,17},{... | collective-permute-start | bytes 835592 | tf_op jit(solution)/shard_map/ppermute | solution.py:38
  123.2 25.0 %collective-permute-start.42 = (bf16[384,512]{1,0:T(8,128)(2,1)S(1)}, bf16[384,512]{1,0:T(8,128)(2,1)S(1)}, u32[]{:S(2)}, u32[]{:S(2)}) collective-permute-start(bf16[384,512]{1,0:T(8,128)(2,1)S(1)} %shard_map.134.refs_9_), channel_id=1, source_target_pairs={{0,3},{1,2},{2,1},{3,0},{4,7},{5,6},{6,5},{7,4},{8,11},{9,10},{10,... | collective-permute-start | bytes 1179656 | tf_op jit(solution)/shard_map/ppermute | solution.py:38
  132.2 15.7 %collective-permute-start.31 = (bf16[136,1024]{1,0:T(8,128)(2,1)S(1)}, bf16[136,1024]{1,0:T(8,128)(2,1)S(1)}, u32[]{:S(2)}, u32[]{:S(2)}) collective-permute-start(bf16[136,1024]{1,0:T(8,128)(2,1)S(1)} %get-tuple-element.88), channel_id=1, source_target_pairs={{0,24},{4,28},{8,16},{12,20},{16,8},{20,12},{24,0},{28,4},{1,25},{... | collective-permute-start | bytes 835592 | tf_op jit(solution)/shard_map/ppermute | solution.py:38
  143.4 11.6 %collective-permute-start.43 = (bf16[384,512]{1,0:T(8,128)(2,1)S(1)}, bf16[384,512]{1,0:T(8,128)(2,1)S(1)}, u32[]{:S(2)}, u32[]{:S(2)}) collective-permute-start(bf16[384,512]{1,0:T(8,128)(2,1)S(1)} %shard_map.134.refs_9_), channel_id=1, source_target_pairs={{0,2},{1,3},{2,0},{3,1},{4,6},{5,7},{6,4},{7,5},{8,10},{9,11},{10,... | collective-permute-start | bytes 1179656 | tf_op jit(solution)/shard_map/ppermute | solution.py:38
  147.9 18.7 %collective-permute-start.34 = (bf16[384,512]{1,0:T(8,128)(2,1)S(1)}, bf16[384,512]{1,0:T(8,128)(2,1)S(1)}, u32[]{:S(2)}, u32[]{:S(2)}) collective-permute-start(bf16[384,512]{1,0:T(8,128)(2,1)S(1)} %shard_map.132.refs_0_), channel_id=1, source_target_pairs={{0,2},{1,3},{2,0},{3,1},{4,6},{5,7},{6,4},{7,5},{8,10},{9,11},{10,... | collective-permute-start | bytes 1179656 | tf_op jit(solution)/shard_map/ppermute | solution.py:38
  148.2 18.4 %collective-permute-start.32 = (bf16[72,1024]{1,0:T(8,128)(2,1)S(1)}, bf16[72,1024]{1,0:T(8,128)(2,1)S(1)}, u32[]{:S(2)}, u32[]{:S(2)}) collective-permute-start(bf16[72,1024]{1,0:T(8,128)(2,1)S(1)} %get-tuple-element.92), channel_id=1, source_target_pairs={{0,2},{1,3},{2,0},{3,1},{4,6},{5,7},{6,4},{7,5},{8,10},{9,11},{10,... | collective-permute-start | bytes 442376 | tf_op jit(solution)/shard_map/ppermute | solution.py:38
  151.3 23.8 %collective-permute-start.35 = (bf16[384,512]{1,0:T(8,128)(2,1)S(1)}, bf16[384,512]{1,0:T(8,128)(2,1)S(1)}, u32[]{:S(2)}, u32[]{:S(2)}) collective-permute-start(bf16[384,512]{1,0:T(8,128)(2,1)S(1)} %shard_map.132.refs_0_), channel_id=1, source_target_pairs={{0,1},{1,0},{2,3},{3,2},{4,5},{5,4},{6,7},{7,6},{8,9},{9,8},{10,11... | collective-permute-start | bytes 1179656 | tf_op jit(solution)/shard_map/ppermute | solution.py:38
  151.3 25.6 %collective-permute-start.36 = (bf16[384,512]{1,0:T(8,128)(2,1)S(1)}, bf16[384,512]{1,0:T(8,128)(2,1)S(1)}, u32[]{:S(2)}, u32[]{:S(2)}) collective-permute-start(bf16[384,512]{1,0:T(8,128)(2,1)S(1)} %shard_map.132.refs_0_), channel_id=1, source_target_pairs={{0,3},{1,2},{2,1},{3,0},{4,7},{5,6},{6,5},{7,4},{8,11},{9,10},{10,... | collective-permute-start | bytes 1179656 | tf_op jit(solution)/shard_map/ppermute | solution.py:38
  155.0 28.2 %collective-permute-start.39 = (bf16[288,512]{1,0:T(8,128)(2,1)S(1)}, bf16[288,512]{1,0:T(8,128)(2,1)S(1)}, u32[]{:S(2)}, u32[]{:S(2)}) collective-permute-start(bf16[288,512]{1,0:T(8,128)(2,1)S(1)} %slice.8), channel_id=1, source_target_pairs={{0,3},{1,2},{2,1},{3,0},{4,7},{5,6},{6,5},{7,4},{8,11},{9,10},{10,... | collective-permute-start | bytes 884744 | tf_op jit(solution)/shard_map/ppermute | solution.py:38
  166.6 16.6 %collective-permute-start.40 = (bf16[288,512]{1,0:T(8,128)(2,1)S(1)}, bf16[288,512]{1,0:T(8,128)(2,1)S(1)}, u32[]{:S(2)}, u32[]{:S(2)}) collective-permute-start(bf16[288,512]{1,0:T(8,128)(2,1)S(1)} %slice.9), channel_id=1, source_target_pairs={{0,1},{1,0},{2,3},{3,2},{4,5},{5,4},{6,7},{7,6},{8,9},{9,8},{10,11... | collective-permute-start | bytes 884744 | tf_op jit(solution)/shard_map/ppermute | solution.py:38
  166.7 21.0 %copy-start.1 = (bf16[32,512]{1,0:T(8,128)(2,1)S(1)}, bf16[32,512]{1,0:T(8,128)(2,1)}, u32[]{:S(2)}) copy-start(bf16[32,512]{1,0:T(8,128)(2,1)} %tok_ref.3) | copy-start | bytes 98308
  166.7 21.0 %copy-start.2 = (bf16[32,512]{1,0:T(8,128)(2,1)S(1)}, bf16[32,512]{1,0:T(8,128)(2,1)}, u32[]{:S(2)}) copy-start(bf16[32,512]{1,0:T(8,128)(2,1)} %cot_ref.3) | copy-start | bytes 98308
  166.7 21.0 %collective-permute-start.33 = (bf16[40,1024]{1,0:T(8,128)(2,1)S(1)}, bf16[40,1024]{1,0:T(8,128)(2,1)S(1)}, u32[]{:S(2)}, u32[]{:S(2)}) collective-permute-start(bf16[40,1024]{1,0:T(8,128)(2,1)S(1)} %get-tuple-element.97), channel_id=1, source_target_pairs={{0,1},{1,0},{2,3},{3,2},{4,5},{5,4},{6,7},{7,6},{8,9},{9,8},{10,11... | collective-permute-start | bytes 245768 | tf_op jit(solution)/shard_map/ppermute | solution.py:38
